TPU v7x, 256 devices: a whole 4x4x8 slice. The times are simulated.
256 devices in a mesh: seq: 32 (over x_hi, z, core), tp: 8 (over x_lo, y).
Axes of the slice: x: 4 (x_hi: 2, x_lo: 2; x = x_hi * 2 + x_lo), y: 4, z: 8, core: 2. Of those that a mesh axis runs over, the one named last changes fastest.
Arguments:
- tokens: bfloat16 [16384, 1536], P(('seq', 'tp')), may hold values from -3 to 3
- segment_ids: int32 [16384], P(('seq', 'tp')), may hold values from 0 to 5, never falling along the last dimension, each value on 1 to 4096 neighbouring positions
- routes: int32 [16384, 4], P(('seq', 'tp')), may hold values from 0 to 31, all different within a row; in each aligned block of 512 rows (0 to 511, 512 to 1023, ...) at most 128 rows name the same one
- attn_gain: float32 [1536], replicated, may hold values from 0.5 to 1.5
- w_query: bfloat16 [1536, 1024], P(None, 'tp'), may hold values from -9 to 9
- w_key: bfloat16 [1536, 256], replicated, may hold values from -0.5 to 0.5
- w_value: bfloat16 [1536, 256], replicated, may hold values from -2.5 to 2.5
- w_out: bfloat16 [1024, 1536], P('tp'), may hold values from -0.1875 to 0.1875
- moe_gain: float32 [1536], replicated, may hold values from 0.5 to 1.5
- w_router: bfloat16 [1536, 32], replicated, may hold values from -30 to 30
- w_gate: bfloat16 [32, 1536, 768], P('seq'), may hold values from -0.15625 to 0.15625
- w_up: bfloat16 [32, 1536, 768], P('seq'), may hold values from -0.15625 to 0.15625
- w_down: bfloat16 [32, 768, 1536], P('seq'), may hold values from -0.21875 to 0.21875
Outputs:
- layer_out: bfloat16 [16384, 1536], P(('seq', 'tp'))
- kv_cache: bfloat16 [2, 2, 16384, 128], P(None, None, ('seq', 'tp'))
Inputs may be any that keep to these rules, and one draw needn't show every extreme that they name: `segment_ids`: numbers never fall along the stream; every prompt has at most 4096 tokens and one has exactly 4096. `routes`: A token names 4 different experts. In each aligned block of 512 tokens no expert is named by more than 128 tokens, a bound that some block reaches.
All inputs are finite; a program needn't handle non-finite values.
Results may differ from a plain program's by a relative error of at most 0.018.
Values may be sent and summed in bfloat16 or wider, within the bound.
A program may use at most 128 MiB of HBM per device.

v0:
```python
import math

import jax
import jax.numpy as jnp
from jax import lax
from jax.sharding import PartitionSpec as P

HD = 128
QH = 8
KVH = 2


ROTARY = 1000000.0
NEGATIVE = -1e30


def passed_along(array, axis, by):
    count = lax.axis_size(axis)
    pairs = [(i, i + by) for i in range(count) if 0 <= i + by < count]
    return lax.ppermute(array, axis, pairs)


def rms_rows(values_in, gain):
    wide = values_in.astype(jnp.float32)
    scale = lax.rsqrt(jnp.mean(wide * wide, axis=-1, keepdims=True) + 1e-06)
    return wide * scale * gain


def rotate(matrix, position):
    count = matrix.shape[0]
    shaped = matrix.reshape(count, -1, HD)
    half = HD // 2
    inverse = ROTARY ** (-(jnp.arange(half, dtype=jnp.float32) * 2.0 / HD))
    angle = position.astype(jnp.float32)[:, None] * inverse[None, :]
    cosine = jnp.cos(angle)[:, None, :]
    sine = jnp.sin(angle)[:, None, :]
    first = shaped[..., :half]
    second = shaped[..., half:]
    turned = jnp.concatenate(
        [first * cosine - second * sine, second * cosine + first * sine], axis=-1
    )
    return turned.reshape(count, -1)


def on_device(
    tokens,
    segment_ids,
    routes,
    attn_gain,
    w_query,
    w_key,
    w_value,
    w_out,
    moe_gain,
    w_router,
    w_gate,
    w_up,
    w_down,
):
    tp_size = lax.axis_size("tp")
    seq_size = lax.axis_size("seq")
    tp_rank = lax.axis_index("tp")
    seq_rank = lax.axis_index("seq")
    tok_dev = tokens.shape[0]
    tok_seq = tok_dev * tp_size
    width = tokens.shape[1]
    head_count = w_query.shape[1] // HD
    group = QH // KVH
    kv_local = max(1, head_count // group)
    per_kv = head_count // kv_local
    seg_count = 3 * seq_size // 16
    labels = jnp.arange(seg_count, dtype=jnp.int32)
    normed = rms_rows(tokens, attn_gain).astype(jnp.bfloat16)
    own_index = (seq_rank * tp_size + tp_rank) * tok_dev + jnp.arange(tok_dev, dtype=jnp.int32)
    local_first = jnp.min(
        jnp.where(segment_ids[:, None] == labels[None, :], own_index[:, None], tok_seq * seq_size),
        axis=0,
    )
    firsts = lax.pmin(local_first, ("seq", "tp"))

    def segment_start(segs):
        return jnp.sum(jnp.where(segs[:, None] == labels[None, :], firsts[None, :], 0), axis=1)

    wide_rows, wide_segs, wide_routes = (
        lax.all_gather(normed, "tp", axis=0, tiled=True),
        lax.all_gather(segment_ids, "tp", axis=0, tiled=True),
        lax.all_gather(routes, "tp", axis=0, tiled=True),
    )
    block_first = seq_rank * tok_seq
    block_index = block_first + jnp.arange(tok_seq, dtype=jnp.int32)
    query_start = segment_start(wide_segs)
    query = rotate(
        jnp.dot(wide_rows, w_query, preferred_element_type=jnp.float32), block_index - query_start
    ).astype(jnp.bfloat16)
    own_position = own_index - segment_start(segment_ids)
    keys_new = rotate(
        jnp.dot(normed, w_key, preferred_element_type=jnp.float32), own_position
    ).astype(jnp.bfloat16)
    values_new = jnp.dot(normed, w_value, preferred_element_type=jnp.float32).astype(jnp.bfloat16)
    keys_heads = keys_new.reshape(tok_dev, KVH, HD)
    values_heads = values_new.reshape(tok_dev, KVH, HD)
    kv_cache = jnp.stack(
        [jnp.transpose(keys_heads, (1, 0, 2)), jnp.transpose(values_heads, (1, 0, 2))]
    )
    block_keys, block_values = (
        lax.all_gather(keys_heads, "tp", axis=0, tiled=True),
        lax.all_gather(values_heads, "tp", axis=0, tiled=True),
    )
    kv_first = tp_rank * head_count // group
    kv_pair = jnp.stack(
        [
            lax.dynamic_slice_in_dim(block_keys, kv_first, kv_local, 1),
            lax.dynamic_slice_in_dim(block_values, kv_first, kv_local, 1),
        ]
    )
    grouped_query = query.reshape(tok_seq, kv_local, per_kv, HD)
    scale = 1.0 / math.sqrt(HD)

    def attend(running, arrived, offset):
        peak_score, denominator, accumulated = running
        key_index = offset + jnp.arange(arrived.shape[1], dtype=jnp.int32)
        scores = (
            jnp.einsum(
                "qcgd,kcd->cgqk", grouped_query, arrived[0], preferred_element_type=jnp.float32
            )
            * scale
        )
        allowed = (key_index[None, :] <= block_index[:, None]) & (
            key_index[None, :] >= query_start[:, None]
        )
        masked = jnp.where(allowed, scores, NEGATIVE)
        newest = jnp.maximum(peak_score, jnp.max(masked, axis=-1))
        factor = jnp.exp(peak_score - newest)
        weights = jnp.where(allowed, jnp.exp(masked - newest[..., None]), 0.0)
        denominator = denominator * factor + jnp.sum(weights, axis=-1)
        mixed = jnp.einsum(
            "cgqk,kcd->cgqd",
            weights.astype(jnp.bfloat16),
            arrived[1],
            preferred_element_type=jnp.float32,
        )
        accumulated = accumulated * factor[..., None] + mixed
        return (newest, denominator, accumulated)

    initial = (
        jnp.full((kv_local, per_kv, tok_seq), NEGATIVE, jnp.float32),
        jnp.zeros((kv_local, per_kv, tok_seq), jnp.float32),
        jnp.zeros((kv_local, per_kv, tok_seq, HD), jnp.float32),
    )
    running = attend(initial, kv_pair, block_first)
    reach = min(8, seq_size - 1)

    def one_hop(hop_count, loop_state):
        carried, arrived = loop_state
        arrived = passed_along(arrived, "seq", 1)
        return (attend(carried, arrived, block_first - hop_count * tok_seq), arrived)

    running, _ = lax.fori_loop(1, reach + 1, one_hop, (running, kv_pair))
    peak_score, denominator, accumulated = running
    heads_out = accumulated / denominator[..., None]
    attention = (
        jnp.transpose(heads_out, (2, 0, 1, 3))
        .reshape(tok_seq, head_count * HD)
        .astype(jnp.bfloat16)
    )
    resid = tokens.astype(jnp.float32) + lax.psum_scatter(
        jnp.dot(attention, w_out, preferred_element_type=jnp.float32).astype(jnp.bfloat16),
        "tp",
        scatter_dimension=0,
        tiled=True,
    ).astype(jnp.float32)
    moe_rows = rms_rows(resid, moe_gain).astype(jnp.bfloat16)
    experts = w_router.shape[1]
    top = routes.shape[1]
    capacity = tok_seq * top * 2 // experts
    share = capacity // tp_size
    slot_start = tp_rank * share
    source = lax.all_gather(moe_rows, "tp", axis=0, tiled=True)
    logits = jnp.dot(source, w_router, preferred_element_type=jnp.float32)
    expert_ids = jnp.arange(experts, dtype=jnp.int32)
    chosen = jnp.sum(
        jnp.where(wide_routes[:, :, None] == expert_ids[None, None, :], logits[:, None, :], 0.0),
        axis=-1,
    )
    gates = jax.nn.softmax(chosen, axis=-1).astype(jnp.bfloat16)
    flat_routes = wide_routes.reshape(-1)
    pair_count = flat_routes.shape[0]
    one_hot = (flat_routes[:, None] == expert_ids[None, :]).astype(jnp.int32)
    earlier = jnp.cumsum(one_hot, axis=0) - one_hot
    slot_index = jnp.sum(earlier * one_hot, axis=1)
    destination = flat_routes * capacity + slot_index
    owner_row = jnp.arange(pair_count, dtype=jnp.int32) // top
    token_of = (
        jnp.zeros((experts * capacity,), jnp.int32)
        .at[destination]
        .set(owner_row)
        .reshape(experts, capacity)
    )
    filled = (
        jnp.zeros((experts * capacity,), jnp.int32)
        .at[destination]
        .set(1)
        .reshape(experts, capacity)
    )
    gate_of = (
        jnp.zeros((experts * capacity,), jnp.bfloat16)
        .at[destination]
        .set(gates.reshape(-1))
        .reshape(experts, capacity)
    )
    token_of = lax.dynamic_slice_in_dim(token_of, slot_start, share, 1)
    filled = lax.dynamic_slice_in_dim(filled, slot_start, share, 1)
    gate_of = lax.dynamic_slice_in_dim(gate_of, slot_start, share, 1)
    send_rows = jnp.where(filled[..., None] > 0, source[token_of], jnp.zeros((), jnp.bfloat16))
    got_rows, got_gates = (
        lax.all_to_all(send_rows, "seq", split_axis=0, concat_axis=0, tiled=True),
        lax.all_to_all(gate_of, "seq", split_axis=0, concat_axis=0, tiled=True),
    )
    exp_dev = w_gate.shape[0]
    got_rows = got_rows.reshape(seq_size, exp_dev, share, width)
    got_gates = got_gates.reshape(seq_size, exp_dev, share).astype(jnp.float32)
    gate_out = jnp.einsum("secd,edf->secf", got_rows, w_gate, preferred_element_type=jnp.float32)
    up_out = jnp.einsum("secd,edf->secf", got_rows, w_up, preferred_element_type=jnp.float32)
    active = (jax.nn.relu(gate_out) * up_out).astype(jnp.bfloat16)
    down_out = (
        jnp.einsum("secf,efd->secd", active, w_down, preferred_element_type=jnp.float32)
        * got_gates[..., None]
    )
    contribution = down_out.astype(jnp.bfloat16)
    returned = lax.all_to_all(
        contribution.reshape(seq_size * exp_dev, share, width),
        "seq",
        split_axis=0,
        concat_axis=0,
        tiled=True,
    )
    returned_flat = returned.reshape(experts * share, width)
    inside = (slot_index >= slot_start) & (slot_index < slot_start + share)
    local_slot = flat_routes * share + jnp.clip(slot_index - slot_start, 0, share - 1)
    picked = jnp.where(inside[:, None], returned_flat[local_slot].astype(jnp.float32), 0.0)
    partial_moe = jnp.sum(picked.reshape(tok_seq, top, width), axis=1)
    moe = lax.psum_scatter(partial_moe.astype(jnp.bfloat16), "tp", scatter_dimension=0, tiled=True)
    layer_out = (resid + moe.astype(jnp.float32)).astype(jnp.bfloat16)
    return (layer_out, kv_cache)


def solution(mesh):
    placed = (
        P(("seq", "tp"), None),
        P(("seq", "tp")),
        P(("seq", "tp"), None),
        P(),
        P(None, "tp"),
        P(),
        P(),
        P("tp", None),
        P(),
        P(),
        P("seq", None, None),
        P("seq", None, None),
        P("seq", None, None),
    )
    return jax.shard_map(
        on_device,
        mesh=mesh,
        in_specs=placed,
        out_specs=(P(("seq", "tp"), None), P(None, None, ("seq", "tp"), None)),
        check_vma=False,
    )
```

profile of v0, /device:TPU:8, one launch (start us, length us, event | category | flops | bytes accessed | tf_op | source)
XLA Modules:
  0.0 606.6 jit_solution(9368189847051557091)
XLA Ops:
  7.3 1.2 fusion.41
  8.5 1.7 fusion.43
  11.1 80.5 %pmin.7 = s32[6]{0:T(128)S(1)} all-reduce(s32[6]{0:T(128)S(1)} %select_reduce_fusion.4), channel_id=1, replica_groups=mesh['seq'=32,'tp'=8] {'seq','tp'}, use_global_device_ids=true, to_apply=%region_1.2 | all-reduce | flops 6 | bytes 48 | tf_op jit(solution)/shard_map/pmin | solution.py:79
  91.6 1.5 fusion.83
  95.9 10.2 %all-reduce = s32[512]{0:T(512)S(1)} all-reduce(s32[512]{0:T(512)S(1)} %dynamic-update-slice), channel_id=1, replica_groups=mesh['seq'=32,'tp'=8] {'tp'}, use_global_device_ids=true, to_apply=%add | all-reduce | flops 512 | bytes 4096
  106.7 27.8 %all_gather.19 = bf16[512,2,128]{2,0,1:T(8,128)(2,1)S(1)} all-gather(bf16[64,2,128]{2,0,1:T(8,128)(2,1)S(1)} %pad_maximum_fusion.2), channel_id=1, replica_groups=mesh['seq'=32,'tp'=8] {'tp'}, dimensions={0}, use_global_device_ids=true | all-gather | bytes 294912 | tf_op jit(solution)/shard_map/all_gather | solution.py:106
  134.5 28.4 %all_gather.21 = bf16[512,2,128]{2,0,1:T(8,128)(2,1)S(1)} all-gather(bf16[64,2,128]{2,0,1:T(8,128)(2,1)S(1)} %bitcast.181), channel_id=1, replica_groups=mesh['seq'=32,'tp'=8] {'tp'}, dimensions={0}, use_global_device_ids=true | all-gather | bytes 294912 | tf_op jit(solution)/shard_map/all_gather | solution.py:107
  163.6 2.1 convolution_bitcast_fusion.2
  168.4 79.9 %while.21 = (s32[]{:T(128)}, f32[1,1,512]{2,1,0:T(1,128)S(1)}, f32[1,1,512]{2,1,0:T(1,128)S(1)}, f32[1,1,512,128]{3,2,1,0:T(8,128)}, bf16[2,512,1,128]{3,1,2,0:T...) while((s32[]{:T(128)}, f32[1,1,512]{2,1,0:T(1,128)S(1)}, ...), condition=%wide.region_10.11_spmd.clone.clone, body=%wide.region_7.10_spmd.clone.clone.sunk | while | flops 139069440 | bytes 7788773 | solution.py:158
  168.4 1.4 collective-permute-start
  169.8 1.3 collective-permute-done
  173.9 6.8 %collective-permute-start = (bf16[2,512,1,128]{3,1,2,0:T(8,128)(2,1)}, bf16[2,512,1,128]{3,1,2,0:T(8,128)(2,1)S(1)}, u32[]{:S(2)}, u32[]{:S(2)}) collective-permute-start(bf16[2,512,1,128]{3,1,2,0:T(8,128)(2,1)} %get-tuple-element.363), channel_id=1, source_target_pairs={{0,8},{8,16},{16,24},{24,32},{32,40},{40,48},{48,56},{56,64},{64,7... | collective-permute-start | bytes 786440 | tf_op jit(solution)/shard_map/while/body/eval_jaxpr/ppermute | solution.py:20
  180.7 1.3 collective-permute-done
  184.7 6.5 %collective-permute-start = (bf16[2,512,1,128]{3,1,2,0:T(8,128)(2,1)}, bf16[2,512,1,128]{3,1,2,0:T(8,128)(2,1)S(1)}, u32[]{:S(2)}, u32[]{:S(2)}) collective-permute-start(bf16[2,512,1,128]{3,1,2,0:T(8,128)(2,1)} %get-tuple-element.363), channel_id=1, source_target_pairs={{0,8},{8,16},{16,24},{24,32},{32,40},{40,48},{48,56},{56,64},{64,7... | collective-permute-start | bytes 786440 | tf_op jit(solution)/shard_map/while/body/eval_jaxpr/ppermute | solution.py:20
  191.3 1.3 collective-permute-done
  195.3 6.5 %collective-permute-start = (bf16[2,512,1,128]{3,1,2,0:T(8,128)(2,1)}, bf16[2,512,1,128]{3,1,2,0:T(8,128)(2,1)S(1)}, u32[]{:S(2)}, u32[]{:S(2)}) collective-permute-start(bf16[2,512,1,128]{3,1,2,0:T(8,128)(2,1)} %get-tuple-element.363), channel_id=1, source_target_pairs={{0,8},{8,16},{16,24},{24,32},{32,40},{40,48},{48,56},{56,64},{64,7... | collective-permute-start | bytes 786440 | tf_op jit(solution)/shard_map/while/body/eval_jaxpr/ppermute | solution.py:20
  201.9 1.3 collective-permute-done
  205.9 6.5 %collective-permute-start = (bf16[2,512,1,128]{3,1,2,0:T(8,128)(2,1)}, bf16[2,512,1,128]{3,1,2,0:T(8,128)(2,1)S(1)}, u32[]{:S(2)}, u32[]{:S(2)}) collective-permute-start(bf16[2,512,1,128]{3,1,2,0:T(8,128)(2,1)} %get-tuple-element.363), channel_id=1, source_target_pairs={{0,8},{8,16},{16,24},{24,32},{32,40},{40,48},{48,56},{56,64},{64,7... | collective-permute-start | bytes 786440 | tf_op jit(solution)/shard_map/while/body/eval_jaxpr/ppermute | solution.py:20
  212.5 1.3 collective-permute-done
  216.5 6.5 %collective-permute-start = (bf16[2,512,1,128]{3,1,2,0:T(8,128)(2,1)}, bf16[2,512,1,128]{3,1,2,0:T(8,128)(2,1)S(1)}, u32[]{:S(2)}, u32[]{:S(2)}) collective-permute-start(bf16[2,512,1,128]{3,1,2,0:T(8,128)(2,1)} %get-tuple-element.363), channel_id=1, source_target_pairs={{0,8},{8,16},{16,24},{24,32},{32,40},{40,48},{48,56},{56,64},{64,7... | collective-permute-start | bytes 786440 | tf_op jit(solution)/shard_map/while/body/eval_jaxpr/ppermute | solution.py:20
  223.1 1.3 collective-permute-done
  227.1 6.5 %collective-permute-start = (bf16[2,512,1,128]{3,1,2,0:T(8,128)(2,1)}, bf16[2,512,1,128]{3,1,2,0:T(8,128)(2,1)S(1)}, u32[]{:S(2)}, u32[]{:S(2)}) collective-permute-start(bf16[2,512,1,128]{3,1,2,0:T(8,128)(2,1)} %get-tuple-element.363), channel_id=1, source_target_pairs={{0,8},{8,16},{16,24},{24,32},{32,40},{40,48},{48,56},{56,64},{64,7... | collective-permute-start | bytes 786440 | tf_op jit(solution)/shard_map/while/body/eval_jaxpr/ppermute | solution.py:20
  233.7 1.3 collective-permute-done
  237.7 6.5 %collective-permute-start = (bf16[2,512,1,128]{3,1,2,0:T(8,128)(2,1)}, bf16[2,512,1,128]{3,1,2,0:T(8,128)(2,1)S(1)}, u32[]{:S(2)}, u32[]{:S(2)}) collective-permute-start(bf16[2,512,1,128]{3,1,2,0:T(8,128)(2,1)} %get-tuple-element.363), channel_id=1, source_target_pairs={{0,8},{8,16},{16,24},{24,32},{32,40},{40,48},{48,56},{56,64},{64,7... | collective-permute-start | bytes 786440 | tf_op jit(solution)/shard_map/while/body/eval_jaxpr/ppermute | solution.py:20
  244.3 1.3 collective-permute-done
  248.3 2.8 convolution_convert_fusion
  251.1 70.3 %reduce-scatter.3.cloned.1.call-done = bf16[64,1536]{1,0:T(8,128)(2,1)} async-done(((bf16[512,1536]{1,0:T(8,128)(2,1)}), bf16[64,1536]{1,0:T(8,128)(2,1)}) %reduce-scatter.3.cloned.1.call-update) | async-done | bytes 196624 | tf_op jit(solution)/shard_map/reduce_scatter | solution.py:166
  322.6 1.7 multiply_convert_fusion.1
  324.3 24.3 %all-gather = s32[8,64,4]{1,2,0:T(4,128)S(1)} all-gather(s32[1,64,4]{1,2,0:T(4,128)S(1)} %bitcast.201), channel_id=1, replica_groups=mesh['seq'=32,'tp'=8] {'tp'}, dimensions={0}, use_global_device_ids=true | all-gather | bytes 9216 | tf_op jit(solution)/shard_map/all_gather | solution.py:87
  349.2 9.1 %reduce-window.6 = s32[32,16,128]{2,1,0:T(8,128)S(1)} reduce-window(s32[32,16,128]{2,1,0:T(8,128)S(1)} %fusion.47, s32[]{:T(128)} %constant.114.clone.1), window={size=1x1x128 pad=0_0x0_0x127_0}, to_apply=%region_12.13 | reduce-window | flops 8323072 | bytes 524292 | tf_op jit(solution)/shard_map/reduce-window
  359.9 8.1 %scatter_custom_fusion.1 = s32[4096]{0:T(1024)S(1)} fusion(s32[2048]{0:T(1024)S(1)} %bitcast.198, s32[2048]{0:T(1024)S(1)} %add_select_fusion, s32[]{:T(128)} %constant.114.clone.1), kind=kCustom, calls=%fused_computation.123 | custom fusion | bytes 16388 | tf_op jit(solution)/shard_map/scatter | solution.py:196
  368.1 8.2 %scatter_custom_fusion = s32[4096]{0:T(1024)S(1)} fusion(s32[2048]{0:T(1024)S(1)} %bitcast.199, s32[2048]{0:T(1024)S(1)} %broadcast.532, s32[]{:T(128)} %constant.114.clone.1), kind=kCustom, calls=%fused_computation.125 | custom fusion | bytes 16388 | tf_op jit(solution)/shard_map/scatter | solution.py:202
  376.5 2.0 fusion.84
  378.9 14.6 %scatter_custom_fusion.2 = bf16[4096]{0:T(1024)(128)(2,1)S(1)} fusion(s32[2048]{0:T(1024)S(1)} %bitcast.200, bf16[2048]{0:T(1024)(128)(2,1)S(1)} %reshape.733, bf16[]{:T(256)} %constant.138.clone.1), kind=kCustom, calls=%fused_computation.134 | custom fusion | bytes 8194 | tf_op jit(solution)/shard_map/scatter | solution.py:208
  394.2 9.5 %all-to-all-start.1 = ((bf16[32,1,16]{2,1,0:T(2,128)(2,1)}), bf16[32,1,16]{2,1,0:T(2,128)(2,1)S(1)}, u32[]{:S(2)}, u32[]{:S(2)}) async-start(bf16[32,1,16]{2,1,0:T(2,128)(2,1)} %copy.91), calls=%async_computation.2 | async-start | bytes 32768 | tf_op jit(solution)/shard_map/all_to_all | solution.py:217
  403.8 6.0 gather_fusion
  409.8 2.7 broadcast_select_fusion
  413.6 8.8 %all-to-all-start = ((bf16[32,16,1536]{2,1,0:T(8,128)(2,1)}), bf16[32,16,1536]{2,1,0:T(8,128)(2,1)}, u32[]{:S(2)}, u32[]{:S(2)}) async-start(bf16[32,16,1536]{2,1,0:T(8,128)(2,1)} %broadcast_select_fusion), calls=%async_computation.1 | async-start | bytes 3145728 | tf_op jit(solution)/shard_map/all_to_all | solution.py:216
  422.5 40.6 %all-to-all-done = bf16[32,16,1536]{2,1,0:T(8,128)(2,1)} async-done(((bf16[32,16,1536]{2,1,0:T(8,128)(2,1)}), bf16[32,16,1536]{2,1,0:T(8,128)(2,1)}, u32[]{:S(2)}, u32[]{:S(2)}) %all-to-all-start) | async-done | bytes 1572896 | tf_op jit(solution)/shard_map/all_to_all | solution.py:216
  463.1 4.7 fusion.20
  467.7 6.9 %fusion.18 = bf16[32,16,1536]{2,1,0:T(8,128)(2,1)} fusion(bf16[1,768,1536]{2,1,0:T(8,128)(2,1)S(1)} %copy-done, f32[32,16]{1,0:T(8,128)S(1)} %bitcast.196, f32[32,16,768]{2,1,0:T(8,128)} %fusion.20, bf16[32,16,1536]{2,1,0:T(8,128)(2,1)} %all-to-all-done, bf16[1,1536,768]{2,1,0:T(8,128)(2,1)} %param.25), kind=kOutput, calls=%fused_computation.34 | convolution fusion | flops 2418671616 | bytes 9439232 | tf_op jit(solution)/shard_map/secf,efd->secd/dot_general | solution.py:226
  474.6 4.7 all-to-all-start.2
  479.9 40.0 %all-to-all-done.2 = bf16[32,16,1536]{2,1,0:T(8,128)(2,1)} async-done(((bf16[32,16,1536]{2,1,0:T(8,128)(2,1)}), bf16[32,16,1536]{2,1,0:T(8,128)(2,1)}, u32[]{:S(2)}, u32[]{:S(2)}) %all-to-all-start.2) | async-done | bytes 1572896 | tf_op jit(solution)/shard_map/all_to_all | solution.py:230
  519.9 14.9 %gather_fusion.1 = bf16[2048,1536]{1,0:T(8,128)(2,1)} fusion(bf16[512,1536]{1,0:T(8,128)(2,1)} %bitcast.39, s32[2048]{0:T(1024)S(1)} %broadcast_clamp_fusion), kind=kCustom, calls=%fused_computation.1 | custom fusion | bytes 12591104 | tf_op jit(solution)/shard_map/gather | solution.py:240
  534.8 12.2 %reshape.696 = f32[512,4,1536]{2,1,0:T(4,128)} reshape(bf16[2048,1536]{1,0:T(8,128)(2,1)} %gather_fusion.1) | data formatting | bytes 18874368 | tf_op jit(solution)/shard_map/convert_element_type | solution.py:240
  547.1 13.5 %select_reduce_fusion = bf16[512,1536]{1,0:T(8,128)(2,1)} fusion(f32[512,4,1536]{2,1,0:T(4,128)} %reshape.696, pred[512,4]{1,0:T(8,128)(4,1)S(1)} %and.49), kind=kLoop, calls=%fused_computation.29 | loop fusion | flops 5505024 | bytes 14157824 | tf_op jit(solution)/shard_map/reduce_sum | solution.py:241
  561.3 37.1 %reduce-scatter.5.cloned.1.call-done = bf16[64,1536]{1,0:T(8,128)(2,1)} async-done(((bf16[512,1536]{1,0:T(8,128)(2,1)}), bf16[64,1536]{1,0:T(8,128)(2,1)}) %reduce-scatter.5.cloned.1.call-update) | async-done | bytes 196624 | tf_op jit(solution)/shard_map/reduce_scatter | solution.py:242
  598.4 1.7 add_convert_fusion
  (198 shorter events, 35.6 us)
Async XLA Ops:
  7.2 460.6 %copy-start = (bf16[1,768,1536]{2,1,0:T(8,128)(2,1)S(1)}, bf16[1,768,1536]{2,1,0:T(8,128)(2,1)}, u32[]{:S(2)}) copy-start(bf16[1,768,1536]{2,1,0:T(8,128)(2,1)} %param.27) | copy-start | bytes 7077892
  7.2 87.2 %copy-start.12 = (u32[256]{0:T(256)S(1)}, u32[256]{0:T(256)}, u32[]{:S(2)}) copy-start(u32[256]{0:T(256)} %constant.148) | copy-start | bytes 3076
  7.2 88.4 %copy-start.11 = (s32[64]{0:T(128)S(1)}, s32[64]{0:T(128)}, u32[]{:S(2)}) copy-start(s32[64]{0:T(128)} %param.16) | copy-start | bytes 772
  7.2 86.0 %copy-start.3 = (bf16[1536,256]{1,0:T(8,128)(2,1)S(1)}, bf16[1536,256]{1,0:T(8,128)(2,1)}, u32[]{:S(2)}) copy-start(bf16[1536,256]{1,0:T(8,128)(2,1)} %param.21) | copy-start | bytes 2359300
  7.2 156.4 %all-gather.4.cloned.1.call-start = ((), (), s32[]{:S(2)}) async-start(), calls=%async_computation.5 | async-start | bytes 1769472 | tf_op jit(solution)/shard_map/all_gather | solution.py:85
  10.3 311.2 %reduce-scatter.3.cloned.1.call-start = ((), (), s32[]{:S(2)}) async-start(), calls=%async_computation.6 | async-start | bytes 1769472 | tf_op jit(solution)/shard_map/reduce_scatter | solution.py:166
  106.5 57.2 %copy-start.5 = (bf16[1536,128]{1,0:T(8,128)(2,1)S(1)}, bf16[1536,128]{1,0:T(8,128)(2,1)}, u32[]{:S(2)}) copy-start(bf16[1536,128]{1,0:T(8,128)(2,1)} %param.19) | copy-start | bytes 1179652
  168.3 79.9 %copy-start.4 = (bf16[128,1536]{1,0:T(8,128)(2,1)S(1)}, bf16[128,1536]{1,0:T(8,128)(2,1)}, u32[]{:S(2)}) copy-start(bf16[128,1536]{1,0:T(8,128)(2,1)} %param.22) | copy-start | bytes 1179652
  168.4 2.8 collective-permute-start
  171.2 1.5 copy-start.6
  173.2 0.7 copy-start.7
  173.9 8.1 %collective-permute-start = (bf16[2,512,1,128]{3,1,2,0:T(8,128)(2,1)}, bf16[2,512,1,128]{3,1,2,0:T(8,128)(2,1)S(1)}, u32[]{:S(2)}, u32[]{:S(2)}) collective-permute-start(bf16[2,512,1,128]{3,1,2,0:T(8,128)(2,1)} %get-tuple-element.363), channel_id=1, source_target_pairs={{0,8},{8,16},{16,24},{24,32},{32,40},{40,48},{48,56},{56,64},{64,7... | collective-permute-start | bytes 786440 | tf_op jit(solution)/shard_map/while/body/eval_jaxpr/ppermute | solution.py:20
  182.0 1.5 copy-start.6
  184.0 0.7 copy-start.7
  184.7 7.9 %collective-permute-start = (bf16[2,512,1,128]{3,1,2,0:T(8,128)(2,1)}, bf16[2,512,1,128]{3,1,2,0:T(8,128)(2,1)S(1)}, u32[]{:S(2)}, u32[]{:S(2)}) collective-permute-start(bf16[2,512,1,128]{3,1,2,0:T(8,128)(2,1)} %get-tuple-element.363), channel_id=1, source_target_pairs={{0,8},{8,16},{16,24},{24,32},{32,40},{40,48},{48,56},{56,64},{64,7... | collective-permute-start | bytes 786440 | tf_op jit(solution)/shard_map/while/body/eval_jaxpr/ppermute | solution.py:20
  192.6 1.5 copy-start.6
  194.6 0.7 copy-start.7
  195.3 7.9 %collective-permute-start = (bf16[2,512,1,128]{3,1,2,0:T(8,128)(2,1)}, bf16[2,512,1,128]{3,1,2,0:T(8,128)(2,1)S(1)}, u32[]{:S(2)}, u32[]{:S(2)}) collective-permute-start(bf16[2,512,1,128]{3,1,2,0:T(8,128)(2,1)} %get-tuple-element.363), channel_id=1, source_target_pairs={{0,8},{8,16},{16,24},{24,32},{32,40},{40,48},{48,56},{56,64},{64,7... | collective-permute-start | bytes 786440 | tf_op jit(solution)/shard_map/while/body/eval_jaxpr/ppermute | solution.py:20
  203.2 1.5 copy-start.6
  205.2 0.7 copy-start.7
  205.9 7.9 %collective-permute-start = (bf16[2,512,1,128]{3,1,2,0:T(8,128)(2,1)}, bf16[2,512,1,128]{3,1,2,0:T(8,128)(2,1)S(1)}, u32[]{:S(2)}, u32[]{:S(2)}) collective-permute-start(bf16[2,512,1,128]{3,1,2,0:T(8,128)(2,1)} %get-tuple-element.363), channel_id=1, source_target_pairs={{0,8},{8,16},{16,24},{24,32},{32,40},{40,48},{48,56},{56,64},{64,7... | collective-permute-start | bytes 786440 | tf_op jit(solution)/shard_map/while/body/eval_jaxpr/ppermute | solution.py:20
  213.8 1.5 copy-start.6
  215.8 0.7 copy-start.7
  216.5 7.9 %collective-permute-start = (bf16[2,512,1,128]{3,1,2,0:T(8,128)(2,1)}, bf16[2,512,1,128]{3,1,2,0:T(8,128)(2,1)S(1)}, u32[]{:S(2)}, u32[]{:S(2)}) collective-permute-start(bf16[2,512,1,128]{3,1,2,0:T(8,128)(2,1)} %get-tuple-element.363), channel_id=1, source_target_pairs={{0,8},{8,16},{16,24},{24,32},{32,40},{40,48},{48,56},{56,64},{64,7... | collective-permute-start | bytes 786440 | tf_op jit(solution)/shard_map/while/body/eval_jaxpr/ppermute | solution.py:20
  224.4 1.5 copy-start.6
  226.4 0.7 copy-start.7
  227.1 7.9 %collective-permute-start = (bf16[2,512,1,128]{3,1,2,0:T(8,128)(2,1)}, bf16[2,512,1,128]{3,1,2,0:T(8,128)(2,1)S(1)}, u32[]{:S(2)}, u32[]{:S(2)}) collective-permute-start(bf16[2,512,1,128]{3,1,2,0:T(8,128)(2,1)} %get-tuple-element.363), channel_id=1, source_target_pairs={{0,8},{8,16},{16,24},{24,32},{32,40},{40,48},{48,56},{56,64},{64,7... | collective-permute-start | bytes 786440 | tf_op jit(solution)/shard_map/while/body/eval_jaxpr/ppermute | solution.py:20
  235.0 1.5 copy-start.6
  237.0 0.7 copy-start.7
  237.7 7.9 %collective-permute-start = (bf16[2,512,1,128]{3,1,2,0:T(8,128)(2,1)}, bf16[2,512,1,128]{3,1,2,0:T(8,128)(2,1)S(1)}, u32[]{:S(2)}, u32[]{:S(2)}) collective-permute-start(bf16[2,512,1,128]{3,1,2,0:T(8,128)(2,1)} %get-tuple-element.363), channel_id=1, source_target_pairs={{0,8},{8,16},{16,24},{24,32},{32,40},{40,48},{48,56},{56,64},{64,7... | collective-permute-start | bytes 786440 | tf_op jit(solution)/shard_map/while/body/eval_jaxpr/ppermute | solution.py:20
  245.6 1.5 copy-start.6
  247.6 0.7 copy-start.7
  248.3 73.2 %copy-start.1 = (bf16[64,1536]{1,0:T(8,128)(2,1)S(1)}, bf16[64,1536]{1,0:T(8,128)(2,1)}, u32[]{:S(2)}) copy-start(bf16[64,1536]{1,0:T(8,128)(2,1)} %param.15) | copy-start | bytes 589828
  248.3 74.3 %copy-start.9 = (f32[1536]{0:T(1024)S(1)}, f32[1536]{0:T(1024)}, u32[]{:S(2)}) copy-start(f32[1536]{0:T(1024)} %param.23) | copy-start | bytes 18436
  251.1 73.3 %copy-start.10 = (s32[64,4]{0,1:T(4,128)S(1)}, s32[64,4]{0,1:T(4,128)}, u32[]{:S(2)}) copy-start(s32[64,4]{0,1:T(4,128)} %param.17) | copy-start | bytes 3076
  251.1 125.4 %all-gather.6.cloned.1.call-start = ((), (), s32[]{:S(2)}) async-start(), calls=%async_computation.7 | async-start | bytes 1769472 | tf_op jit(solution)/shard_map/all_gather | solution.py:178
  358.2 18.2 %copy-start.8 = (bf16[1536,32]{0,1:T(8,128)(2,1)S(1)}, bf16[1536,32]{0,1:T(8,128)(2,1)}, u32[]{:S(2)}) copy-start(bf16[1536,32]{0,1:T(8,128)(2,1)} %param.24) | copy-start | bytes 294916
  394.2 19.4 %all-to-all-start.1 = ((bf16[32,1,16]{2,1,0:T(2,128)(2,1)}), bf16[32,1,16]{2,1,0:T(2,128)(2,1)S(1)}, u32[]{:S(2)}, u32[]{:S(2)}) async-start(bf16[32,1,16]{2,1,0:T(2,128)(2,1)} %copy.91), calls=%async_computation.2 | async-start | bytes 32768 | tf_op jit(solution)/shard_map/all_to_all | solution.py:217
  413.6 49.5 %all-to-all-start = ((bf16[32,16,1536]{2,1,0:T(8,128)(2,1)}), bf16[32,16,1536]{2,1,0:T(8,128)(2,1)}, u32[]{:S(2)}, u32[]{:S(2)}) async-start(bf16[32,16,1536]{2,1,0:T(8,128)(2,1)} %broadcast_select_fusion), calls=%async_computation.1 | async-start | bytes 3145728 | tf_op jit(solution)/shard_map/all_to_all | solution.py:216
  474.6 45.3 %all-to-all-start.2 = ((bf16[32,16,1536]{2,1,0:T(8,128)(2,1)}), bf16[32,16,1536]{2,1,0:T(8,128)(2,1)}, u32[]{:S(2)}, u32[]{:S(2)}) async-start(bf16[32,16,1536]{2,1,0:T(8,128)(2,1)} %fusion.18), calls=%async_computation.3 | async-start | bytes 3145728 | tf_op jit(solution)/shard_map/all_to_all | solution.py:230
  479.3 119.1 %reduce-scatter.5.cloned.1.call-start = ((), (), s32[]{:S(2)}) async-start(), calls=%async_computation.8 | async-start | bytes 1769472 | tf_op jit(solution)/shard_map/reduce_scatter | solution.py:242
  560.5 37.8 %copy-start.2 = (bf16[64,1536]{1,0:T(8,128)(2,1)S(1)}, bf16[64,1536]{1,0:T(8,128)(2,1)}, u32[]{:S(2)}) copy-start(bf16[64,1536]{1,0:T(8,128)(2,1)} %reduce-scatter.3.cloned.1.call-done) | copy-start | bytes 589828
Sparse Core Ops, SparseCore 0:
  10.4 43.1 all-gather.3
  251.2 70.2 reduce-scatter.2
  324.4 41.9 all-gather.5
  560.7 37.6 reduce-scatter.4
where the time goes:
time: 610 us; the launch traced here: 607 us
  waiting for transfers between devices  200 us (33%)
  blocking collectives  171 us (28%)
  local copies, waits for them, and re-layouts  79.6 us (13%)
  starting transfers between devices  70.9 us (12%)
  other arithmetic  40 us (7%)
  matrix products  29.9 us (5%)
  between operations  14.9 us (2%)
    pmin x1, blocking collectives, on_device(): firsts = lax.pmin(local_first, ('seq', 'tp'))  80.5 us
    reduce_scatter x1, waiting for transfers between devices, on_device(): lax.psum_scatter(jnp.dot(attention, w_out, preferred_element_type=jnp.flo...  70.3 us
    ppermute x8, starting transfers between devices, passed_along(): return lax.ppermute(array, axis, pairs)  47.5 us
    all_to_all x1, waiting for transfers between devices, on_device(): lax.all_to_all(send_rows, 'seq', split_axis=0, concat_axis=0, tiled=True)  40.6 us
    all_to_all x1, waiting for transfers between devices, on_device(): lax.all_to_all(contribution.reshape(seq_size * exp_dev, share, width), 's...  40 us
    reduce_scatter x1, waiting for transfers between devices, on_device(): lax.psum_scatter(partial_moe.astype(jnp.bfloat16), 'tp', scatter_dimensio...  37.1 us
    all_gather x1, blocking collectives, on_device(): lax.all_gather(values_heads, 'tp', axis=0, tiled=True)  28.4 us
    all_gather x1, blocking collectives, on_device(): lax.all_gather(keys_heads, 'tp', axis=0, tiled=True)  27.8 us
  transfers between devices with their start and end apart: 15, of which 13 were waited for; matrix products, arithmetic and copies ran while one was open for 7% of the time, Pallas kernels for 0%

commit v1 on v0

v1 whole, which is shorter than its diff:
```python
import functools
import math

import jax
import jax.numpy as jnp
from jax import lax
from jax.experimental import pallas as pl
from jax.experimental.pallas import tpu as pltpu
from jax.sharding import PartitionSpec as P

HD = 128
QH = 8
KVH = 2
ROTARY = 1000000.0
NEGATIVE = -1e30
MESH = pl.DeviceIdType.MESH
ANY = pl.BlockSpec(memory_space=pl.ANY)
IN_VMEM = pl.BlockSpec(memory_space=pltpu.VMEM)


def rms_rows(values_in, gain):
    wide = values_in.astype(jnp.float32)
    scale = lax.rsqrt(jnp.mean(wide * wide, axis=-1, keepdims=True) + 1e-06)
    return wide * scale * gain


def rotate(matrix, cosine, sine):
    count = matrix.shape[0]
    shaped = matrix.reshape(count, -1, HD)
    half = HD // 2
    cosine, sine = cosine[:, None, :], sine[:, None, :]
    first = shaped[..., :half]
    second = shaped[..., half:]
    turned = jnp.concatenate(
        [first * cosine - second * sine, second * cosine + first * sine], axis=-1
    )
    return turned.reshape(count, -1)


def greet(peers):
    barrier = pltpu.get_barrier_semaphore()
    for peer in peers:
        pl.semaphore_signal(barrier, inc=1, device_id=peer, device_id_type=MESH)
    pl.semaphore_wait(barrier, len(peers))


def places():
    s, t = lax.axis_index("seq"), lax.axis_index("tp")
    return s, t, s // 16, (s // 2) % 8, s % 2, t // 4, t % 4


def params(number, **more):
    return pltpu.CompilerParams(collective_id=number, has_side_effects=True, **more)


def tp_gather_kernel(
    rows_ref, weight_ref, seg_ref, wide_ref, full_ref, segs_ref,
    send, recv, seg_send, seg_recv, far_send, far_recv, half_send, half_recv, local,
):
    s, t, _, _, core, x, y = places()
    across = (1 - x) * 4
    own = x * 4
    up, down, two = (y + 1) % 4, (y + 3) % 4, (y + 2) % 4
    xp, yn, yp = (s, across + y), (s, own + up), (s, own + down)
    twin = (s + 1 - 2 * core, t)
    tp_peers = [(s, (t + k) % 8) for k in range(1, 8)]
    ahead = [((s + k) % 32, t) for k in range(1, 9)]
    behind = [((s + 32 - k) % 32, t) for k in range(1, 9)]
    greet(tp_peers + ahead + behind + [twin])

    seg_own = pltpu.make_async_copy(seg_ref, segs_ref.at[0, t], local.at[0])
    seg_own.start()
    seg_copies = []
    for k, peer in enumerate(tp_peers):
        copy = pltpu.make_async_remote_copy(
            src_ref=seg_ref, dst_ref=segs_ref.at[0, t], send_sem=seg_send.at[k],
            recv_sem=seg_recv.at[k], device_id=peer, device_id_type=MESH,
        )
        copy.start()
        seg_copies.append(copy)

    sent = []

    def pass_on(bank, number, src, dst, peer):
        copy = pltpu.make_async_remote_copy(
            src_ref=src, dst_ref=dst, send_sem=send.at[bank, number],
            recv_sem=recv.at[bank, number], device_id=peer, device_id_type=MESH,
        )
        copy.start()
        sent.append(copy)

    def landed(bank, number, dst):
        pltpu.make_async_remote_copy(
            src_ref=dst, dst_ref=dst, send_sem=send.at[bank, number],
            recv_sem=recv.at[bank, number], device_id=xp, device_id_type=MESH,
        ).wait_recv()

    banks = [(rows_ref, wide_ref), (weight_ref.at[core], full_ref.at[core])]
    locals_ = []
    for bank, (src, out) in enumerate(banks):
        copy = pltpu.make_async_copy(src, out.at[t], local.at[1 + bank])
        copy.start()
        locals_.append(copy)
        pass_on(bank, 0, src, out.at[t], xp)
        pass_on(bank, 1, src, out.at[t], yn)
        pass_on(bank, 2, src, out.at[t], yp)
    for copy in seg_copies:
        copy.wait()
    seg_own.wait()
    far_copies = []
    for k, peer in enumerate(ahead):
        copy = pltpu.make_async_remote_copy(
            src_ref=segs_ref.at[0], dst_ref=segs_ref.at[k + 1], send_sem=far_send.at[k],
            recv_sem=far_recv.at[k], device_id=peer, device_id_type=MESH,
        )
        copy.start()
        far_copies.append(copy)
    low, high = pl.ds(0, 32), pl.ds(32, 32)
    for bank, (src, out) in enumerate(banks):
        landed(bank, 0, out.at[across + y])
        pass_on(bank, 3, out.at[across + y], out.at[across + y], yn)
        pass_on(bank, 4, out.at[across + y], out.at[across + y], yp)
        landed(bank, 1, out.at[own + down])
        pass_on(bank, 5, out.at[own + down, low], out.at[own + down, low], yn)
        landed(bank, 2, out.at[own + up])
        pass_on(bank, 6, out.at[own + up, high], out.at[own + up, high], yp)
        landed(bank, 3, out.at[across + down])
        pass_on(bank, 7, out.at[across + down, low], out.at[across + down, low], yn)
        landed(bank, 4, out.at[across + up])
        pass_on(bank, 8, out.at[across + up, high], out.at[across + up, high], yp)
    for bank, (src, out) in enumerate(banks):
        landed(bank, 5, out.at[own + two, low])
        landed(bank, 6, out.at[own + two, high])
        landed(bank, 7, out.at[across + two, low])
        landed(bank, 8, out.at[across + two, high])
    for copy in locals_:
        copy.wait()
    halves = pltpu.make_async_remote_copy(
        src_ref=full_ref.at[core], dst_ref=full_ref.at[core], send_sem=half_send,
        recv_sem=half_recv, device_id=twin, device_id_type=MESH,
    )
    halves.start()
    for copy in sent:
        copy.wait_send()
    for copy in far_copies:
        copy.wait()
    halves.wait_send()
    pltpu.make_async_remote_copy(
        src_ref=full_ref.at[1 - core], dst_ref=full_ref.at[1 - core], send_sem=half_send,
        recv_sem=half_recv, device_id=twin, device_id_type=MESH,
    ).wait_recv()


def tp_gather(rows, weight, seg):
    count, width = rows.shape
    dma = pltpu.SemaphoreType.DMA
    return pl.pallas_call(
        tp_gather_kernel,
        out_shape=(
            jax.ShapeDtypeStruct((8, count, width), rows.dtype),
            jax.ShapeDtypeStruct((2, 8, 64, width), weight.dtype),
            jax.ShapeDtypeStruct((9, 8, 1, 128), jnp.int32),
        ),
        in_specs=[ANY] * 3,
        out_specs=(ANY,) * 3,
        scratch_shapes=[
            dma((2, 9)), dma((2, 9)), dma((7,)), dma((7,)), dma((8,)), dma((8,)),
            dma(()), dma(()), dma((3,)),
        ],
        compiler_params=params(1),
        name="tp_gather",
    )(rows, weight, seg)


def kv_kernel(kv_ref, out_ref, z_send, z_recv, y_send, y_recv, c_send, c_recv, local):
    s, t, _, _, core, x, y = places()
    own = x * 4
    up, down, two = (y + 1) % 4, (y + 3) % 4, (y + 2) % 4
    ahead, behind = ((s + 2) % 32, t), ((s + 30) % 32, t)
    yn, yp = (s, own + up), (s, own + down)
    twin = (s + 1 - 2 * core, t)
    greet([ahead, behind, yn, yp, twin])
    first = pltpu.make_async_copy(kv_ref, out_ref.at[0], local)
    first.start()
    sent = []

    def pass_on(src, dst, send_sem, recv_sem, peer):
        copy = pltpu.make_async_remote_copy(
            src_ref=src, dst_ref=dst, send_sem=send_sem, recv_sem=recv_sem,
            device_id=peer, device_id_type=MESH,
        )
        copy.start()
        sent.append(copy)

    def landed(dst, send_sem, recv_sem):
        pltpu.make_async_remote_copy(
            src_ref=dst, dst_ref=dst, send_sem=send_sem, recv_sem=recv_sem,
            device_id=twin, device_id_type=MESH,
        ).wait_recv()

    def to_twin(i):
        pass_on(
            out_ref.at[2 * i + 2 * core], out_ref.at[2 * i + 1],
            c_send.at[i], c_recv.at[i], twin,
        )

    pass_on(kv_ref.at[y], out_ref.at[2, y], z_send.at[0], z_recv.at[0], ahead)
    first.wait()

    def middle(k):
        landed(out_ref.at[2 * k, down], y_send.at[k - 1, 0], y_recv.at[k - 1, 0])
        piece = out_ref.at[2 * k, down, 0]
        pass_on(piece, piece, y_send.at[k - 1, 2], y_recv.at[k - 1, 2], yn)
        landed(out_ref.at[2 * k, up], y_send.at[k - 1, 1], y_recv.at[k - 1, 1])
        piece = out_ref.at[2 * k, up, 1]
        pass_on(piece, piece, y_send.at[k - 1, 3], y_recv.at[k - 1, 3], yp)

    def last(k):
        landed(out_ref.at[2 * k, two, 0], y_send.at[k - 1, 2], y_recv.at[k - 1, 2])
        landed(out_ref.at[2 * k, two, 1], y_send.at[k - 1, 3], y_recv.at[k - 1, 3])

    for k in range(1, 7):
        if k <= 4:
            landed(out_ref.at[2 * k, y], z_send.at[k - 1], z_recv.at[k - 1])
            piece = out_ref.at[2 * k, y]
            if k < 4:
                pass_on(piece, out_ref.at[2 * k + 2, y], z_send.at[k], z_recv.at[k], ahead)
            pass_on(piece, piece, y_send.at[k - 1, 0], y_recv.at[k - 1, 0], yn)
            pass_on(piece, piece, y_send.at[k - 1, 1], y_recv.at[k - 1, 1], yp)
        if 1 <= k - 1 <= 4:
            middle(k - 1)
        if 1 <= k - 2 <= 4:
            last(k - 2)
            to_twin(k - 3)
    for copy in sent:
        copy.wait_send()
    for i in range(4):
        landed(out_ref.at[2 * i + 1], c_send.at[i], c_recv.at[i])


def kv_exchange(kv):
    dma = pltpu.SemaphoreType.DMA
    return pl.pallas_call(
        kv_kernel,
        out_shape=jax.ShapeDtypeStruct((9,) + kv.shape, kv.dtype),
        in_specs=[ANY],
        out_specs=ANY,
        scratch_shapes=[dma((4,)), dma((4,)), dma((4, 4)), dma((4, 4)), dma((4,)), dma((4,)), dma(())],
        compiler_params=params(2),
        name="kv_exchange",
    )(kv)


def attention_kernel(base_ref, q_ref, start_ref, kv_ref, out_ref, peak, total, mixed):
    step = pl.program_id(0)

    @pl.when(step == 0)
    def _():
        peak[...] = jnp.full_like(peak, NEGATIVE)
        total[...] = jnp.zeros_like(total)
        mixed[...] = jnp.zeros_like(mixed)

    count = q_ref.shape[0]
    keys = kv_ref[0, :, 0].reshape(count, HD)
    values = kv_ref[0, :, 1].reshape(count, HD)
    scores = lax.dot_general(
        q_ref[...], keys, (((1,), (1,)), ((), ())), preferred_element_type=jnp.float32
    ) * (1.0 / math.sqrt(HD))
    base = base_ref[0]
    key_index = base - step * count + lax.broadcasted_iota(jnp.int32, (1, count), 1)
    query_index = base + lax.broadcasted_iota(jnp.int32, (count, 1), 0)
    allowed = (key_index >= start_ref[...]) & (key_index <= query_index)
    masked = jnp.where(allowed, scores, NEGATIVE)
    old = peak[...]
    newest = jnp.maximum(old, jnp.max(masked, axis=-1, keepdims=True))
    factor = jnp.exp(old - newest)
    weights = jnp.exp(masked - newest)
    total[...] = total[...] * factor + jnp.sum(weights, axis=-1, keepdims=True)
    mixed[...] = mixed[...] * factor + jnp.dot(
        weights.astype(jnp.bfloat16), values, preferred_element_type=jnp.float32
    )
    peak[...] = newest

    @pl.when(step == pl.num_programs(0) - 1)
    def _():
        out_ref[...] = (mixed[...] / total[...]).astype(out_ref.dtype)


def attend(query, starts, kv_all, base):
    count = query.shape[0]
    whole = lambda shape: pl.BlockSpec(shape, lambda j, _: (0,) * len(shape))
    return pl.pallas_call(
        attention_kernel,
        out_shape=jax.ShapeDtypeStruct((count, HD), jnp.bfloat16),
        grid_spec=pltpu.PrefetchScalarGridSpec(
            num_scalar_prefetch=1,
            grid=(9,),
            in_specs=[
                whole((count, HD)),
                whole((count, 1)),
                pl.BlockSpec((1,) + kv_all.shape[1:], lambda j, _: (j, 0, 0, 0, 0)),
            ],
            out_specs=whole((count, HD)),
            scratch_shapes=[
                pltpu.VMEM((count, 1), jnp.float32),
                pltpu.VMEM((count, 1), jnp.float32),
                pltpu.VMEM((count, HD), jnp.float32),
            ],
        ),
        name="attend",
    )(base, query, starts, kv_all)


def heads_kernel(in_ref, out_ref, send, recv, local):
    s, t, *_ = places()
    peers = [(t + k) % 8 for k in range(1, 8)]
    greet([(s, peer) for peer in peers])
    own = pltpu.make_async_copy(in_ref.at[t], out_ref.at[t], local)
    own.start()
    copies = []
    for k, peer in enumerate(peers):
        copy = pltpu.make_async_remote_copy(
            src_ref=in_ref.at[peer], dst_ref=out_ref.at[t], send_sem=send.at[k],
            recv_sem=recv.at[k], device_id=(s, peer), device_id_type=MESH,
        )
        copy.start()
        copies.append(copy)
    own.wait()
    for copy in copies:
        copy.wait()


def heads_to_tokens(attention):
    dma = pltpu.SemaphoreType.DMA
    return pl.pallas_call(
        heads_kernel,
        out_shape=jax.ShapeDtypeStruct(attention.shape, attention.dtype),
        in_specs=[ANY],
        out_specs=ANY,
        scratch_shapes=[dma((7,)), dma((7,)), dma(())],
        compiler_params=params(3),
        name="heads_to_tokens",
    )(attention)


def spread_kernel(rows_ref, out_ref, x_send, x_recv, z_send, z_recv, c_send, c_recv, local):
    s, t, plane, z, core, x, y = places()
    across = ((1 - plane) * 16 + z * 2 + core, (1 - x) * 4 + y)
    twin = (s + 1 - 2 * core, t)
    ring = [(plane * 16 + ((z + d) % 8) * 2 + core, t) for d in (1, 7)]
    greet([across, twin] + ring)
    planes = [plane, 1 - plane]

    def slot(p, way, distance):
        back = (z + 8 - distance) % 8 if way == 0 else (z + distance) % 8
        return planes[p] * 16 + back * 2 + core

    sent = []

    def pass_on(src, dst, send_sem, recv_sem, peer):
        copy = pltpu.make_async_remote_copy(
            src_ref=src, dst_ref=dst, send_sem=send_sem, recv_sem=recv_sem,
            device_id=peer, device_id_type=MESH,
        )
        copy.start()
        sent.append(copy)

    def landed(dst, send_sem, recv_sem):
        pltpu.make_async_remote_copy(
            src_ref=dst, dst_ref=dst, send_sem=send_sem, recv_sem=recv_sem,
            device_id=twin, device_id_type=MESH,
        ).wait_recv()

    def travels(p, way, distance):
        return distance <= 3 or (distance == 4 and p == way)

    twins = []

    def to_twin(src, block):
        k = len(twins)
        twins.append(k)
        pass_on(src, out_ref.at[block], c_send.at[k], c_recv.at[k], twin)

    own = pltpu.make_async_copy(rows_ref, out_ref.at[s], local)
    own.start()
    pass_on(rows_ref, out_ref.at[s], x_send, x_recv, across)
    for way in range(2):
        pass_on(rows_ref, out_ref.at[s], z_send.at[0, way, 0], z_recv.at[0, way, 0], ring[way])
    to_twin(rows_ref, s)
    block = across[0]
    landed(out_ref.at[block], x_send, x_recv)
    for way in range(2):
        pass_on(out_ref.at[block], out_ref.at[block], z_send.at[1, way, 0], z_recv.at[1, way, 0], ring[way])
    to_twin(out_ref.at[block], block)
    for distance in range(1, 5):
        for p in range(2):
            for way in range(2):
                if not travels(p, way, distance):
                    continue
                block = slot(p, way, distance)
                k = distance - 1
                landed(out_ref.at[block], z_send.at[p, way, k], z_recv.at[p, way, k])
                if travels(p, way, distance + 1):
                    pass_on(
                        out_ref.at[block], out_ref.at[block],
                        z_send.at[p, way, k + 1], z_recv.at[p, way, k + 1], ring[way],
                    )
                to_twin(out_ref.at[block], block)
    own.wait()
    for copy in sent:
        copy.wait_send()
    for k in twins:
        landed(out_ref.at[twin[0]], c_send.at[k], c_recv.at[k])


def spread(rows):
    dma = pltpu.SemaphoreType.DMA
    return pl.pallas_call(
        spread_kernel,
        out_shape=jax.ShapeDtypeStruct((32,) + rows.shape, rows.dtype),
        in_specs=[ANY],
        out_specs=ANY,
        scratch_shapes=[dma(()), dma(()), dma((2, 2, 4)), dma((2, 2, 4)), dma((16,)), dma((16,)), dma(())],
        compiler_params=params(4),
        name="spread",
    )(rows)


CHUNK = 256


def expert_kernel(info_ref, rows_ref, lane_ref, column_ref, gate_ref, up_ref, down_ref, out_ref):
    width = gate_ref.shape[0]
    tokens = rows_ref.shape[0]
    expert, routed = info_ref[0], info_ref[1]

    def one_chunk(number, first):
        base = number * CHUNK
        picks = (
            lane_ref[...] == base + lax.broadcasted_iota(jnp.int32, (CHUNK, 1), 0)
        ).astype(jnp.bfloat16)
        rows = jnp.dot(picks, rows_ref[:, :width], preferred_element_type=jnp.float32).astype(jnp.bfloat16)
        all_gates = jnp.dot(picks, rows_ref[:, width:], preferred_element_type=jnp.float32)
        here = lax.broadcasted_iota(jnp.int32, all_gates.shape, 1) == expert
        gates = jnp.sum(jnp.where(here, all_gates, 0.0), axis=1, keepdims=True)
        gate_out = jnp.dot(rows, gate_ref[...], preferred_element_type=jnp.float32)
        up_out = jnp.dot(rows, up_ref[...], preferred_element_type=jnp.float32)
        active = (jnp.maximum(gate_out, 0.0) * up_out).astype(jnp.bfloat16)
        down_out = jnp.dot(active, down_ref[...], preferred_element_type=jnp.float32) * gates
        contribution = down_out.astype(jnp.bfloat16)
        lanes = base + lax.broadcasted_iota(jnp.int32, (1, CHUNK), 1)

        def place(block, _):
            span = pl.ds(pl.multiple_of(block * CHUNK, CHUNK), CHUNK)
            back = (column_ref[span, :] == lanes).astype(jnp.bfloat16)
            placed = jnp.dot(back, contribution, preferred_element_type=jnp.float32)
            if not first:
                placed = placed + out_ref[span, :].astype(jnp.float32)
            out_ref[span, :] = placed.astype(jnp.bfloat16)
            return 0

        lax.fori_loop(0, tokens // CHUNK, place, 0)

    one_chunk(0, True)

    def more(number, _):
        one_chunk(number, False)
        return 0

    lax.fori_loop(1, (routed + CHUNK - 1) // CHUNK, more, 0)


def run_expert(info, rows, lane_slots, column_slots, w_gate, w_up, w_down):
    tokens = rows.shape[0]
    return pl.pallas_call(
        expert_kernel,
        out_shape=jax.ShapeDtypeStruct((tokens, w_gate.shape[0]), jnp.bfloat16),
        in_specs=[pl.BlockSpec(memory_space=pltpu.SMEM)] + [IN_VMEM] * 6,
        out_specs=IN_VMEM,
        compiler_params=pltpu.CompilerParams(vmem_limit_bytes=60 << 20),
        name="run_expert",
    )(info, rows, lane_slots, column_slots, w_gate, w_up, w_down)


def collect_kernel(
    in_ref, out_ref, mine, other, ring_in, final, from_x,
    x_send, x_recv, z_send, z_recv, c_send, c_recv, local,
):
    s, t, plane, z, core, x, y = places()
    across = ((1 - plane) * 16 + z * 2 + core, (1 - x) * 4 + y)
    twin = (s + 1 - 2 * core, t)
    ring = [(plane * 16 + ((z + d) % 8) * 2 + core, t) for d in (1, 7)]
    greet([across, twin] + ring)
    planes = [plane, 1 - plane]

    def place(p, way, distance):
        ahead = (z + distance) % 8 if way == 0 else (z + 8 - distance) % 8
        return planes[p] * 8 + ahead

    order = [(0, 0, 4), (1, 1, 4)]
    for distance in (3, 2, 1):
        for p in range(2):
            for way in range(2):
                order.append((p, way, distance))
    order += [(1, 0, 0), (0, 0, 0)]
    loads, swaps = [], []
    for k, key in enumerate(order):
        i = place(*key)
        swap = pltpu.make_async_remote_copy(
            src_ref=in_ref.at[2 * i + 1 - core], dst_ref=other.at[i], send_sem=c_send.at[k],
            recv_sem=c_recv.at[k], device_id=twin, device_id_type=MESH,
        )
        swap.start()
        swaps.append(swap)
        load = pltpu.make_async_copy(in_ref.at[2 * i + core], mine.at[i], local.at[k])
        load.start()
        loads.append(load)

    sent = []

    def pass_on(src, dst, send_sem, recv_sem, peer):
        copy = pltpu.make_async_remote_copy(
            src_ref=src, dst_ref=dst, send_sem=send_sem, recv_sem=recv_sem,
            device_id=peer, device_id_type=MESH,
        )
        copy.start()
        sent.append(copy)

    def landed(dst, send_sem, recv_sem):
        pltpu.make_async_remote_copy(
            src_ref=dst, dst_ref=dst, send_sem=send_sem, recv_sem=recv_sem,
            device_id=twin, device_id_type=MESH,
        ).wait_recv()

    wide = lambda ref: ref[...].astype(jnp.float32)
    for k, (p, way, distance) in enumerate(order):
        i = place(p, way, distance)
        loads[k].wait()
        swaps[k].wait()
        if distance == 0:
            break
        total = wide(mine.at[i]) + wide(other.at[i])
        farther = 3 if p != way else 4
        if distance < farther:
            piece = ring_in.at[p, way, distance]
            landed(piece, z_send.at[p, way, distance], z_recv.at[p, way, distance])
            total = total + wide(piece)
        mine[i] = total.astype(jnp.bfloat16)
        pass_on(
            mine.at[i], ring_in.at[p, way, distance - 1],
            z_send.at[p, way, distance - 1], z_recv.at[p, way, distance - 1], ring[way],
        )
    loads[-1].wait()
    swaps[-1].wait()
    for p in (1, 0):
        i = planes[p] * 8 + z
        total = wide(mine.at[i]) + wide(other.at[i])
        for way in range(2):
            piece = ring_in.at[p, way, 0]
            landed(piece, z_send.at[p, way, 0], z_recv.at[p, way, 0])
            total = total + wide(piece)
        if p == 1:
            final[...] = total.astype(jnp.bfloat16)
            pass_on(final, from_x, x_send, x_recv, across)
        else:
            landed(from_x, x_send, x_recv)
            out_ref[...] = (total + wide(from_x)).astype(out_ref.dtype)
    for copy in sent:
        copy.wait_send()


def collect(parts):
    dma = pltpu.SemaphoreType.DMA
    rows = parts.shape[1:]
    vmem = lambda *lead: pltpu.VMEM(lead + rows, parts.dtype)
    return pl.pallas_call(
        collect_kernel,
        out_shape=jax.ShapeDtypeStruct(rows, jnp.bfloat16),
        in_specs=[ANY],
        out_specs=IN_VMEM,
        scratch_shapes=[
            vmem(16), vmem(16), vmem(2, 2, 4), vmem(), vmem(),
            dma(()), dma(()), dma((2, 2, 4)), dma((2, 2, 4)), dma((16,)), dma((16,)), dma((16,)),
        ],
        compiler_params=params(5, vmem_limit_bytes=40 << 20),
        name="collect",
    )(parts)


def on_device(
    tokens, segment_ids, routes, attn_gain, w_query, w_key, w_value, w_out,
    moe_gain, w_router, w_gate, w_up, w_down,
):
    tp_rank = lax.axis_index("tp")
    seq_rank = lax.axis_index("seq")
    tok_dev, width = tokens.shape
    tok_seq = tok_dev * 8
    bf16, f32 = jnp.bfloat16, jnp.float32
    block_first = seq_rank * tok_seq

    seg_row = jnp.pad(segment_ids, (0, HD - tok_dev), constant_values=-1).reshape(1, HD)
    wide, w_out_all, segs = tp_gather(tokens, w_out.reshape(2, HD // 2, width), seg_row)

    block_index = block_first + jnp.arange(tok_seq, dtype=jnp.int32)
    near = segs[:, :, 0, :tok_dev].reshape(9, tok_seq)
    near_index = block_index[None, :] - tok_seq * jnp.arange(9, dtype=jnp.int32)[:, None]
    labels = jnp.arange(6, dtype=jnp.int32)
    hits = (near[None] == labels[:, None, None]) & (near_index >= 0)[None]
    firsts = jnp.min(jnp.where(hits, near_index[None], 1 << 30), axis=(1, 2))
    starts = jnp.sum(jnp.where(near[0][:, None] == labels[None, :], firsts[None, :], 0), axis=1)
    position = (block_index - starts).astype(f32)
    inverse = ROTARY ** (-(jnp.arange(HD // 2, dtype=f32) * 2.0 / HD))
    angle = position[:, None] * inverse[None, :]
    cosine, sine = jnp.cos(angle), jnp.sin(angle)

    normed = rms_rows(wide.reshape(tok_seq, width), attn_gain).astype(bf16)
    query = rotate(jnp.dot(normed, w_query, preferred_element_type=f32), cosine, sine).astype(bf16)
    keys = rotate(jnp.dot(normed, w_key, preferred_element_type=f32), cosine, sine).astype(bf16)
    values = jnp.dot(normed, w_value, preferred_element_type=f32).astype(bf16)

    def own_rows(matrix):
        mine = lax.dynamic_slice_in_dim(matrix, tp_rank * tok_dev, tok_dev, 0)
        return jnp.transpose(mine.reshape(tok_dev, KVH, HD), (1, 0, 2))

    kv_cache = jnp.stack([own_rows(keys), own_rows(values)])
    head = tp_rank // 4
    kv_own = jnp.stack(
        [
            lax.dynamic_slice_in_dim(m, head * HD, HD, 1).reshape(4, tok_seq // 4, HD)
            for m in (keys, values)
        ],
        axis=1,
    )
    kv_all = kv_exchange(kv_own)
    attention = attend(query, starts[:, None], kv_all, block_first[None])
    by_head = heads_to_tokens(attention.reshape(8, tok_dev, HD))
    split = jnp.transpose(by_head.reshape(8, tok_dev, 2, HD // 2), (1, 2, 0, 3))
    resid = tokens.astype(f32) + jnp.dot(
        split.reshape(tok_dev, QH * HD), w_out_all.reshape(QH * HD, width), preferred_element_type=f32
    )
    moe_rows = rms_rows(resid, moe_gain).astype(bf16)
    experts = w_router.shape[1]
    logits = jnp.dot(moe_rows, w_router, preferred_element_type=f32)
    expert_ids = jnp.arange(experts, dtype=jnp.int32)
    chosen_one = routes[:, :, None] == expert_ids[None, None, :]
    chosen = jnp.sum(jnp.where(chosen_one, logits[:, None, :], 0.0), axis=-1)
    gates = jax.nn.softmax(chosen, axis=-1).astype(bf16)
    gate_table = jnp.sum(jnp.where(chosen_one, gates[:, :, None], 0), axis=1).astype(bf16)
    payload = jnp.concatenate([moe_rows, jnp.pad(gate_table, ((0, 0), (0, HD - experts)))], axis=1)

    arrived = spread(payload).reshape(32 * tok_dev, width + HD)
    my_gates = lax.dynamic_slice_in_dim(arrived[:, width:], seq_rank, 1, 1)[:, 0]
    routed = (my_gates != 0).reshape(16, HD)
    ones = routed.astype(bf16)
    upto = jnp.arange(HD)[:, None] <= jnp.arange(HD)[None, :]
    inside = jnp.dot(ones, upto.astype(bf16), preferred_element_type=f32)
    sums = inside[:, -1]
    before = jnp.sum(jnp.where(jnp.arange(16)[None, :] < jnp.arange(16)[:, None], sums[None, :], 0.0), axis=1)
    slots = jnp.where(routed, (inside + before[:, None]).astype(jnp.int32) - 1, -1)
    total = jnp.sum(sums).astype(jnp.int32)
    info = jnp.stack([seq_rank.astype(jnp.int32), total])
    parts = run_expert(
        info, arrived, slots.reshape(1, -1), slots.reshape(-1, 1), w_gate[0], w_up[0], w_down[0]
    )
    moe = collect(parts.reshape(32, tok_dev, width))
    layer_out = (resid + moe.astype(f32)).astype(bf16)
    return (layer_out, kv_cache)


def solution(mesh):
    placed = (
        P(("seq", "tp"), None),
        P(("seq", "tp")),
        P(("seq", "tp"), None),
        P(),
        P(None, "tp"),
        P(),
        P(),
        P("tp", None),
        P(),
        P(),
        P("seq", None, None),
        P("seq", None, None),
        P("seq", None, None),
    )
    return jax.shard_map(
        on_device,
        mesh=mesh,
        in_specs=placed,
        out_specs=(P(("seq", "tp"), None), P(None, None, ("seq", "tp"), None)),
        check_vma=False,
    )
```

time: 610 us -> 243 us (0.40)
  Pallas kernels: 0 us -> 212 us
  waiting for transfers between devices: 200 us -> 0 us
  blocking collectives: 171 us -> 0 us
  starting transfers between devices: 70.9 us -> 0 us
  local copies, waits for them, and re-layouts: 79.6 us -> 13.1 us
  other arithmetic: 40 us -> 11.5 us
  matrix products: 29.9 us -> 4.76 us
  between operations: 14.9 us -> 1.63 us
    pallas_call x0 -> x7, Pallas kernels: none -> 212 us  [the longest x1 50 us: collect(): pl.pallas_call(collect_kernel, out_shape=jax.ShapeDtypeStruct(rows, jnp.b...]
    reduce_scatter x2 -> x0, waiting for transfers between devices: 107 us -> none  [the longest x1 70.3 us: on_device(): lax.psum_scatter(jnp.dot(attention, w_out, preferred_element_type=jnp.flo...]
    all_to_all x3 -> x0, waiting for transfers between devices: 81.7 us -> none  [the longest x1 40.6 us: on_device(): lax.all_to_all(send_rows, 'seq', split_axis=0, concat_axis=0, tiled=True)]
    pmin x1 -> x0, blocking collectives: 80.5 us -> none  [on_device(): firsts = lax.pmin(local_first, ('seq', 'tp'))]
    all_gather x3 -> x0, blocking collectives: 80.5 us -> none  [the longest x1 28.4 us: on_device(): lax.all_gather(values_heads, 'tp', axis=0, tiled=True)]
    ppermute x8 -> x0, starting transfers between devices: 47.5 us -> none  [passed_along(): return lax.ppermute(array, axis, pairs)]
    scatter x3 -> x0, local copies, waits for them, and re-layouts: 30.9 us -> none  [the longest x1 14.6 us: on_device(): gate_of = jnp.zeros((experts * capacity,), jnp.bfloat16).at[destination]....]
    dot_general x25 -> x6, matrix products: 29.9 us -> 4.76 us  [the longest x1 2.74 us: on_device(): jnp.dot(split.reshape(tok_dev, QH * HD), w_out_all.reshape(QH * HD, width...]
  transfers between devices with their start and end apart: 15 -> 0, of which waited for: 13 -> 0; matrix products, arithmetic and copies ran while one was open for 7% -> 0% of each run, Pallas kernels for 0% -> 0%
where the time goes in v1:
time: 243 us
  Pallas kernels  212 us (87%)
  local copies, waits for them, and re-layouts  13.1 us (5%)
  other arithmetic  11.5 us (5%)
  matrix products  4.76 us (2%)
    pallas_call x1, Pallas kernels, collect(): pl.pallas_call(collect_kernel, out_shape=jax.ShapeDtypeStruct(rows, jnp.b...  50 us
    pallas_call x1, Pallas kernels, tp_gather(): pl.pallas_call(tp_gather_kernel, out_shape=(jax.ShapeDtypeStruct((8, coun...  43.6 us
    pallas_call x1, Pallas kernels, spread(): pl.pallas_call(spread_kernel, out_shape=jax.ShapeDtypeStruct((32,) + rows...  41.5 us
    pallas_call x1, Pallas kernels, kv_exchange(): pl.pallas_call(kv_kernel, out_shape=jax.ShapeDtypeStruct((9,) + kv.shape,...  32.1 us
    pallas_call x1, Pallas kernels, run_expert(): pl.pallas_call(expert_kernel, out_shape=jax.ShapeDtypeStruct((tokens, w_g...  22.4 us
    pallas_call x1, Pallas kernels, attend(): pl.pallas_call(attention_kernel, out_shape=jax.ShapeDtypeStruct((count, H...  13.8 us
    pallas_call x1, Pallas kernels, heads_to_tokens(): pl.pallas_call(heads_kernel, out_shape=jax.ShapeDtypeStruct(attention.sha...  8.22 us

profile of v1, /device:TPU:8, one launch (start us, length us, event | category | flops | bytes accessed | tf_op | source)
XLA Modules:
  0.0 242.6 jit_solution(15227388713429381115)
XLA Ops:
  0.7 1.2 pad_bitcast_fusion.seg_ref
  1.9 0.1 broadcast_compare_fusion
  2.1 1.4 copy.52
  3.5 43.6 %tp_gather.1 = (bf16[8,64,1536]{2,1,0:T(8,128)(2,1)}, bf16[2,8,64,1536]{3,2,1,0:T(8,128)(2,1)}, s32[9,8,1,128]{3,2,1,0:T(1,128)}) custom-call(bf16[64,1536]{1,0:T(8,128)(2,1)} %rows_ref.1, bf16[2,64,1536]{2,1,0:T(8,128)(2,1)} %bitcast.78, s32[1,128]{1,0:T(1,128)} %pad_bitcast_fusion.seg_ref), custom_call_target="tpu_custom_call" | custom-call | tf_op jit(solution)/shard_map/tp_gather/pallas_call | solution.py:157
  47.1 0.8 slice_reduce_fusion.3
  48.0 0.9 slice_reduce_fusion
  48.9 0.2 select_reduce_fusion
  49.1 0.1 select_reduce_fusion.2
  49.2 1.8 multiply_reduce_fusion
  51.1 0.9 copy.44.start_ref
  51.9 0.5 multiply_cosine_fusion.1
  52.5 0.4 multiply_convert_fusion
  52.9 1.6 fusion.1
  54.5 0.6 fusion.21
  55.1 0.1 subtract_convert_fusion
  55.2 0.1 constant_dynamic-slice_fusion.1
  55.4 0.1 copy.53
  55.5 0.1 copy.55
  55.6 0.3 copy-done.3
  55.9 0.6 convolution_convert_fusion
  56.5 0.6 convolution_bitcast_fusion.1
  57.1 1.4 fusion.9
  58.5 0.8 maximum_bitcast_fusion.q_ref
  59.3 0.7 pad_maximum_fusion.1.kv_ref
  60.0 0.1 pad_maximum_fusion.2
  60.1 0.6 copy.49
  60.8 32.1 %kv_exchange.1.kv_ref = bf16[9,4,2,128,128]{4,3,2,1,0:T(8,128)(2,1)} custom-call(bf16[4,2,128,128]{3,2,1,0:T(8,128)(2,1)} %pad_maximum_fusion.1.kv_ref), custom_call_target="tpu_custom_call" | custom-call | tf_op jit(solution)/shard_map/kv_exchange/pallas_call | solution.py:243
  92.9 13.8 %attend.1 = bf16[512,128]{1,0:T(8,128)(2,1)} custom-call(s32[1]{0:T(128)} %bitcast.base_ref, bf16[512,128]{1,0:T(8,128)(2,1)} %maximum_bitcast_fusion.q_ref, s32[512,1]{1,0:T(8,128)} %copy.44.start_ref, bf16[9,4,2,128,128]{4,3,2,1,0:T(8,128)(2,1)} %kv_exchange.1.kv_ref), custom_call_target="tpu_custom_call" | custom-call | tf_op jit(solution)/shard_map/attend/pallas_call | solution.py:292
  106.7 8.2 %heads_to_tokens.1 = bf16[8,64,128]{2,1,0:T(8,128)(2,1)} custom-call(bf16[8,64,128]{2,1,0:T(8,128)(2,1)} %bitcast.75), custom_call_target="tpu_custom_call" | custom-call | tf_op jit(solution)/shard_map/heads_to_tokens/pallas_call | solution.py:335
  114.9 1.0 reshape.308
  116.0 2.7 %multiply_reduce_fusion.1 = (f32[64]{0:T(128)S(1)}, f32[64,1536]{1,0:T(8,128)S(1)}) fusion(bf16[2,8,64,1536]{3,2,1,0:T(8,128)(2,1)} %get-tuple-element.7, bf16[8,64,2,64]{3,2,1,0:T(2,128)(2,1)S(1)} %reshape.308, bf16[64,1536]{1,0:T(8,128)(2,1)S(1)} %copy-done.4), kind=kOutput, calls=%fused_computation.14 | convolution fusion | flops 201719744 | bytes 3866880 | tf_op jit(solution)/shard_map/dot_general | solution.py:638
  118.8 0.1 multiply_convert_fusion.1
  118.9 0.1 fusion.22
  119.2 0.1 copy.46
  119.3 0.7 fusion.14.rows_ref
  120.0 41.5 %spread.1 = bf16[32,64,1664]{2,1,0:T(8,128)(2,1)} custom-call(bf16[64,1664]{1,0:T(8,128)(2,1)} %fusion.14.rows_ref), custom_call_target="tpu_custom_call" | custom-call | tf_op jit(solution)/shard_map/spread/pallas_call | solution.py:418
  161.4 1.1 slice.38
  162.5 0.5 compare_reduce_fusion
  163.0 0.1 fusion.17
  163.2 0.7 slice_reduce_fusion.1
  164.5 0.6 pad_add_fusion.info_ref
  165.1 0.1 select_reduce_fusion.3
  165.2 0.1 add_select_fusion
  165.3 1.4 copy.47.column_ref
  166.7 22.4 %run_expert.1 = bf16[2048,1536]{1,0:T(8,128)(2,1)} custom-call(s32[2]{0:T(128)} %pad_add_fusion.info_ref, bf16[2048,1664]{1,0:T(8,128)(2,1)} %bitcast.66, s32[1,2048]{1,0:T(1,128)} %bitcast.83, s32[2048,1]{1,0:T(8,128)} %copy.47.column_ref, bf16[1536,768]{1,0:T(8,128)(2,1)} %bitcast.67, bf16[1536,768]{1,0:T(8,128)(2,1)} %bitcast.68, bf16[768,1536]{1,0:T(8,128)(2,1)} %bitcast.69), custom_call_target="tpu_custom_call" | custom-call | tf_op jit(solution)/shard_map/run_expert/pallas_call | solution.py:475
  189.1 2.8 %copy-done.1 = bf16[2048,1536]{1,0:T(8,128)(2,1)S(1)} copy-done((bf16[2048,1536]{1,0:T(8,128)(2,1)S(1)}, bf16[2048,1536]{1,0:T(8,128)(2,1)}, u32[]{:S(2)}) %copy-start.1) | copy-done | bytes 6291480
  191.9 50.0 %collect.1 = bf16[64,1536]{1,0:T(8,128)(2,1)S(1)} custom-call(bf16[32,64,1536]{2,1,0:T(8,128)(2,1)S(1)} %bitcast.64), custom_call_target="tpu_custom_call" | custom-call | tf_op jit(solution)/shard_map/collect/pallas_call | solution.py:576
  241.8 0.7 add_convert_fusion
  (40 shorter events, 0.6 us)
Async XLA Ops:
  0.6 55.0 %copy-start = (bf16[1536,256]{1,0:T(8,128)(2,1)S(1)}, bf16[1536,256]{1,0:T(8,128)(2,1)}, u32[]{:S(2)}) copy-start(bf16[1536,256]{1,0:T(8,128)(2,1)} %param.19) | copy-start | bytes 2359300
  0.6 51.8 %copy-start.8 = (f32[1536]{0:T(1024)S(1)}, f32[1536]{0:T(1024)}, u32[]{:S(2)}) copy-start(f32[1536]{0:T(1024)} %param.16) | copy-start | bytes 18436
  47.1 5.4 %copy-start.2 = (bf16[8,64,1536]{2,1,0:T(8,128)(2,1)S(1)}, bf16[8,64,1536]{2,1,0:T(8,128)(2,1)}, u32[]{:S(2)}) copy-start(bf16[8,64,1536]{2,1,0:T(8,128)(2,1)} %get-tuple-element.5) | copy-start | bytes 4718596
  54.5 1.4 copy-start.3
  55.2 1.3 copy-start.5
  92.8 23.1 %copy-start.4 = (bf16[64,1536]{1,0:T(8,128)(2,1)S(1)}, bf16[64,1536]{1,0:T(8,128)(2,1)}, u32[]{:S(2)}) copy-start(bf16[64,1536]{1,0:T(8,128)(2,1)} %rows_ref.1) | copy-start | bytes 589828
  106.7 12.1 %copy-start.9 = (f32[1536]{0:T(1024)S(1)}, f32[1536]{0:T(1024)}, u32[]{:S(2)}) copy-start(f32[1536]{0:T(1024)} %param.21) | copy-start | bytes 18436
  116.0 2.9 %copy-start.6 = (bf16[1536,32]{0,1:T(8,128)(2,1)S(1)}, bf16[1536,32]{0,1:T(8,128)(2,1)}, u32[]{:S(2)}) copy-start(bf16[1536,32]{0,1:T(8,128)(2,1)} %param.22) | copy-start | bytes 294916
  116.0 3.0 %copy-start.10 = (s32[64,4]{0,1:T(4,128)S(1)}, s32[64,4]{0,1:T(4,128)}, u32[]{:S(2)}) copy-start(s32[64,4]{0,1:T(4,128)} %param.15) | copy-start | bytes 3076
  165.3 1.4 copy-start.7
  189.1 2.8 %copy-start.1 = (bf16[2048,1536]{1,0:T(8,128)(2,1)S(1)}, bf16[2048,1536]{1,0:T(8,128)(2,1)}, u32[]{:S(2)}) copy-start(bf16[2048,1536]{1,0:T(8,128)(2,1)} %run_expert.1) | copy-start | bytes 18874372

commit v2 on v1

--- a/solution.py
+++ b/solution.py
@@ -53,294 +53,320 @@
     return pltpu.CompilerParams(collective_id=number, has_side_effects=True, **more)
 
 
+class Copies:
+    def __init__(self, anyone):
+        self.anyone, self.sent = anyone, []
+
+    def start(self, src, dst, send, recv, peer):
+        copy = pltpu.make_async_remote_copy(
+            src_ref=src, dst_ref=dst, send_sem=send, recv_sem=recv,
+            device_id=peer, device_id_type=MESH,
+        )
+        copy.start()
+        self.sent.append(copy)
+
+    def landed(self, dst, send, recv):
+        pltpu.make_async_remote_copy(
+            src_ref=dst, dst_ref=dst, send_sem=send, recv_sem=recv,
+            device_id=self.anyone, device_id_type=MESH,
+        ).wait_recv()
+
+    def drain(self):
+        for copy in self.sent:
+            copy.wait_send()
+
+
 def tp_gather_kernel(
-    rows_ref, weight_ref, seg_ref, wide_ref, full_ref, segs_ref,
-    send, recv, seg_send, seg_recv, far_send, far_recv, half_send, half_recv, local,
+    rows_ref, seg_ref, out, segs_ref,
+    send, recv, seg_send, seg_recv, far_send, far_recv, local,
 ):
     s, t, _, _, core, x, y = places()
     across = (1 - x) * 4
     own = x * 4
     up, down, two = (y + 1) % 4, (y + 3) % 4, (y + 2) % 4
     xp, yn, yp = (s, across + y), (s, own + up), (s, own + down)
-    twin = (s + 1 - 2 * core, t)
     tp_peers = [(s, (t + k) % 8) for k in range(1, 8)]
     ahead = [((s + k) % 32, t) for k in range(1, 9)]
     behind = [((s + 32 - k) % 32, t) for k in range(1, 9)]
-    greet(tp_peers + ahead + behind + [twin])
+    greet(tp_peers + ahead + behind)
+    moves = Copies(xp)
+
+    def go(number, src, dst, peer):
+        moves.start(src, dst, send.at[number], recv.at[number], peer)
+
+    def landed(number, dst):
+        moves.landed(dst, send.at[number], recv.at[number])
 
     seg_own = pltpu.make_async_copy(seg_ref, segs_ref.at[0, t], local.at[0])
     seg_own.start()
-    seg_copies = []
     for k, peer in enumerate(tp_peers):
-        copy = pltpu.make_async_remote_copy(
-            src_ref=seg_ref, dst_ref=segs_ref.at[0, t], send_sem=seg_send.at[k],
-            recv_sem=seg_recv.at[k], device_id=peer, device_id_type=MESH,
-        )
-        copy.start()
-        seg_copies.append(copy)
-
-    sent = []
-
-    def pass_on(bank, number, src, dst, peer):
-        copy = pltpu.make_async_remote_copy(
-            src_ref=src, dst_ref=dst, send_sem=send.at[bank, number],
-            recv_sem=recv.at[bank, number], device_id=peer, device_id_type=MESH,
-        )
-        copy.start()
-        sent.append(copy)
-
-    def landed(bank, number, dst):
-        pltpu.make_async_remote_copy(
-            src_ref=dst, dst_ref=dst, send_sem=send.at[bank, number],
-            recv_sem=recv.at[bank, number], device_id=xp, device_id_type=MESH,
-        ).wait_recv()
-
-    banks = [(rows_ref, wide_ref), (weight_ref.at[core], full_ref.at[core])]
-    locals_ = []
-    for bank, (src, out) in enumerate(banks):
-        copy = pltpu.make_async_copy(src, out.at[t], local.at[1 + bank])
-        copy.start()
-        locals_.append(copy)
-        pass_on(bank, 0, src, out.at[t], xp)
-        pass_on(bank, 1, src, out.at[t], yn)
-        pass_on(bank, 2, src, out.at[t], yp)
-    for copy in seg_copies:
-        copy.wait()
+        moves.start(seg_ref, segs_ref.at[0, t], seg_send.at[k], seg_recv.at[k], peer)
+    go(0, rows_ref, out.at[t], xp)
+    go(1, rows_ref, out.at[t], yn)
+    go(2, rows_ref, out.at[t], yp)
+    rows_own = pltpu.make_async_copy(rows_ref, out.at[t], local.at[1])
+    rows_own.start()
     seg_own.wait()
-    far_copies = []
+    for k in range(7):
+        moves.landed(segs_ref.at[0, t], seg_send.at[k], seg_recv.at[k])
     for k, peer in enumerate(ahead):
-        copy = pltpu.make_async_remote_copy(
-            src_ref=segs_ref.at[0], dst_ref=segs_ref.at[k + 1], send_sem=far_send.at[k],
-            recv_sem=far_recv.at[k], device_id=peer, device_id_type=MESH,
-        )
-        copy.start()
-        far_copies.append(copy)
+        moves.start(segs_ref.at[0], segs_ref.at[k + 1], far_send.at[k], far_recv.at[k], peer)
     low, high = pl.ds(0, 32), pl.ds(32, 32)
-    for bank, (src, out) in enumerate(banks):
-        landed(bank, 0, out.at[across + y])
-        pass_on(bank, 3, out.at[across + y], out.at[across + y], yn)
-        pass_on(bank, 4, out.at[across + y], out.at[across + y], yp)
-        landed(bank, 1, out.at[own + down])
-        pass_on(bank, 5, out.at[own + down, low], out.at[own + down, low], yn)
-        landed(bank, 2, out.at[own + up])
-        pass_on(bank, 6, out.at[own + up, high], out.at[own + up, high], yp)
-        landed(bank, 3, out.at[across + down])
-        pass_on(bank, 7, out.at[across + down, low], out.at[across + down, low], yn)
-        landed(bank, 4, out.at[across + up])
-        pass_on(bank, 8, out.at[across + up, high], out.at[across + up, high], yp)
-    for bank, (src, out) in enumerate(banks):
-        landed(bank, 5, out.at[own + two, low])
-        landed(bank, 6, out.at[own + two, high])
-        landed(bank, 7, out.at[across + two, low])
-        landed(bank, 8, out.at[across + two, high])
-    for copy in locals_:
-        copy.wait()
-    halves = pltpu.make_async_remote_copy(
-        src_ref=full_ref.at[core], dst_ref=full_ref.at[core], send_sem=half_send,
-        recv_sem=half_recv, device_id=twin, device_id_type=MESH,
-    )
-    halves.start()
-    for copy in sent:
-        copy.wait_send()
-    for copy in far_copies:
-        copy.wait()
-    halves.wait_send()
-    pltpu.make_async_remote_copy(
-        src_ref=full_ref.at[1 - core], dst_ref=full_ref.at[1 - core], send_sem=half_send,
-        recv_sem=half_recv, device_id=twin, device_id_type=MESH,
-    ).wait_recv()
-
-
-def tp_gather(rows, weight, seg):
+    landed(0, out.at[across + y])
+    go(3, out.at[across + y], out.at[across + y], yn)
+    go(4, out.at[across + y], out.at[across + y], yp)
+    landed(1, out.at[own + down])
+    go(5, out.at[own + down, low], out.at[own + down, low], yn)
+    landed(2, out.at[own + up])
+    go(6, out.at[own + up, high], out.at[own + up, high], yp)
+    landed(3, out.at[across + down])
+    go(7, out.at[across + down, low], out.at[across + down, low], yn)
+    landed(4, out.at[across + up])
+    go(8, out.at[across + up, high], out.at[across + up, high], yp)
+    landed(5, out.at[own + two, low])
+    landed(6, out.at[own + two, high])
+    landed(7, out.at[across + two, low])
+    landed(8, out.at[across + two, high])
+    rows_own.wait()
+    for k in range(8):
+        moves.landed(segs_ref.at[k + 1], far_send.at[k], far_recv.at[k])
+    moves.drain()
+
+
+def tp_gather(rows, seg):
     count, width = rows.shape
     dma = pltpu.SemaphoreType.DMA
     return pl.pallas_call(
         tp_gather_kernel,
         out_shape=(
             jax.ShapeDtypeStruct((8, count, width), rows.dtype),
-            jax.ShapeDtypeStruct((2, 8, 64, width), weight.dtype),
             jax.ShapeDtypeStruct((9, 8, 1, 128), jnp.int32),
         ),
-        in_specs=[ANY] * 3,
-        out_specs=(ANY,) * 3,
-        scratch_shapes=[
-            dma((2, 9)), dma((2, 9)), dma((7,)), dma((7,)), dma((8,)), dma((8,)),
-            dma(()), dma(()), dma((3,)),
-        ],
-        compiler_params=params(1),
+        in_specs=[IN_VMEM] * 2,
+        out_specs=(IN_VMEM,) * 2,
+        scratch_shapes=[dma((9,)), dma((9,)), dma((7,)), dma((7,)), dma((8,)), dma((8,)), dma((2,))],
+        compiler_params=params(1, vmem_limit_bytes=16 << 20),
         name="tp_gather",
-    )(rows, weight, seg)
-
-
-def kv_kernel(kv_ref, out_ref, z_send, z_recv, y_send, y_recv, c_send, c_recv, local):
+    )(rows, seg)
+
+
+TILE = 128
+
+
+def attention_kernel(
+    kv_ref, q_ref, start_ref, tokens_ref, w_out_ref, gain_ref, router_ref, routes_ref,
+    resid_ref, payload_ref,
+    slots, w_full, peak, total, mixed, heads_out, heads_in,
+    z_send, z_recv, y_send, y_recv, c_send, c_recv,
+    w_send, w_recv, t_send, t_recv, h_send, h_recv, local,
+):
     s, t, _, _, core, x, y = places()
-    own = x * 4
+    across, own = (1 - x) * 4, x * 4
     up, down, two = (y + 1) % 4, (y + 3) % 4, (y + 2) % 4
-    ahead, behind = ((s + 2) % 32, t), ((s + 30) % 32, t)
-    yn, yp = (s, own + up), (s, own + down)
+    far = ((s + 4) % 32, t)
+    near = ((s + 2) % 32, t)
+    xp, yn, yp = (s, across + y), (s, own + up), (s, own + down)
     twin = (s + 1 - 2 * core, t)
-    greet([ahead, behind, yn, yp, twin])
-    first = pltpu.make_async_copy(kv_ref, out_ref.at[0], local)
-    first.start()
-    sent = []
-
-    def pass_on(src, dst, send_sem, recv_sem, peer):
-        copy = pltpu.make_async_remote_copy(
-            src_ref=src, dst_ref=dst, send_sem=send_sem, recv_sem=recv_sem,
-            device_id=peer, device_id_type=MESH,
+    tp_peers = [(s, (t + k) % 8) for k in range(1, 8)]
+    greet(tp_peers + [twin, near, far, ((s + 30) % 32, t), ((s + 28) % 32, t)])
+    moves = Copies(twin)
+    count = q_ref.shape[0]
+
+    def w_piece(rank, half, first=0, rows=64):
+        return w_full.at[rank, pl.ds(pl.multiple_of(half * 64 + first, 32), rows)]
+
+    def w_go(number, rank, peer, first=0, rows=64):
+        piece = w_piece(rank, core, first, rows)
+        moves.start(piece, piece, w_send.at[number], w_recv.at[number], peer)
+
+    def w_landed(number, rank, first=0, rows=64):
+        moves.landed(w_piece(rank, core, first, rows), w_send.at[number], w_recv.at[number])
+
+    def w_twin(number, rank):
+        piece = w_piece(rank, core)
+        moves.start(piece, piece, t_send.at[number], t_recv.at[number], twin)
+
+    kv_own = pltpu.make_async_copy(kv_ref, slots.at[0], local.at[0])
+    kv_own.start()
+    w_own = pltpu.make_async_copy(w_out_ref, w_full.at[t], local.at[1])
+    w_own.start()
+    moves.start(kv_ref.at[y], slots.at[2, y], z_send.at[0], z_recv.at[0], near)
+    moves.start(kv_ref.at[y], slots.at[4, y], z_send.at[1], z_recv.at[1], far)
+    w_own.wait()
+    w_go(0, t, xp)
+    w_go(1, t, yn)
+    w_go(2, t, yp)
+
+    peak[...] = jnp.full_like(peak, NEGATIVE)
+    total[...] = jnp.zeros_like(total)
+    mixed[...] = jnp.zeros_like(mixed)
+    base = s * count
+    unit = math.log2(math.e) / math.sqrt(HD)
+
+    def attend(j):
+        def tile(number, _):
+            rows = pl.ds(pl.multiple_of(number * TILE, TILE), TILE)
+            keys = slots[j, :, 0].reshape(count, HD)
+            values = slots[j, :, 1].reshape(count, HD)
+            scores = lax.dot_general(
+                q_ref[rows, :], keys, (((1,), (1,)), ((), ())), preferred_element_type=jnp.float32
+            ) * unit
+            key_index = base - j * count + lax.broadcasted_iota(jnp.int32, (1, count), 1)
+            allowed = key_index >= start_ref[rows, :]
+            if j == 0:
+                query_index = base + number * TILE + lax.broadcasted_iota(jnp.int32, (TILE, 1), 0)
+                allowed = allowed & (key_index <= query_index)
+            masked = jnp.where(allowed, scores, NEGATIVE)
+            old = peak[rows, :]
+            newest = jnp.maximum(old, jnp.max(masked, axis=-1, keepdims=True))
+            factor = jnp.exp2(old - newest)
+            weights = jnp.exp2(masked - newest)
+            total[rows, :] = total[rows, :] * factor + jnp.sum(weights, axis=-1, keepdims=True)
+            mixed[rows, :] = mixed[rows, :] * factor + jnp.dot(
+                weights.astype(jnp.bfloat16), values, preferred_element_type=jnp.float32
+            )
+            peak[rows, :] = newest
+            return 0
+
+        lax.fori_loop(0, count // TILE, tile, 0)
+
+    def z_step(k, onward):
+        piece = slots.at[2 * k, y]
+        moves.landed(piece, z_send.at[k - 1], z_recv.at[k - 1])
+        if onward:
+            moves.start(piece, slots.at[2 * k + 4, y], z_send.at[k + 1], z_recv.at[k + 1], far)
+        moves.start(piece, piece, y_send.at[k - 1, 0], y_recv.at[k - 1, 0], yn)
+        moves.start(piece, piece, y_send.at[k - 1, 1], y_recv.at[k - 1, 1], yp)
+
+    def y_step(k):
+        moves.landed(slots.at[2 * k, down], y_send.at[k - 1, 0], y_recv.at[k - 1, 0])
+        piece = slots.at[2 * k, down, 0]
+        moves.start(piece, piece, y_send.at[k - 1, 2], y_recv.at[k - 1, 2], yn)
+        moves.landed(slots.at[2 * k, up], y_send.at[k - 1, 1], y_recv.at[k - 1, 1])
+        piece = slots.at[2 * k, up, 1]
+        moves.start(piece, piece, y_send.at[k - 1, 3], y_recv.at[k - 1, 3], yp)
+
+    def block_step(k):
+        moves.landed(slots.at[2 * k, two, 0], y_send.at[k - 1, 2], y_recv.at[k - 1, 2])
+        moves.landed(slots.at[2 * k, two, 1], y_send.at[k - 1, 3], y_recv.at[k - 1, 3])
+        moves.start(
+            slots.at[2 * k - 2 + 2 * core], slots.at[2 * k - 1], c_send.at[k - 1], c_recv.at[k - 1], twin
         )
-        copy.start()
-        sent.append(copy)
-
-    def landed(dst, send_sem, recv_sem):
-        pltpu.make_async_remote_copy(
-            src_ref=dst, dst_ref=dst, send_sem=send_sem, recv_sem=recv_sem,
-            device_id=twin, device_id_type=MESH,
-        ).wait_recv()
-
-    def to_twin(i):
-        pass_on(
-            out_ref.at[2 * i + 2 * core], out_ref.at[2 * i + 1],
-            c_send.at[i], c_recv.at[i], twin,
-        )
-
-    pass_on(kv_ref.at[y], out_ref.at[2, y], z_send.at[0], z_recv.at[0], ahead)
-    first.wait()
-
-    def middle(k):
-        landed(out_ref.at[2 * k, down], y_send.at[k - 1, 0], y_recv.at[k - 1, 0])
-        piece = out_ref.at[2 * k, down, 0]
-        pass_on(piece, piece, y_send.at[k - 1, 2], y_recv.at[k - 1, 2], yn)
-        landed(out_ref.at[2 * k, up], y_send.at[k - 1, 1], y_recv.at[k - 1, 1])
-        piece = out_ref.at[2 * k, up, 1]
-        pass_on(piece, piece, y_send.at[k - 1, 3], y_recv.at[k - 1, 3], yp)
-
-    def last(k):
-        landed(out_ref.at[2 * k, two, 0], y_send.at[k - 1, 2], y_recv.at[k - 1, 2])
-        landed(out_ref.at[2 * k, two, 1], y_send.at[k - 1, 3], y_recv.at[k - 1, 3])
-
-    for k in range(1, 7):
-        if k <= 4:
-            landed(out_ref.at[2 * k, y], z_send.at[k - 1], z_recv.at[k - 1])
-            piece = out_ref.at[2 * k, y]
-            if k < 4:
-                pass_on(piece, out_ref.at[2 * k + 2, y], z_send.at[k], z_recv.at[k], ahead)
-            pass_on(piece, piece, y_send.at[k - 1, 0], y_recv.at[k - 1, 0], yn)
-            pass_on(piece, piece, y_send.at[k - 1, 1], y_recv.at[k - 1, 1], yp)
-        if 1 <= k - 1 <= 4:
-            middle(k - 1)
-        if 1 <= k - 2 <= 4:
-            last(k - 2)
-            to_twin(k - 3)
-    for copy in sent:
-        copy.wait_send()
-    for i in range(4):
-        landed(out_ref.at[2 * i + 1], c_send.at[i], c_recv.at[i])
-
-
-def kv_exchange(kv):
+
+    def twin_step(k):
+        moves.landed(slots.at[2 * k - 1], c_send.at[k - 1], c_recv.at[k - 1])
+        attend(2 * k - 1)
+
+    kv_own.wait()
+    attend(0)
+    z_step(1, True)
+    z_step(2, True)
+    w_landed(0, across + y)
+    w_go(3, across + y, yn)
+    w_go(4, across + y, yp)
+    w_twin(0, across + y)
+    y_step(1)
+    y_step(2)
+    w_landed(1, own + down)
+    w_go(5, own + down, yn, 0, 32)
+    w_twin(1, own + down)
+    w_landed(2, own + up)
+    w_go(6, own + up, yp, 32, 32)
+    w_twin(2, own + up)
+    block_step(1)
+    attend(2)
+    z_step(3, False)
+    z_step(4, False)
+    block_step(2)
+    twin_step(1)
+    y_step(3)
+    y_step(4)
+    attend(4)
+    w_landed(3, across + down)
+    w_go(7, across + down, yn, 0, 32)
+    w_twin(3, across + down)
+    w_landed(4, across + up)
+    w_go(8, across + up, yp, 32, 32)
+    w_twin(4, across + up)
+    block_step(3)
+    twin_step(2)
+    block_step(4)
+    attend(6)
+    twin_step(3)
+    w_landed(5, own + two, 0, 32)
+    w_landed(6, own + two, 32, 32)
+    w_twin(5, own + two)
+    attend(8)
+    w_landed(7, across + two, 0, 32)
+    w_landed(8, across + two, 32, 32)
+    w_twin(6, across + two)
+    twin_step(4)
+
+    for rank in range(8):
+        rows = pl.ds(rank * 64, 64)
+        heads_out[rank] = (mixed[rows, :] / total[rows, :]).astype(heads_out.dtype)
+    heads_own = pltpu.make_async_copy(heads_out.at[t], heads_in.at[t], local.at[0])
+    heads_own.start()
+    for k, peer in enumerate(tp_peers):
+        moves.start(heads_out.at[peer[1]], heads_in.at[t], h_send.at[k], h_recv.at[k], peer)
+    ranks = [across + y, own + down, own + up, across + down, across + up, own + two, across + two]
+    for number, rank in enumerate(ranks):
+        moves.landed(w_piece(rank, 1 - core), t_send.at[number], t_recv.at[number])
+    heads_own.wait()
+    for k in range(7):
+        moves.landed(heads_in.at[t], h_send.at[k], h_recv.at[k])
+    attention = jnp.concatenate([heads_in[rank] for rank in range(8)], axis=1)
+    width = tokens_ref.shape[1]
+    resid = tokens_ref[...].astype(jnp.float32) + jnp.dot(
+        attention, w_full[...].reshape(8 * HD, width), preferred_element_type=jnp.float32
+    )
+    resid_ref[...] = resid
+    moe_rows = rms_rows(resid, gain_ref[...]).astype(jnp.bfloat16)
+    payload_ref[:, :width] = moe_rows
+    logits = jnp.dot(moe_rows, router_ref[...], preferred_element_type=jnp.float32)
+    experts = logits.shape[1]
+    expert_ids = lax.broadcasted_iota(jnp.int32, logits.shape, 1)
+    routes = routes_ref[...]
+    picked = [routes[:, k : k + 1] == expert_ids for k in range(routes.shape[1])]
+    chosen = [jnp.sum(jnp.where(one, logits, 0.0), axis=1, keepdims=True) for one in picked]
+    highest = functools.reduce(jnp.maximum, chosen)
+    powers = [jnp.exp(one - highest) for one in chosen]
+    whole = functools.reduce(jnp.add, powers)
+    table = jnp.zeros_like(logits)
+    for one, power in zip(picked, powers):
+        table = jnp.where(one, power / whole, table)
+    payload_ref[:, width:] = jnp.zeros((logits.shape[0], HD), jnp.bfloat16)
+    payload_ref[:, width : width + experts] = table.astype(jnp.bfloat16)
+    moves.drain()
+
+
+def attention_layer(kv, query, starts, tokens, w_out, gain, router, routes):
     dma = pltpu.SemaphoreType.DMA
-    return pl.pallas_call(
-        kv_kernel,
-        out_shape=jax.ShapeDtypeStruct((9,) + kv.shape, kv.dtype),
-        in_specs=[ANY],
-        out_specs=ANY,
-        scratch_shapes=[dma((4,)), dma((4,)), dma((4, 4)), dma((4, 4)), dma((4,)), dma((4,)), dma(())],
-        compiler_params=params(2),
-        name="kv_exchange",
-    )(kv)
-
-
-def attention_kernel(base_ref, q_ref, start_ref, kv_ref, out_ref, peak, total, mixed):
-    step = pl.program_id(0)
-
-    @pl.when(step == 0)
-    def _():
-        peak[...] = jnp.full_like(peak, NEGATIVE)
-        total[...] = jnp.zeros_like(total)
-        mixed[...] = jnp.zeros_like(mixed)
-
-    count = q_ref.shape[0]
-    keys = kv_ref[0, :, 0].reshape(count, HD)
-    values = kv_ref[0, :, 1].reshape(count, HD)
-    scores = lax.dot_general(
-        q_ref[...], keys, (((1,), (1,)), ((), ())), preferred_element_type=jnp.float32
-    ) * (1.0 / math.sqrt(HD))
-    base = base_ref[0]
-    key_index = base - step * count + lax.broadcasted_iota(jnp.int32, (1, count), 1)
-    query_index = base + lax.broadcasted_iota(jnp.int32, (count, 1), 0)
-    allowed = (key_index >= start_ref[...]) & (key_index <= query_index)
-    masked = jnp.where(allowed, scores, NEGATIVE)
-    old = peak[...]
-    newest = jnp.maximum(old, jnp.max(masked, axis=-1, keepdims=True))
-    factor = jnp.exp(old - newest)
-    weights = jnp.exp(masked - newest)
-    total[...] = total[...] * factor + jnp.sum(weights, axis=-1, keepdims=True)
-    mixed[...] = mixed[...] * factor + jnp.dot(
-        weights.astype(jnp.bfloat16), values, preferred_element_type=jnp.float32
-    )
-    peak[...] = newest
-
-    @pl.when(step == pl.num_programs(0) - 1)
-    def _():
-        out_ref[...] = (mixed[...] / total[...]).astype(out_ref.dtype)
-
-
-def attend(query, starts, kv_all, base):
+    bf16, f32 = jnp.bfloat16, jnp.float32
+    rows, width = tokens.shape
     count = query.shape[0]
-    whole = lambda shape: pl.BlockSpec(shape, lambda j, _: (0,) * len(shape))
     return pl.pallas_call(
         attention_kernel,
-        out_shape=jax.ShapeDtypeStruct((count, HD), jnp.bfloat16),
-        grid_spec=pltpu.PrefetchScalarGridSpec(
-            num_scalar_prefetch=1,
-            grid=(9,),
-            in_specs=[
-                whole((count, HD)),
-                whole((count, 1)),
-                pl.BlockSpec((1,) + kv_all.shape[1:], lambda j, _: (j, 0, 0, 0, 0)),
-            ],
-            out_specs=whole((count, HD)),
-            scratch_shapes=[
-                pltpu.VMEM((count, 1), jnp.float32),
-                pltpu.VMEM((count, 1), jnp.float32),
-                pltpu.VMEM((count, HD), jnp.float32),
-            ],
+        out_shape=(
+            jax.ShapeDtypeStruct((rows, width), f32),
+            jax.ShapeDtypeStruct((rows, width + HD), bf16),
         ),
-        name="attend",
-    )(base, query, starts, kv_all)
-
-
-def heads_kernel(in_ref, out_ref, send, recv, local):
-    s, t, *_ = places()
-    peers = [(t + k) % 8 for k in range(1, 8)]
-    greet([(s, peer) for peer in peers])
-    own = pltpu.make_async_copy(in_ref.at[t], out_ref.at[t], local)
-    own.start()
-    copies = []
-    for k, peer in enumerate(peers):
-        copy = pltpu.make_async_remote_copy(
-            src_ref=in_ref.at[peer], dst_ref=out_ref.at[t], send_sem=send.at[k],
-            recv_sem=recv.at[k], device_id=(s, peer), device_id_type=MESH,
-        )
-        copy.start()
-        copies.append(copy)
-    own.wait()
-    for copy in copies:
-        copy.wait()
-
-
-def heads_to_tokens(attention):
-    dma = pltpu.SemaphoreType.DMA
-    return pl.pallas_call(
-        heads_kernel,
-        out_shape=jax.ShapeDtypeStruct(attention.shape, attention.dtype),
-        in_specs=[ANY],
-        out_specs=ANY,
-        scratch_shapes=[dma((7,)), dma((7,)), dma(())],
-        compiler_params=params(3),
-        name="heads_to_tokens",
-    )(attention)
+        in_specs=[IN_VMEM] * 8,
+        out_specs=(IN_VMEM,) * 2,
+        scratch_shapes=[
+            pltpu.VMEM((9,) + kv.shape, bf16),
+            pltpu.VMEM((8, HD, width), bf16),
+            pltpu.VMEM((count, 1), f32),
+            pltpu.VMEM((count, 1), f32),
+            pltpu.VMEM((count, HD), f32),
+            pltpu.VMEM((8, rows, HD), bf16),
+            pltpu.VMEM((8, rows, HD), bf16),
+            dma((4,)), dma((4,)), dma((4, 4)), dma((4, 4)), dma((4,)), dma((4,)),
+            dma((9,)), dma((9,)), dma((7,)), dma((7,)), dma((7,)), dma((7,)), dma((2,)),
+        ],
+        compiler_params=params(2, vmem_limit_bytes=32 << 20),
+        name="attention_layer",
+    )(kv, query, starts, tokens, w_out, gain, router, routes)
 
 
 def spread_kernel(rows_ref, out_ref, x_send, x_recv, z_send, z_recv, c_send, c_recv, local):
@@ -599,7 +625,7 @@
     block_first = seq_rank * tok_seq
 
     seg_row = jnp.pad(segment_ids, (0, HD - tok_dev), constant_values=-1).reshape(1, HD)
-    wide, w_out_all, segs = tp_gather(tokens, w_out.reshape(2, HD // 2, width), seg_row)
+    wide, segs = tp_gather(tokens, seg_row)
 
     block_index = block_first + jnp.arange(tok_seq, dtype=jnp.int32)
     near = segs[:, :, 0, :tok_dev].reshape(9, tok_seq)
@@ -631,23 +657,9 @@
         ],
         axis=1,
     )
-    kv_all = kv_exchange(kv_own)
-    attention = attend(query, starts[:, None], kv_all, block_first[None])
-    by_head = heads_to_tokens(attention.reshape(8, tok_dev, HD))
-    split = jnp.transpose(by_head.reshape(8, tok_dev, 2, HD // 2), (1, 2, 0, 3))
-    resid = tokens.astype(f32) + jnp.dot(
-        split.reshape(tok_dev, QH * HD), w_out_all.reshape(QH * HD, width), preferred_element_type=f32
+    resid, payload = attention_layer(
+        kv_own, query, starts[:, None], tokens, w_out, moe_gain[None], w_router, routes
     )
-    moe_rows = rms_rows(resid, moe_gain).astype(bf16)
-    experts = w_router.shape[1]
-    logits = jnp.dot(moe_rows, w_router, preferred_element_type=f32)
-    expert_ids = jnp.arange(experts, dtype=jnp.int32)
-    chosen_one = routes[:, :, None] == expert_ids[None, None, :]
-    chosen = jnp.sum(jnp.where(chosen_one, logits[:, None, :], 0.0), axis=-1)
-    gates = jax.nn.softmax(chosen, axis=-1).astype(bf16)
-    gate_table = jnp.sum(jnp.where(chosen_one, gates[:, :, None], 0), axis=1).astype(bf16)
-    payload = jnp.concatenate([moe_rows, jnp.pad(gate_table, ((0, 0), (0, HD - experts)))], axis=1)
-
     arrived = spread(payload).reshape(32 * tok_dev, width + HD)
     my_gates = lax.dynamic_slice_in_dim(arrived[:, width:], seq_rank, 1, 1)[:, 0]
     routed = (my_gates != 0).reshape(16, HD)

time: 243 us -> 209 us (0.86)
  Pallas kernels: 212 us -> 181 us
  other arithmetic: 11.5 us -> 7.64 us
  matrix products: 4.76 us -> 1.87 us
    pallas_call x1, Pallas kernels: 43.6 us -> 28 us  [tp_gather(): pl.pallas_call(tp_gather_kernel, out_shape=(jax.ShapeDtypeStruct((8, coun...]
    pallas_call x3 -> x1, Pallas kernels: 54.1 us -> 45.6 us  [attention_layer(): pl.pallas_call(attention_kernel, out_shape=(jax.ShapeDtypeStruct((rows, w...]
    pallas_call x1, Pallas kernels: 50 us -> 46 us  [collect(): pl.pallas_call(collect_kernel, out_shape=jax.ShapeDtypeStruct(rows, jnp.b...]
    dot_general x2 -> x0, matrix products: 2.88 us -> none  [the longest x1 2.74 us: on_device(): jnp.dot(split.reshape(tok_dev, QH * HD), w_out_all.reshape(QH * HD, width...]
    unnamed x24, local copies, waits for them, and re-layouts: 3.89 us -> 6.53 us
where the time goes in v2:
time: 209 us; the launch traced here: 207 us
  Pallas kernels  181 us (87%)
  local copies, waits for them, and re-layouts  14.9 us (7%)
  other arithmetic  7.64 us (4%)
    pallas_call x1, Pallas kernels, collect(): pl.pallas_call(collect_kernel, out_shape=jax.ShapeDtypeStruct(rows, jnp.b...  46 us
    pallas_call x1, Pallas kernels, attention_layer(): pl.pallas_call(attention_kernel, out_shape=(jax.ShapeDtypeStruct((rows, w...  45.6 us
    pallas_call x1, Pallas kernels, spread(): pl.pallas_call(spread_kernel, out_shape=jax.ShapeDtypeStruct((32,) + rows...  39.6 us
    pallas_call x1, Pallas kernels, tp_gather(): pl.pallas_call(tp_gather_kernel, out_shape=(jax.ShapeDtypeStruct((8, coun...  28 us
    pallas_call x1, Pallas kernels, run_expert(): pl.pallas_call(expert_kernel, out_shape=jax.ShapeDtypeStruct((tokens, w_g...  22.4 us
    unnamed x24, local copies, waits for them, and re-layouts  6.53 us

profile of v2, /device:TPU:8, one launch (start us, length us, event | category | flops | bytes accessed | tf_op | source)
XLA Modules:
  0.0 207.4 jit_solution(6059741578769888809)
XLA Ops:
  0.6 0.0 copy-start
  0.7 0.8 pad_bitcast_fusion.seg_ref
  1.5 0.7 broadcast_in_dim.45.gain_ref
  2.2 0.1 broadcast_compare_fusion
  2.3 0.1 broadcast_subtract_fusion
  2.3 0.8 copy.44.routes_ref
  3.1 1.1 copy.43.router_ref
  4.2 2.3 %copy.49 = bf16[256,1536]{1,0:T(8,128)(2,1)} copy(bf16[256,1536]{0,1:T(8,128)(2,1)} %bitcast.56) | data formatting | bytes 1572864 | tf_op jit(solution)/shard_map/dot_general | solution.py:644
  6.5 28.0 %tp_gather.1 = (bf16[8,64,1536]{2,1,0:T(8,128)(2,1)S(1)}, s32[9,8,1,128]{3,2,1,0:T(1,128)S(1)}) custom-call(bf16[64,1536]{1,0:T(8,128)(2,1)S(1)} %copy-done.2, s32[1,128]{1,0:T(1,128)S(1)} %pad_bitcast_fusion.seg_ref), custom_call_target="tpu_custom_call" | custom-call | tf_op jit(solution)/shard_map/tp_gather/pallas_call | solution.py:139
  34.5 0.1 eq.30
  34.6 0.1 slice_reduce_fusion
  34.7 0.1 eq.34
  34.8 0.2 select_reduce_fusion
  34.9 0.1 select_reduce_fusion.1
  35.0 0.4 multiply_reduce_fusion
  35.4 0.1 rsqrt.13
  35.5 0.1 copy.42.start_ref
  35.7 0.5 multiply_cosine_fusion.1
  36.2 0.4 multiply_convert_fusion
  36.7 1.6 fusion.1
  38.2 0.6 fusion.13
  38.8 0.1 subtract_convert_fusion
  39.0 0.7 constant_dynamic-slice_fusion.1
  39.7 0.1 copy.50
  39.8 0.9 copy.52
  40.8 0.0 copy-start.7
  40.8 0.6 convolution_convert_fusion
  41.4 0.4 copy-done.7
  41.8 0.6 convolution_bitcast_fusion
  42.4 1.2 fusion.7
  43.6 0.1 maximum_bitcast_fusion.q_ref
  43.8 45.6 %attention_layer.1 = (f32[64,1536]{1,0:T(8,128)S(1)}, bf16[64,1664]{1,0:T(8,128)(2,1)S(1)}) custom-call(bf16[4,2,128,128]{3,2,1,0:T(8,128)(2,1)S(1)} %pad_maximum_fusion.1.kv_ref, bf16[512,128]{1,0:T(8,128)(2,1)S(1)} %maximum_bitcast_fusion.q_ref, s32[512,1]{1,0:T(8,128)S(1)} %copy.42.start_ref, bf16[64,1536]{1,0:T(8,128)(2,1)S(1)} %copy-done.2, ...), custom_call_target="tpu_custom_call" | custom-call | tf_op jit(solution)/shard_map/attention_layer/pallas_call | solution.py:348
  89.4 0.7 copy-done.4
  90.1 0.1 pad_maximum_fusion.2
  90.2 0.6 copy.47
  90.8 39.6 %spread.1 = bf16[32,64,1664]{2,1,0:T(8,128)(2,1)} custom-call(bf16[64,1664]{1,0:T(8,128)(2,1)} %copy-done.4), custom_call_target="tpu_custom_call" | custom-call | tf_op jit(solution)/shard_map/spread/pallas_call | solution.py:444
  130.4 1.1 slice.38
  131.5 0.5 compare_reduce_fusion
  132.0 0.1 fusion.11
  132.1 0.7 slice_reduce_fusion.1
  133.4 0.6 pad_add_fusion.info_ref
  134.0 0.1 select_reduce_fusion.2
  134.1 0.1 add_select_fusion
  134.2 1.4 copy.45.column_ref
  135.6 22.4 %run_expert.1 = bf16[2048,1536]{1,0:T(8,128)(2,1)} custom-call(s32[2]{0:T(128)} %pad_add_fusion.info_ref, bf16[2048,1664]{1,0:T(8,128)(2,1)} %bitcast.49, s32[1,2048]{1,0:T(1,128)} %bitcast.64, s32[2048,1]{1,0:T(8,128)} %copy.45.column_ref, bf16[1536,768]{1,0:T(8,128)(2,1)} %bitcast.50, bf16[1536,768]{1,0:T(8,128)(2,1)} %bitcast.51, bf16[768,1536]{1,0:T(8,128)(2,1)} %bitcast.52), custom_call_target="tpu_custom_call" | custom-call | tf_op jit(solution)/shard_map/run_expert/pallas_call | solution.py:501
  158.0 2.8 %copy-done.1 = bf16[2048,1536]{1,0:T(8,128)(2,1)S(1)} copy-done((bf16[2048,1536]{1,0:T(8,128)(2,1)S(1)}, bf16[2048,1536]{1,0:T(8,128)(2,1)}, u32[]{:S(2)}) %copy-start.1) | copy-done | bytes 6291480
  160.7 46.0 %collect.1 = bf16[64,1536]{1,0:T(8,128)(2,1)S(1)} custom-call(bf16[32,64,1536]{2,1,0:T(8,128)(2,1)S(1)} %bitcast.47), custom_call_target="tpu_custom_call" | custom-call | tf_op jit(solution)/shard_map/collect/pallas_call | solution.py:602
  206.7 0.7 add_convert_fusion
  (27 shorter events, 0.2 us)
Async XLA Ops:
  0.6 40.2 %copy-start = (bf16[1536,256]{1,0:T(8,128)(2,1)S(1)}, bf16[1536,256]{1,0:T(8,128)(2,1)}, u32[]{:S(2)}) copy-start(bf16[1536,256]{1,0:T(8,128)(2,1)} %param.19) | copy-start | bytes 2359300
  0.6 5.9 %copy-start.2 = (bf16[64,1536]{1,0:T(8,128)(2,1)S(1)}, bf16[64,1536]{1,0:T(8,128)(2,1)}, u32[]{:S(2)}) copy-start(bf16[64,1536]{1,0:T(8,128)(2,1)} %tokens_ref.1) | copy-start | bytes 589828
  2.2 34.0 %copy-start.9 = (f32[1536]{0:T(1024)S(1)}, f32[1536]{0:T(1024)}, u32[]{:S(2)}) copy-start(f32[1536]{0:T(1024)} %param.16) | copy-start | bytes 18436
  36.6 1.6 copy-start.6
  38.2 2.6 %copy-start.5 = (bf16[512,1536]{1,0:T(8,128)(2,1)S(1)}, bf16[512,1536]{1,0:T(8,128)(2,1)}, u32[]{:S(2)}) copy-start(bf16[512,1536]{1,0:T(8,128)(2,1)} %fusion.1) | copy-start | bytes 4718596
  40.8 1.0 copy-start.7
  41.8 2.0 copy-start.3
  89.4 0.7 copy-start.4
  134.2 1.4 copy-start.8
  158.0 2.8 %copy-start.1 = (bf16[2048,1536]{1,0:T(8,128)(2,1)S(1)}, bf16[2048,1536]{1,0:T(8,128)(2,1)}, u32[]{:S(2)}) copy-start(bf16[2048,1536]{1,0:T(8,128)(2,1)} %run_expert.1) | copy-start | bytes 18874372

commit v3 on v2

--- a/solution.py
+++ b/solution.py
@@ -369,74 +369,112 @@
     )(kv, query, starts, tokens, w_out, gain, router, routes)
 
 
-def spread_kernel(rows_ref, out_ref, x_send, x_recv, z_send, z_recv, c_send, c_recv, local):
+HALF = 32
+
+
+def ring_places():
     s, t, plane, z, core, x, y = places()
     across = ((1 - plane) * 16 + z * 2 + core, (1 - x) * 4 + y)
     twin = (s + 1 - 2 * core, t)
     ring = [(plane * 16 + ((z + d) % 8) * 2 + core, t) for d in (1, 7)]
+    return s, z, core, [plane, 1 - plane], across, twin, ring
+
+
+def spread_kernel(
+    rows_ref, out_ref, ax_send, ax_recv, az_send, az_recv,
+    bx_send, bx_recv, bz_send, bz_recv, c_send, c_recv, local,
+):
+    s, z, core, planes, across, twin, ring = ring_places()
     greet([across, twin] + ring)
-    planes = [plane, 1 - plane]
+    moves = Copies(twin)
+    part_a, part_b = pl.ds(0, HALF), pl.ds(HALF, HALF)
+    quarters = [pl.ds(HALF, HALF // 2), pl.ds(HALF + HALF // 2, HALF // 2)]
 
     def slot(p, way, distance):
         back = (z + 8 - distance) % 8 if way == 0 else (z + distance) % 8
         return planes[p] * 16 + back * 2 + core
 
-    sent = []
-
-    def pass_on(src, dst, send_sem, recv_sem, peer):
-        copy = pltpu.make_async_remote_copy(
-            src_ref=src, dst_ref=dst, send_sem=send_sem, recv_sem=recv_sem,
-            device_id=peer, device_id_type=MESH,
-        )
-        copy.start()
-        sent.append(copy)
-
-    def landed(dst, send_sem, recv_sem):
-        pltpu.make_async_remote_copy(
-            src_ref=dst, dst_ref=dst, send_sem=send_sem, recv_sem=recv_sem,
-            device_id=twin, device_id_type=MESH,
-        ).wait_recv()
-
-    def travels(p, way, distance):
+    twins = []
+
+    def to_twin(src, block, part):
+        k = len(twins)
+        twins.append(part)
+        moves.start(src, out_ref.at[block, part], c_send.at[k], c_recv.at[k], twin)
+
+    crossed = []
+
+    def cross(src, block):
+        k = len(crossed)
+        crossed.append(k)
+        moves.start(src, out_ref.at[block, part_b], bx_send.at[k], bx_recv.at[k], across)
+
+    def a_travels(p, way, distance):
         return distance <= 3 or (distance == 4 and p == way)
 
-    twins = []
-
-    def to_twin(src, block):
-        k = len(twins)
-        twins.append(k)
-        pass_on(src, out_ref.at[block], c_send.at[k], c_recv.at[k], twin)
+    def a_arrives(p, way, distance):
+        if not a_travels(p, way, distance):
+            return
+        block, k = slot(p, way, distance), distance - 1
+        piece = out_ref.at[block, part_a]
+        moves.landed(piece, az_send.at[p, way, k], az_recv.at[p, way, k])
+        if a_travels(p, way, distance + 1):
+            moves.start(piece, piece, az_send.at[p, way, k + 1], az_recv.at[p, way, k + 1], ring[way])
+        to_twin(piece, block, part_a)
+
+    def b_arrives(way, distance):
+        block, k = slot(0, way, distance), distance - 1
+        if distance == 4:
+            piece = out_ref.at[block, quarters[way]]
+            moves.landed(piece, bz_send.at[way, k], bz_recv.at[way, k])
+            if way == 0:
+                return
+        piece = out_ref.at[block, part_b]
+        if distance < 4:
+            moves.landed(piece, bz_send.at[way, k], bz_recv.at[way, k])
+            onward = out_ref.at[block, quarters[way]] if distance == 3 else piece
+            moves.start(onward, onward, bz_send.at[way, k + 1], bz_recv.at[way, k + 1], ring[way])
+        cross(piece, block)
+        to_twin(piece, block, part_b)
+
+    def b_crossed(k, way, distance):
+        block = slot(1, way, distance)
+        piece = out_ref.at[block, part_b]
+        moves.landed(piece, bx_send.at[k], bx_recv.at[k])
+        to_twin(piece, block, part_b)
 
     own = pltpu.make_async_copy(rows_ref, out_ref.at[s], local)
     own.start()
-    pass_on(rows_ref, out_ref.at[s], x_send, x_recv, across)
+    own_a, own_b = rows_ref.at[part_a], rows_ref.at[part_b]
+    moves.start(own_a, out_ref.at[s, part_a], ax_send, ax_recv, across)
     for way in range(2):
-        pass_on(rows_ref, out_ref.at[s], z_send.at[0, way, 0], z_recv.at[0, way, 0], ring[way])
-    to_twin(rows_ref, s)
+        moves.start(own_b, out_ref.at[s, part_b], bz_send.at[way, 0], bz_recv.at[way, 0], ring[way])
+    for way in range(2):
+        moves.start(own_a, out_ref.at[s, part_a], az_send.at[0, way, 0], az_recv.at[0, way, 0], ring[way])
+    cross(own_b, s)
+    to_twin(own_a, s, part_a)
+    to_twin(own_b, s, part_b)
     block = across[0]
-    landed(out_ref.at[block], x_send, x_recv)
+    piece = out_ref.at[block, part_a]
+    moves.landed(piece, ax_send, ax_recv)
     for way in range(2):
-        pass_on(out_ref.at[block], out_ref.at[block], z_send.at[1, way, 0], z_recv.at[1, way, 0], ring[way])
-    to_twin(out_ref.at[block], block)
+        moves.start(piece, piece, az_send.at[1, way, 0], az_recv.at[1, way, 0], ring[way])
+    to_twin(piece, block, part_a)
     for distance in range(1, 5):
+        for way in range(2):
+            b_arrives(way, distance)
         for p in range(2):
             for way in range(2):
-                if not travels(p, way, distance):
-                    continue
-                block = slot(p, way, distance)
-                k = distance - 1
-                landed(out_ref.at[block], z_send.at[p, way, k], z_recv.at[p, way, k])
-                if travels(p, way, distance + 1):
-                    pass_on(
-                        out_ref.at[block], out_ref.at[block],
-                        z_send.at[p, way, k + 1], z_recv.at[p, way, k + 1], ring[way],
-                    )
-                to_twin(out_ref.at[block], block)
+                a_arrives(p, way, distance)
+        if distance == 1:
+            b_crossed(0, 0, 0)
+        else:
+            b_crossed(2 * distance - 3, 0, distance - 1)
+            b_crossed(2 * distance - 2, 1, distance - 1)
+    b_crossed(7, 0, 4)
     own.wait()
-    for copy in sent:
-        copy.wait_send()
-    for k in twins:
-        landed(out_ref.at[twin[0]], c_send.at[k], c_recv.at[k])
+    for k, part in enumerate(twins):
+        moves.landed(out_ref.at[twin[0], part], c_send.at[k], c_recv.at[k])
+    moves.drain()
 
 
 def spread(rows):
@@ -444,10 +482,13 @@
     return pl.pallas_call(
         spread_kernel,
         out_shape=jax.ShapeDtypeStruct((32,) + rows.shape, rows.dtype),
-        in_specs=[ANY],
-        out_specs=ANY,
-        scratch_shapes=[dma(()), dma(()), dma((2, 2, 4)), dma((2, 2, 4)), dma((16,)), dma((16,)), dma(())],
-        compiler_params=params(4),
+        in_specs=[IN_VMEM],
+        out_specs=IN_VMEM,
+        scratch_shapes=[
+            dma(()), dma(()), dma((2, 2, 4)), dma((2, 2, 4)), dma((8,)), dma((8,)),
+            dma((2, 4)), dma((2, 4)), dma((32,)), dma((32,)), dma(()),
+        ],
+        compiler_params=params(4, vmem_limit_bytes=12 << 20),
         name="spread",
     )(rows)
 
@@ -455,160 +496,229 @@
 CHUNK = 256
 
 
-def expert_kernel(info_ref, rows_ref, lane_ref, column_ref, gate_ref, up_ref, down_ref, out_ref):
+def expert_kernel(rows_ref, gate_ref, up_ref, down_ref, out_ref, column, lane, gathered, contribution, starts):
     width = gate_ref.shape[0]
-    tokens = rows_ref.shape[0]
-    expert, routed = info_ref[0], info_ref[1]
-
-    def one_chunk(number, first):
+    blocks = rows_ref.shape[0] // CHUNK
+    expert = lax.axis_index("seq")
+    bf16, f32 = jnp.bfloat16, jnp.float32
+    down_index = lax.broadcasted_iota(jnp.int32, (CHUNK, CHUNK), 0)
+    along_index = lax.broadcasted_iota(jnp.int32, (CHUNK, CHUNK), 1)
+    zero_first = (((0,), (0,)), ((), ()))
+
+    def span(block):
+        return pl.ds(pl.multiple_of(block * CHUNK, CHUNK), CHUNK)
+
+    def number_rows(block, before):
+        routed = (rows_ref[span(block), width:].astype(f32) != 0.0).astype(f32)
+        here = lax.broadcasted_iota(jnp.int32, routed.shape, 1) == expert
+        routed = jnp.where(here, routed, 0.0)
+        ones = routed.astype(bf16)
+        upto = jnp.dot((along_index <= down_index).astype(f32).astype(bf16), ones, preferred_element_type=f32)
+        hit = jnp.sum(routed, axis=1, keepdims=True)
+        rank = jnp.sum(jnp.where(here, upto, 0.0), axis=1, keepdims=True)
+        column[span(block), :] = jnp.where(hit > 0.0, rank + (before - 1.0), -1.0)
+        upto = lax.dot_general(
+            ones, (down_index <= along_index).astype(f32).astype(bf16), zero_first, preferred_element_type=f32
+        )
+        same = lax.dot_general(
+            ones, (down_index == along_index).astype(f32).astype(bf16), zero_first, preferred_element_type=f32
+        )
+        hit = jnp.sum(same, axis=0, keepdims=True)
+        mine = lax.broadcasted_iota(jnp.int32, upto.shape, 0) == expert
+        rank = jnp.sum(jnp.where(mine, upto, 0.0), axis=0, keepdims=True)
+        lane[block] = jnp.where(hit > 0.0, rank + (before - 1.0), -1.0)
+        starts[block] = before.astype(jnp.int32)
+        return before + jnp.sum(routed)
+
+    routed = lax.fori_loop(0, blocks, number_rows, jnp.float32(0.0)).astype(jnp.int32)
+    starts[blocks] = routed
+
+    def one_chunk(number, _):
         base = number * CHUNK
-        picks = (
-            lane_ref[...] == base + lax.broadcasted_iota(jnp.int32, (CHUNK, 1), 0)
-        ).astype(jnp.bfloat16)
-        rows = jnp.dot(picks, rows_ref[:, :width], preferred_element_type=jnp.float32).astype(jnp.bfloat16)
-        all_gates = jnp.dot(picks, rows_ref[:, width:], preferred_element_type=jnp.float32)
+        gathered[...] = jnp.zeros_like(gathered)
+
+        def touches(block):
+            first, end = starts[block], starts[block + 1]
+            return (first < base + CHUNK) & ((end > base) | (first >= base))
+
+        def gather(block, _):
+            @pl.when(touches(block))
+            def _():
+                slots = base + lax.broadcasted_iota(jnp.int32, (CHUNK, 1), 0)
+                picks = (lane[block] == slots.astype(f32)).astype(f32).astype(bf16)
+                gathered[...] += jnp.dot(picks, rows_ref[span(block), :], preferred_element_type=f32)
+
+            return 0
+
+        lax.fori_loop(0, blocks, gather, 0)
+        all_gates = gathered[:, width:]
         here = lax.broadcasted_iota(jnp.int32, all_gates.shape, 1) == expert
         gates = jnp.sum(jnp.where(here, all_gates, 0.0), axis=1, keepdims=True)
-        gate_out = jnp.dot(rows, gate_ref[...], preferred_element_type=jnp.float32)
-        up_out = jnp.dot(rows, up_ref[...], preferred_element_type=jnp.float32)
-        active = (jnp.maximum(gate_out, 0.0) * up_out).astype(jnp.bfloat16)
-        down_out = jnp.dot(active, down_ref[...], preferred_element_type=jnp.float32) * gates
-        contribution = down_out.astype(jnp.bfloat16)
-        lanes = base + lax.broadcasted_iota(jnp.int32, (1, CHUNK), 1)
+        rows = gathered[:, :width].astype(bf16)
+        gate_out = jnp.dot(rows, gate_ref[...], preferred_element_type=f32)
+        up_out = jnp.dot(rows, up_ref[...], preferred_element_type=f32)
+        active = (jnp.maximum(gate_out, 0.0) * up_out).astype(bf16)
+        down_out = jnp.dot(active, down_ref[...], preferred_element_type=f32) * gates
+        contribution[...] = down_out.astype(bf16)
 
         def place(block, _):
-            span = pl.ds(pl.multiple_of(block * CHUNK, CHUNK), CHUNK)
-            back = (column_ref[span, :] == lanes).astype(jnp.bfloat16)
-            placed = jnp.dot(back, contribution, preferred_element_type=jnp.float32)
-            if not first:
-                placed = placed + out_ref[span, :].astype(jnp.float32)
-            out_ref[span, :] = placed.astype(jnp.bfloat16)
+            @pl.when(touches(block))
+            def _():
+                slots = base + lax.broadcasted_iota(jnp.int32, (1, CHUNK), 1)
+                back = (column[span(block), :] == slots.astype(f32)).astype(f32).astype(bf16)
+                placed = jnp.dot(back, contribution[...], preferred_element_type=f32)
+
+                @pl.when(starts[block] >= base)
+                def _():
+                    out_ref[span(block), :] = placed.astype(bf16)
+
+                @pl.when(starts[block] < base)
+                def _():
+                    out_ref[span(block), :] = (out_ref[span(block), :].astype(f32) + placed).astype(bf16)
+
             return 0
 
-        lax.fori_loop(0, tokens // CHUNK, place, 0)
-
-    one_chunk(0, True)
-
-    def more(number, _):
-        one_chunk(number, False)
+        lax.fori_loop(0, blocks, place, 0)
         return 0
 
-    lax.fori_loop(1, (routed + CHUNK - 1) // CHUNK, more, 0)
-
-
-def run_expert(info, rows, lane_slots, column_slots, w_gate, w_up, w_down):
-    tokens = rows.shape[0]
+    lax.fori_loop(0, routed // CHUNK + 1, one_chunk, 0)
+
+
+def run_expert(rows, w_gate, w_up, w_down):
+    tokens, columns = rows.shape
+    width = w_gate.shape[0]
     return pl.pallas_call(
         expert_kernel,
-        out_shape=jax.ShapeDtypeStruct((tokens, w_gate.shape[0]), jnp.bfloat16),
-        in_specs=[pl.BlockSpec(memory_space=pltpu.SMEM)] + [IN_VMEM] * 6,
+        out_shape=jax.ShapeDtypeStruct((tokens, width), jnp.bfloat16),
+        in_specs=[IN_VMEM] * 4,
         out_specs=IN_VMEM,
-        compiler_params=pltpu.CompilerParams(vmem_limit_bytes=60 << 20),
+        scratch_shapes=[
+            pltpu.VMEM((tokens, 1), jnp.float32),
+            pltpu.VMEM((tokens // CHUNK, 1, CHUNK), jnp.float32),
+            pltpu.VMEM((CHUNK, columns), jnp.float32),
+            pltpu.VMEM((CHUNK, width), jnp.bfloat16),
+            pltpu.SMEM((tokens // CHUNK + 1,), jnp.int32),
+        ],
+        compiler_params=pltpu.CompilerParams(vmem_limit_bytes=28 << 20),
         name="run_expert",
-    )(info, rows, lane_slots, column_slots, w_gate, w_up, w_down)
+    )(rows, w_gate, w_up, w_down)
 
 
 def collect_kernel(
-    in_ref, out_ref, mine, other, ring_in, final, from_x,
-    x_send, x_recv, z_send, z_recv, c_send, c_recv, local,
+    in_ref, out_ref, other, total_a, total_b, a_in, b_in, bx_in, from_x,
+    ax_send, ax_recv, az_send, az_recv, bx_send, bx_recv, bz_send, bz_recv, c_send, c_recv,
 ):
-    s, t, plane, z, core, x, y = places()
-    across = ((1 - plane) * 16 + z * 2 + core, (1 - x) * 4 + y)
-    twin = (s + 1 - 2 * core, t)
-    ring = [(plane * 16 + ((z + d) % 8) * 2 + core, t) for d in (1, 7)]
+    s, z, core, planes, across, twin, ring = ring_places()
     greet([across, twin] + ring)
-    planes = [plane, 1 - plane]
+    moves = Copies(twin)
+    part_a, part_b = pl.ds(0, HALF), pl.ds(HALF, HALF)
+    quarters = [pl.ds(0, HALF // 2), pl.ds(HALF // 2, HALF // 2)]
+    wide = lambda values: values.astype(jnp.float32)
 
     def place(p, way, distance):
         ahead = (z + distance) % 8 if way == 0 else (z + 8 - distance) % 8
-        return planes[p] * 8 + ahead
-
-    order = [(0, 0, 4), (1, 1, 4)]
+        return ahead, planes[p] * 8 + ahead
+
+    order = [(1, 0, 4), (0, 0, 4)]
     for distance in (3, 2, 1):
-        for p in range(2):
-            for way in range(2):
-                order.append((p, way, distance))
+        order += [(p, way, distance) for p in (1, 0) for way in range(2)]
     order += [(1, 0, 0), (0, 0, 0)]
-    loads, swaps = [], []
     for k, key in enumerate(order):
-        i = place(*key)
-        swap = pltpu.make_async_remote_copy(
-            src_ref=in_ref.at[2 * i + 1 - core], dst_ref=other.at[i], send_sem=c_send.at[k],
-            recv_sem=c_recv.at[k], device_id=twin, device_id_type=MESH,
-        )
-        swap.start()
-        swaps.append(swap)
-        load = pltpu.make_async_copy(in_ref.at[2 * i + core], mine.at[i], local.at[k])
-        load.start()
-        loads.append(load)
-
-    sent = []
-
-    def pass_on(src, dst, send_sem, recv_sem, peer):
-        copy = pltpu.make_async_remote_copy(
-            src_ref=src, dst_ref=dst, send_sem=send_sem, recv_sem=recv_sem,
-            device_id=peer, device_id_type=MESH,
-        )
-        copy.start()
-        sent.append(copy)
-
-    def landed(dst, send_sem, recv_sem):
-        pltpu.make_async_remote_copy(
-            src_ref=dst, dst_ref=dst, send_sem=send_sem, recv_sem=recv_sem,
-            device_id=twin, device_id_type=MESH,
-        ).wait_recv()
-
-    wide = lambda ref: ref[...].astype(jnp.float32)
+        _, i = place(*key)
+        moves.start(in_ref.at[2 * i + 1 - core], other.at[i], c_send.at[k], c_recv.at[k], twin)
+
+    crossed = {}
     for k, (p, way, distance) in enumerate(order):
-        i = place(p, way, distance)
-        loads[k].wait()
-        swaps[k].wait()
-        if distance == 0:
-            break
-        total = wide(mine.at[i]) + wide(other.at[i])
-        farther = 3 if p != way else 4
-        if distance < farther:
-            piece = ring_in.at[p, way, distance]
-            landed(piece, z_send.at[p, way, distance], z_recv.at[p, way, distance])
-            total = total + wide(piece)
-        mine[i] = total.astype(jnp.bfloat16)
-        pass_on(
-            mine.at[i], ring_in.at[p, way, distance - 1],
-            z_send.at[p, way, distance - 1], z_recv.at[p, way, distance - 1], ring[way],
-        )
-    loads[-1].wait()
-    swaps[-1].wait()
-    for p in (1, 0):
-        i = planes[p] * 8 + z
-        total = wide(mine.at[i]) + wide(other.at[i])
-        for way in range(2):
-            piece = ring_in.at[p, way, 0]
-            landed(piece, z_send.at[p, way, 0], z_recv.at[p, way, 0])
-            total = total + wide(piece)
+        ahead, i = place(p, way, distance)
+        moves.landed(other.at[i], c_send.at[k], c_recv.at[k])
+
+        mine = wide(in_ref[2 * i + core, part_b]) + wide(other[i, part_b])
         if p == 1:
-            final[...] = total.astype(jnp.bfloat16)
-            pass_on(final, from_x, x_send, x_recv, across)
+            total_b[i] = mine.astype(jnp.bfloat16)
+            j = len(crossed)
+            crossed[way, distance] = j
+            moves.start(total_b.at[i], bx_in.at[ahead], bx_send.at[j], bx_recv.at[j], across)
+
+        ours = wide(in_ref[2 * i + core, part_a]) + wide(other[i, part_a])
+        if distance > 0:
+            ways = [p] if distance == 4 else [way]
+            for w in ways:
+                if distance < (4 if p == w else 3):
+                    piece = a_in.at[p, w, distance]
+                    moves.landed(piece, az_send.at[p, w, distance], az_recv.at[p, w, distance])
+                    ours = ours + wide(piece[...])
+                total_a[i] = ours.astype(jnp.bfloat16)
+                moves.start(
+                    total_a.at[i], a_in.at[p, w, distance - 1],
+                    az_send.at[p, w, distance - 1], az_recv.at[p, w, distance - 1], ring[w],
+                )
         else:
-            landed(from_x, x_send, x_recv)
-            out_ref[...] = (total + wide(from_x)).astype(out_ref.dtype)
-    for copy in sent:
-        copy.wait_send()
+            for w in range(2):
+                piece = a_in.at[p, w, 0]
+                moves.landed(piece, az_send.at[p, w, 0], az_recv.at[p, w, 0])
+                ours = ours + wide(piece[...])
+            if p == 1:
+                total_a[i] = ours.astype(jnp.bfloat16)
+                moves.start(total_a.at[i], from_x, ax_send, ax_recv, across)
+
+        if p == 0:
+            j = crossed[way, distance]
+            moves.landed(bx_in.at[ahead], bx_send.at[j], bx_recv.at[j])
+            mine = mine + wide(bx_in[ahead])
+            if distance == 4:
+                total_b[i] = mine.astype(jnp.bfloat16)
+                for w in range(2):
+                    moves.start(
+                        total_b.at[i, quarters[w]], b_in.at[w, 3, quarters[w]],
+                        bz_send.at[w, 3], bz_recv.at[w, 3], ring[w],
+                    )
+            elif distance == 3:
+                piece = b_in.at[way, 3, quarters[way]]
+                moves.landed(piece, bz_send.at[way, 3], bz_recv.at[way, 3])
+                split = HALF // 2
+                first, second = mine[:split], mine[split:]
+                if way == 0:
+                    first = first + wide(piece[...])
+                else:
+                    second = second + wide(piece[...])
+                total_b[i, quarters[0]] = first.astype(jnp.bfloat16)
+                total_b[i, quarters[1]] = second.astype(jnp.bfloat16)
+            elif distance > 0:
+                piece = b_in.at[way, distance]
+                moves.landed(piece, bz_send.at[way, distance], bz_recv.at[way, distance])
+                total_b[i] = (mine + wide(piece[...])).astype(jnp.bfloat16)
+            if 0 < distance < 4:
+                moves.start(
+                    total_b.at[i], b_in.at[way, distance - 1],
+                    bz_send.at[way, distance - 1], bz_recv.at[way, distance - 1], ring[way],
+                )
+            if distance == 0:
+                for w in range(2):
+                    piece = b_in.at[w, 0]
+                    moves.landed(piece, bz_send.at[w, 0], bz_recv.at[w, 0])
+                    mine = mine + wide(piece[...])
+                out_ref[part_b, :] = mine.astype(out_ref.dtype)
+                moves.landed(from_x, ax_send, ax_recv)
+                out_ref[part_a, :] = (ours + wide(from_x[...])).astype(out_ref.dtype)
+    moves.drain()
 
 
 def collect(parts):
     dma = pltpu.SemaphoreType.DMA
-    rows = parts.shape[1:]
-    vmem = lambda *lead: pltpu.VMEM(lead + rows, parts.dtype)
+    _, rows, width = parts.shape
+    vmem = lambda *lead: pltpu.VMEM(lead + (width,), parts.dtype)
     return pl.pallas_call(
         collect_kernel,
-        out_shape=jax.ShapeDtypeStruct(rows, jnp.bfloat16),
-        in_specs=[ANY],
+        out_shape=jax.ShapeDtypeStruct((rows, width), jnp.bfloat16),
+        in_specs=[IN_VMEM],
         out_specs=IN_VMEM,
         scratch_shapes=[
-            vmem(16), vmem(16), vmem(2, 2, 4), vmem(), vmem(),
-            dma(()), dma(()), dma((2, 2, 4)), dma((2, 2, 4)), dma((16,)), dma((16,)), dma((16,)),
+            vmem(16, rows), vmem(16, HALF), vmem(16, HALF), vmem(2, 2, 4, HALF), vmem(2, 4, HALF),
+            vmem(8, HALF), vmem(HALF),
+            dma(()), dma(()), dma((2, 2, 4)), dma((2, 2, 4)), dma((8,)), dma((8,)),
+            dma((2, 4)), dma((2, 4)), dma((16,)), dma((16,)),
         ],
-        compiler_params=params(5, vmem_limit_bytes=40 << 20),
+        compiler_params=params(5, vmem_limit_bytes=28 << 20),
         name="collect",
     )(parts)
 
@@ -661,19 +771,7 @@
         kv_own, query, starts[:, None], tokens, w_out, moe_gain[None], w_router, routes
     )
     arrived = spread(payload).reshape(32 * tok_dev, width + HD)
-    my_gates = lax.dynamic_slice_in_dim(arrived[:, width:], seq_rank, 1, 1)[:, 0]
-    routed = (my_gates != 0).reshape(16, HD)
-    ones = routed.astype(bf16)
-    upto = jnp.arange(HD)[:, None] <= jnp.arange(HD)[None, :]
-    inside = jnp.dot(ones, upto.astype(bf16), preferred_element_type=f32)
-    sums = inside[:, -1]
-    before = jnp.sum(jnp.where(jnp.arange(16)[None, :] < jnp.arange(16)[:, None], sums[None, :], 0.0), axis=1)
-    slots = jnp.where(routed, (inside + before[:, None]).astype(jnp.int32) - 1, -1)
-    total = jnp.sum(sums).astype(jnp.int32)
-    info = jnp.stack([seq_rank.astype(jnp.int32), total])
-    parts = run_expert(
-        info, arrived, slots.reshape(1, -1), slots.reshape(-1, 1), w_gate[0], w_up[0], w_down[0]
-    )
+    parts = run_expert(arrived, w_gate[0], w_up[0], w_down[0])
     moe = collect(parts.reshape(32, tok_dev, width))
     layer_out = (resid + moe.astype(f32)).astype(bf16)
     return (layer_out, kv_cache)

time: 209 us -> 172 us (0.82)
  Pallas kernels: 181 us -> 154 us
  local copies, waits for them, and re-layouts: 14.9 us -> 9 us
    pallas_call x2, Pallas kernels: 68.3 us -> 48.9 us  [the longest x1 36.9 us: collect(): pl.pallas_call(collect_kernel, out_shape=jax.ShapeDtypeStruct((rows, widt...]
    pallas_call x1, Pallas kernels: 39.6 us -> 32.2 us  [spread(): pl.pallas_call(spread_kernel, out_shape=jax.ShapeDtypeStruct((32,) + rows...]
    unnamed x24 -> x30, local copies, waits for them, and re-layouts: 6.53 us -> 4.47 us
where the time goes in v3:
time: 172 us
  Pallas kernels  154 us (90%)
  local copies, waits for them, and re-layouts  9 us (5%)
  other arithmetic  5.65 us (3%)
  matrix products  1.74 us (1%)
    pallas_call x1, Pallas kernels, attention_layer(): pl.pallas_call(attention_kernel, out_shape=(jax.ShapeDtypeStruct((rows, w...  45.3 us
    pallas_call x1, Pallas kernels, collect(): pl.pallas_call(collect_kernel, out_shape=jax.ShapeDtypeStruct((rows, widt...  36.9 us
    pallas_call x1, Pallas kernels, spread(): pl.pallas_call(spread_kernel, out_shape=jax.ShapeDtypeStruct((32,) + rows...  32.2 us
    pallas_call x1, Pallas kernels, tp_gather(): pl.pallas_call(tp_gather_kernel, out_shape=(jax.ShapeDtypeStruct((8, coun...  28 us
    pallas_call x1, Pallas kernels, run_expert(): pl.pallas_call(expert_kernel, out_shape=jax.ShapeDtypeStruct((tokens, wid...  12 us
    unnamed x30, local copies, waits for them, and re-layouts  4.47 us

profile of v3, /device:TPU:8, one launch (start us, length us, event | category | flops | bytes accessed | tf_op | source)
XLA Modules:
  0.0 171.7 jit_solution(7383946029736833487)
XLA Ops:
  0.6 0.0 copy-start
  0.6 0.0 copy-start.4
  0.7 0.8 pad_bitcast_fusion.seg_ref
  1.5 0.7 broadcast_in_dim.30.gain_ref
  2.2 0.1 broadcast_compare_fusion
  2.3 0.1 broadcast_subtract_fusion
  2.3 0.8 copy.42.routes_ref
  3.1 1.1 copy.41.router_ref
  4.2 2.3 %copy.46 = bf16[256,1536]{1,0:T(8,128)(2,1)} copy(bf16[256,1536]{0,1:T(8,128)(2,1)} %bitcast.47) | data formatting | bytes 1572864 | tf_op jit(solution)/shard_map/dot_general | solution.py:754
  6.5 0.0 copy-done.4
  6.5 28.0 %tp_gather.1 = (bf16[8,64,1536]{2,1,0:T(8,128)(2,1)S(1)}, s32[9,8,1,128]{3,2,1,0:T(1,128)S(1)}) custom-call(bf16[64,1536]{1,0:T(8,128)(2,1)S(1)} %copy-done.4, s32[1,128]{1,0:T(1,128)S(1)} %pad_bitcast_fusion.seg_ref), custom_call_target="tpu_custom_call" | custom-call | tf_op jit(solution)/shard_map/tp_gather/pallas_call | solution.py:139
  34.5 0.1 eq.30
  34.6 0.1 slice_reduce_fusion
  34.7 0.1 eq.34
  34.8 0.2 select_reduce_fusion
  35.0 0.1 select_reduce_fusion.1
  35.1 0.4 multiply_reduce_fusion
  35.4 0.1 rsqrt.13
  35.5 0.1 copy.40.start_ref
  35.7 0.5 multiply_cosine_fusion.1
  36.2 0.0 copy-done.12
  36.2 0.4 multiply_convert_fusion
  36.7 0.0 copy-start.9
  36.7 1.6 fusion.1
  38.3 0.0 copy-done.9
  38.3 0.6 fusion.11
  38.9 0.1 subtract_convert_fusion
  39.0 0.1 constant_dynamic-slice_fusion.1
  39.1 0.8 copy.47
  39.9 0.1 copy.49
  40.0 0.0 copy-start.11
  40.0 0.0 copy-done
  40.0 0.0 copy-done.8
  40.0 0.6 convolution_convert_fusion
  40.6 0.4 copy-done.11
  41.0 0.6 convolution_bitcast_fusion
  41.6 1.2 fusion.7
  42.8 0.1 maximum_bitcast_fusion.q_ref
  43.0 0.0 copy-done.10
  43.0 0.0 copy-done.7
  43.0 45.3 %attention_layer.1 = (f32[64,1536]{1,0:T(8,128)S(1)}, bf16[64,1664]{1,0:T(8,128)(2,1)S(1)}) custom-call(bf16[4,2,128,128]{3,2,1,0:T(8,128)(2,1)S(1)} %pad_maximum_fusion.1.kv_ref, bf16[512,128]{1,0:T(8,128)(2,1)S(1)} %maximum_bitcast_fusion.q_ref, s32[512,1]{1,0:T(8,128)S(1)} %copy.40.start_ref, bf16[64,1536]{1,0:T(8,128)(2,1)S(1)} %copy-done.4, ...), custom_call_target="tpu_custom_call" | custom-call | tf_op jit(solution)/shard_map/attention_layer/pallas_call | solution.py:348
  88.3 0.7 copy-done.5
  89.1 0.1 pad_maximum_fusion.2
  89.2 0.6 copy.44
  89.8 32.2 %spread.1 = bf16[32,64,1664]{2,1,0:T(8,128)(2,1)S(1)} custom-call(bf16[64,1664]{1,0:T(8,128)(2,1)S(1)} %get-tuple-element.9.rows_ref), custom_call_target="tpu_custom_call" | custom-call | tf_op jit(solution)/shard_map/spread/pallas_call | solution.py:482
  122.0 12.0 %run_expert.1 = bf16[2048,1536]{1,0:T(8,128)(2,1)S(1)} custom-call(bf16[2048,1664]{1,0:T(8,128)(2,1)S(1)} %bitcast.39, bf16[1536,768]{1,0:T(8,128)(2,1)S(1)} %bitcast.41, bf16[1536,768]{1,0:T(8,128)(2,1)S(1)} %bitcast.42, bf16[768,1536]{1,0:T(8,128)(2,1)S(1)} %bitcast.43), custom_call_target="tpu_custom_call" | custom-call | tf_op jit(solution)/shard_map/run_expert/pallas_call | solution.py:590
  134.1 36.9 %collect.1 = bf16[64,1536]{1,0:T(8,128)(2,1)S(1)} custom-call(bf16[32,64,1536]{2,1,0:T(8,128)(2,1)S(1)} %bitcast.40), custom_call_target="tpu_custom_call" | custom-call | tf_op jit(solution)/shard_map/collect/pallas_call | solution.py:710
  171.0 0.7 add_convert_fusion
  (25 shorter events, 0.2 us)
Async XLA Ops:
  0.6 39.4 %copy-start = (bf16[1536,256]{1,0:T(8,128)(2,1)S(1)}, bf16[1536,256]{1,0:T(8,128)(2,1)}, u32[]{:S(2)}) copy-start(bf16[1536,256]{1,0:T(8,128)(2,1)} %param.19) | copy-start | bytes 2359300
  0.6 5.9 %copy-start.4 = (bf16[64,1536]{1,0:T(8,128)(2,1)S(1)}, bf16[64,1536]{1,0:T(8,128)(2,1)}, u32[]{:S(2)}) copy-start(bf16[64,1536]{1,0:T(8,128)(2,1)} %tokens_ref.1) | copy-start | bytes 589828
  2.2 34.0 %copy-start.12 = (f32[1536]{0:T(1024)S(1)}, f32[1536]{0:T(1024)}, u32[]{:S(2)}) copy-start(f32[1536]{0:T(1024)} %param.16) | copy-start | bytes 18436
  36.7 1.6 copy-start.9
  38.3 1.7 %copy-start.8 = (bf16[512,1536]{1,0:T(8,128)(2,1)S(1)}, bf16[512,1536]{1,0:T(8,128)(2,1)}, u32[]{:S(2)}) copy-start(bf16[512,1536]{1,0:T(8,128)(2,1)} %fusion.1) | copy-start | bytes 4718596
  40.0 1.0 copy-start.11
  41.0 2.0 %copy-start.10 = (bf16[512,128]{1,0:T(8,128)(2,1)S(1)}, bf16[512,128]{1,0:T(8,128)(2,1)}, u32[]{:S(2)}) copy-start(bf16[512,128]{1,0:T(8,128)(2,1)} %copy.47) | copy-start | bytes 393220
  41.0 2.0 %copy-start.7 = (bf16[128,1536]{1,0:T(8,128)(2,1)S(1)}, bf16[128,1536]{1,0:T(8,128)(2,1)}, u32[]{:S(2)}) copy-start(bf16[128,1536]{1,0:T(8,128)(2,1)} %w_out_ref.1) | copy-start | bytes 1179652
  88.3 0.8 copy-start.5
  89.1 32.9 %copy-start.3 = (bf16[1,768,1536]{2,1,0:T(8,128)(2,1)S(1)}, bf16[1,768,1536]{2,1,0:T(8,128)(2,1)}, u32[]{:S(2)}) copy-start(bf16[1,768,1536]{2,1,0:T(8,128)(2,1)} %param.25) | copy-start | bytes 7077892
  89.8 32.2 %copy-start.1 = (bf16[1,1536,768]{2,1,0:T(8,128)(2,1)S(1)}, bf16[1,1536,768]{2,1,0:T(8,128)(2,1)}, u32[]{:S(2)}) copy-start(bf16[1,1536,768]{2,1,0:T(8,128)(2,1)} %param.23) | copy-start | bytes 7077892
  89.8 32.2 %copy-start.2 = (bf16[1,1536,768]{2,1,0:T(8,128)(2,1)S(1)}, bf16[1,1536,768]{2,1,0:T(8,128)(2,1)}, u32[]{:S(2)}) copy-start(bf16[1,1536,768]{2,1,0:T(8,128)(2,1)} %param.24) | copy-start | bytes 7077892
  134.1 36.9 %copy-start.6 = (f32[64,1536]{1,0:T(8,128)S(1)}, f32[64,1536]{1,0:T(8,128)}, u32[]{:S(2)}) copy-start(f32[64,1536]{1,0:T(8,128)} %copy-done.5) | copy-start | bytes 1179652

commit v4 on v3

--- a/solution.py
+++ b/solution.py
@@ -77,10 +77,11 @@
 
 
 def tp_gather_kernel(
-    rows_ref, seg_ref, out, segs_ref,
-    send, recv, seg_send, seg_recv, far_send, far_recv, local,
+    rows_ref, seg_ref, w_ref, out, segs_ref, w_full,
+    send, recv, seg_send, seg_recv, far_send, far_recv,
+    wp_send, wp_recv, wz_send, wz_recv, wt_send, wt_recv, local,
 ):
-    s, t, _, _, core, x, y = places()
+    s, t, plane, z, core, x, y = places()
     across = (1 - x) * 4
     own = x * 4
     up, down, two = (y + 1) % 4, (y + 3) % 4, (y + 2) % 4
@@ -88,8 +89,34 @@
     tp_peers = [(s, (t + k) % 8) for k in range(1, 8)]
     ahead = [((s + k) % 32, t) for k in range(1, 9)]
     behind = [((s + 32 - k) % 32, t) for k in range(1, 9)]
-    greet(tp_peers + ahead + behind)
+    twin = (s + 1 - 2 * core, t)
+    ring = [(plane * 16 + ((z + d) % 8) * 2 + core, t) for d in (1, 7)]
+    greet(tp_peers + ahead + behind + ring + [twin])
     moves = Copies(xp)
+    sub = 2 * z + core
+    lanes = [pl.ds(0, 4), pl.ds(4, 4)]
+    twins = []
+
+    def w_twin(back):
+        k = len(twins)
+        twins.append(k)
+        piece = w_full.at[:, 2 * back + core]
+        moves.start(piece, piece, wt_send.at[k], wt_recv.at[k], twin)
+
+    def w_step(distance):
+        for way in range(2):
+            back = (z + 8 - distance) % 8 if way == 0 else (z + distance) % 8
+            k = distance - 1
+            span = lanes[way] if distance == 4 else slice(None)
+            piece = w_full.at[span, 2 * back + core]
+            moves.landed(piece, wz_send.at[way, k], wz_recv.at[way, k])
+            if distance < 4:
+                span = lanes[way] if distance == 3 else slice(None)
+                piece = w_full.at[span, 2 * back + core]
+                moves.start(piece, piece, wz_send.at[way, k + 1], wz_recv.at[way, k + 1], ring[way])
+                w_twin(back)
+        if distance == 4:
+            w_twin((z + 4) % 8)
 
     def go(number, src, dst, peer):
         moves.start(src, dst, send.at[number], recv.at[number], peer)
@@ -106,6 +133,10 @@
     go(2, rows_ref, out.at[t], yp)
     rows_own = pltpu.make_async_copy(rows_ref, out.at[t], local.at[1])
     rows_own.start()
+    w_own = pltpu.make_async_copy(w_ref.at[sub], w_full.at[t, sub], local.at[2])
+    w_own.start()
+    for k, peer in enumerate(tp_peers):
+        moves.start(w_ref.at[sub], w_full.at[t, sub], wp_send.at[k], wp_recv.at[k], peer)
     seg_own.wait()
     for k in range(7):
         moves.landed(segs_ref.at[0, t], seg_send.at[k], seg_recv.at[k])
@@ -115,25 +146,38 @@
     landed(0, out.at[across + y])
     go(3, out.at[across + y], out.at[across + y], yn)
     go(4, out.at[across + y], out.at[across + y], yp)
+    w_own.wait()
+    for k in range(7):
+        moves.landed(w_full.at[t, sub], wp_send.at[k], wp_recv.at[k])
+    for way in range(2):
+        piece = w_full.at[:, sub]
+        moves.start(piece, piece, wz_send.at[way, 0], wz_recv.at[way, 0], ring[way])
+    w_twin(z)
     landed(1, out.at[own + down])
     go(5, out.at[own + down, low], out.at[own + down, low], yn)
     landed(2, out.at[own + up])
     go(6, out.at[own + up, high], out.at[own + up, high], yp)
+    w_step(1)
     landed(3, out.at[across + down])
     go(7, out.at[across + down, low], out.at[across + down, low], yn)
     landed(4, out.at[across + up])
     go(8, out.at[across + up, high], out.at[across + up, high], yp)
+    w_step(2)
     landed(5, out.at[own + two, low])
     landed(6, out.at[own + two, high])
     landed(7, out.at[across + two, low])
     landed(8, out.at[across + two, high])
     rows_own.wait()
+    w_step(3)
+    w_step(4)
+    for k in twins:
+        moves.landed(w_full.at[:, sub], wt_send.at[k], wt_recv.at[k])
     for k in range(8):
         moves.landed(segs_ref.at[k + 1], far_send.at[k], far_recv.at[k])
     moves.drain()
 
 
-def tp_gather(rows, seg):
+def tp_gather(rows, seg, weight):
     count, width = rows.shape
     dma = pltpu.SemaphoreType.DMA
     return pl.pallas_call(
@@ -141,13 +185,17 @@
         out_shape=(
             jax.ShapeDtypeStruct((8, count, width), rows.dtype),
             jax.ShapeDtypeStruct((9, 8, 1, 128), jnp.int32),
+            jax.ShapeDtypeStruct((8,) + weight.shape, weight.dtype),
         ),
-        in_specs=[IN_VMEM] * 2,
-        out_specs=(IN_VMEM,) * 2,
-        scratch_shapes=[dma((9,)), dma((9,)), dma((7,)), dma((7,)), dma((8,)), dma((8,)), dma((2,))],
+        in_specs=[IN_VMEM] * 3,
+        out_specs=(IN_VMEM,) * 3,
+        scratch_shapes=[
+            dma((9,)), dma((9,)), dma((7,)), dma((7,)), dma((8,)), dma((8,)),
+            dma((7,)), dma((7,)), dma((2, 4)), dma((2, 4)), dma((8,)), dma((8,)), dma((3,)),
+        ],
         compiler_params=params(1, vmem_limit_bytes=16 << 20),
         name="tp_gather",
-    )(rows, seg)
+    )(rows, seg, weight)
 
 
 TILE = 128
@@ -156,47 +204,26 @@
 def attention_kernel(
     kv_ref, q_ref, start_ref, tokens_ref, w_out_ref, gain_ref, router_ref, routes_ref,
     resid_ref, payload_ref,
-    slots, w_full, peak, total, mixed, heads_out, heads_in,
+    slots, peak, total, mixed, heads_out, heads_in,
     z_send, z_recv, y_send, y_recv, c_send, c_recv,
-    w_send, w_recv, t_send, t_recv, h_send, h_recv, local,
+    h_send, h_recv, local,
 ):
     s, t, _, _, core, x, y = places()
-    across, own = (1 - x) * 4, x * 4
+    own = x * 4
     up, down, two = (y + 1) % 4, (y + 3) % 4, (y + 2) % 4
     far = ((s + 4) % 32, t)
     near = ((s + 2) % 32, t)
-    xp, yn, yp = (s, across + y), (s, own + up), (s, own + down)
+    yn, yp = (s, own + up), (s, own + down)
     twin = (s + 1 - 2 * core, t)
     tp_peers = [(s, (t + k) % 8) for k in range(1, 8)]
     greet(tp_peers + [twin, near, far, ((s + 30) % 32, t), ((s + 28) % 32, t)])
     moves = Copies(twin)
     count = q_ref.shape[0]
 
-    def w_piece(rank, half, first=0, rows=64):
-        return w_full.at[rank, pl.ds(pl.multiple_of(half * 64 + first, 32), rows)]
-
-    def w_go(number, rank, peer, first=0, rows=64):
-        piece = w_piece(rank, core, first, rows)
-        moves.start(piece, piece, w_send.at[number], w_recv.at[number], peer)
-
-    def w_landed(number, rank, first=0, rows=64):
-        moves.landed(w_piece(rank, core, first, rows), w_send.at[number], w_recv.at[number])
-
-    def w_twin(number, rank):
-        piece = w_piece(rank, core)
-        moves.start(piece, piece, t_send.at[number], t_recv.at[number], twin)
-
     kv_own = pltpu.make_async_copy(kv_ref, slots.at[0], local.at[0])
     kv_own.start()
-    w_own = pltpu.make_async_copy(w_out_ref, w_full.at[t], local.at[1])
-    w_own.start()
     moves.start(kv_ref.at[y], slots.at[2, y], z_send.at[0], z_recv.at[0], near)
     moves.start(kv_ref.at[y], slots.at[4, y], z_send.at[1], z_recv.at[1], far)
-    w_own.wait()
-    w_go(0, t, xp)
-    w_go(1, t, yn)
-    w_go(2, t, yp)
-
     peak[...] = jnp.full_like(peak, NEGATIVE)
     total[...] = jnp.zeros_like(total)
     mixed[...] = jnp.zeros_like(mixed)
@@ -261,45 +288,23 @@
     attend(0)
     z_step(1, True)
     z_step(2, True)
-    w_landed(0, across + y)
-    w_go(3, across + y, yn)
-    w_go(4, across + y, yp)
-    w_twin(0, across + y)
     y_step(1)
     y_step(2)
-    w_landed(1, own + down)
-    w_go(5, own + down, yn, 0, 32)
-    w_twin(1, own + down)
-    w_landed(2, own + up)
-    w_go(6, own + up, yp, 32, 32)
-    w_twin(2, own + up)
     block_step(1)
+    block_step(2)
     attend(2)
     z_step(3, False)
     z_step(4, False)
-    block_step(2)
     twin_step(1)
     y_step(3)
     y_step(4)
     attend(4)
-    w_landed(3, across + down)
-    w_go(7, across + down, yn, 0, 32)
-    w_twin(3, across + down)
-    w_landed(4, across + up)
-    w_go(8, across + up, yp, 32, 32)
-    w_twin(4, across + up)
     block_step(3)
+    block_step(4)
     twin_step(2)
-    block_step(4)
     attend(6)
     twin_step(3)
-    w_landed(5, own + two, 0, 32)
-    w_landed(6, own + two, 32, 32)
-    w_twin(5, own + two)
     attend(8)
-    w_landed(7, across + two, 0, 32)
-    w_landed(8, across + two, 32, 32)
-    w_twin(6, across + two)
     twin_step(4)
 
     for rank in range(8):
@@ -309,16 +314,13 @@
     heads_own.start()
     for k, peer in enumerate(tp_peers):
         moves.start(heads_out.at[peer[1]], heads_in.at[t], h_send.at[k], h_recv.at[k], peer)
-    ranks = [across + y, own + down, own + up, across + down, across + up, own + two, across + two]
-    for number, rank in enumerate(ranks):
-        moves.landed(w_piece(rank, 1 - core), t_send.at[number], t_recv.at[number])
     heads_own.wait()
     for k in range(7):
         moves.landed(heads_in.at[t], h_send.at[k], h_recv.at[k])
     attention = jnp.concatenate([heads_in[rank] for rank in range(8)], axis=1)
     width = tokens_ref.shape[1]
     resid = tokens_ref[...].astype(jnp.float32) + jnp.dot(
-        attention, w_full[...].reshape(8 * HD, width), preferred_element_type=jnp.float32
+        attention, w_out_ref[...], preferred_element_type=jnp.float32
     )
     resid_ref[...] = resid
     moe_rows = rms_rows(resid, gain_ref[...]).astype(jnp.bfloat16)
@@ -355,16 +357,15 @@
         out_specs=(IN_VMEM,) * 2,
         scratch_shapes=[
             pltpu.VMEM((9,) + kv.shape, bf16),
-            pltpu.VMEM((8, HD, width), bf16),
             pltpu.VMEM((count, 1), f32),
             pltpu.VMEM((count, 1), f32),
             pltpu.VMEM((count, HD), f32),
             pltpu.VMEM((8, rows, HD), bf16),
             pltpu.VMEM((8, rows, HD), bf16),
             dma((4,)), dma((4,)), dma((4, 4)), dma((4, 4)), dma((4,)), dma((4,)),
-            dma((9,)), dma((9,)), dma((7,)), dma((7,)), dma((7,)), dma((7,)), dma((2,)),
+            dma((7,)), dma((7,)), dma((1,)),
         ],
-        compiler_params=params(2, vmem_limit_bytes=32 << 20),
+        compiler_params=params(2, vmem_limit_bytes=20 << 20),
         name="attention_layer",
     )(kv, query, starts, tokens, w_out, gain, router, routes)
 
@@ -735,7 +736,7 @@
     block_first = seq_rank * tok_seq
 
     seg_row = jnp.pad(segment_ids, (0, HD - tok_dev), constant_values=-1).reshape(1, HD)
-    wide, segs = tp_gather(tokens, seg_row)
+    wide, segs, w_out_all = tp_gather(tokens, seg_row, w_out.reshape(16, 8, width))
 
     block_index = block_first + jnp.arange(tok_seq, dtype=jnp.int32)
     near = segs[:, :, 0, :tok_dev].reshape(9, tok_seq)
@@ -768,7 +769,7 @@
         axis=1,
     )
     resid, payload = attention_layer(
-        kv_own, query, starts[:, None], tokens, w_out, moe_gain[None], w_router, routes
+        kv_own, query, starts[:, None], tokens, w_out_all.reshape(QH * HD, width), moe_gain[None], w_router, routes
     )
     arrived = spread(payload).reshape(32 * tok_dev, width + HD)
     parts = run_expert(arrived, w_gate[0], w_up[0], w_down[0])

time: 172 us -> 190 us (1.10)
  Pallas kernels: 154 us -> 169 us
  local copies, waits for them, and re-layouts: 9 us -> 11.6 us
    pallas_call x1, Pallas kernels: 28 us -> 42.4 us  [tp_gather(): pl.pallas_call(tp_gather_kernel, out_shape=(jax.ShapeDtypeStruct((8, coun...]
    pallas_call x1, Pallas kernels: 12 us -> 15.3 us  [run_expert(): pl.pallas_call(expert_kernel, out_shape=jax.ShapeDtypeStruct((tokens, wid...]
    unnamed x30 -> x34, local copies, waits for them, and re-layouts: 4.47 us -> 7.11 us
    pallas_call x1, Pallas kernels: 36.9 us -> 34.4 us  [collect(): pl.pallas_call(collect_kernel, out_shape=jax.ShapeDtypeStruct((rows, widt...]
where the time goes in v4:
time: 190 us; the launch traced here: 189 us
  Pallas kernels  169 us (89%)
  local copies, waits for them, and re-layouts  11.6 us (6%)
  other arithmetic  5.64 us (3%)
    pallas_call x1, Pallas kernels, attention_layer(): pl.pallas_call(attention_kernel, out_shape=(jax.ShapeDtypeStruct((rows, w...  46.4 us
    pallas_call x1, Pallas kernels, tp_gather(): pl.pallas_call(tp_gather_kernel, out_shape=(jax.ShapeDtypeStruct((8, coun...  42.4 us
    pallas_call x1, Pallas kernels, collect(): pl.pallas_call(collect_kernel, out_shape=jax.ShapeDtypeStruct((rows, widt...  34.4 us
    pallas_call x1, Pallas kernels, spread(): pl.pallas_call(spread_kernel, out_shape=jax.ShapeDtypeStruct((32,) + rows...  31 us
    pallas_call x1, Pallas kernels, run_expert(): pl.pallas_call(expert_kernel, out_shape=jax.ShapeDtypeStruct((tokens, wid...  15.3 us
    unnamed x34, local copies, waits for them, and re-layouts  7.11 us

profile of v4, /device:TPU:8, one launch (start us, length us, event | category | flops | bytes accessed | tf_op | source)
XLA Modules:
  0.0 189.4 jit_solution(5060638043073166651)
XLA Ops:
  0.6 0.0 copy-start
  0.6 0.0 copy-start.6
  0.7 0.8 pad_bitcast_fusion.seg_ref
  1.5 0.7 broadcast_in_dim.30.gain_ref
  2.2 0.1 broadcast_compare_fusion
  2.2 0.1 broadcast_subtract_fusion
  2.3 0.8 copy.42.routes_ref
  3.1 1.1 copy.41.router_ref
  4.2 0.0 copy-start.14
  4.2 2.3 %copy.46 = bf16[256,1536]{1,0:T(8,128)(2,1)} copy(bf16[256,1536]{0,1:T(8,128)(2,1)} %bitcast.51) | data formatting | bytes 1572864 | tf_op jit(solution)/shard_map/dot_general | solution.py:755
  6.5 0.0 copy-done.6
  6.5 1.0 copy-done.9
  7.5 42.4 %tp_gather.1 = (bf16[8,64,1536]{2,1,0:T(8,128)(2,1)S(1)}, s32[9,8,1,128]{3,2,1,0:T(1,128)S(1)}, bf16[8,16,8,1536]{3,2,1,0:T(8,128)(2,1)S(1)}) custom-call(bf16[64,1536]{1,0:T(8,128)(2,1)S(1)} %copy-done.6, s32[1,128]{1,0:T(1,128)S(1)} %pad_bitcast_fusion.seg_ref, bf16[16,8,1536]{2,1,0:T(8,128)(2,1)S(1)} %bitcast.47), custom_call_target="tpu_custom_call" | custom-call | tf_op jit(solution)/shard_map/tp_gather/pallas_call | solution.py:183
  49.9 0.0 copy-start.1
  50.0 1.6 copy-done.1
  51.6 0.1 eq.30
  51.7 0.1 slice_reduce_fusion
  51.8 0.1 eq.34
  51.9 0.2 select_reduce_fusion
  52.0 0.1 select_reduce_fusion.1
  52.1 0.4 multiply_reduce_fusion
  52.5 0.1 rsqrt.13
  52.6 0.1 copy.40.start_ref
  52.7 0.5 multiply_cosine_fusion.1
  53.3 0.0 copy-done.14
  53.3 0.4 multiply_convert_fusion
  53.7 1.6 fusion.1
  55.3 0.6 fusion.11
  55.9 0.1 subtract_convert_fusion
  56.1 0.1 constant_dynamic-slice_fusion.1
  56.2 0.8 copy.47
  56.9 0.1 copy.49
  57.1 0.0 copy-start.13
  57.1 0.6 convolution_convert_fusion
  57.7 0.4 copy-done.13
  58.1 0.6 convolution_bitcast_fusion
  58.6 1.2 fusion.7
  59.9 0.1 maximum_bitcast_fusion.q_ref
  60.0 0.0 copy-done.12
  60.1 46.4 %attention_layer.1 = (f32[64,1536]{1,0:T(8,128)S(1)}, bf16[64,1664]{1,0:T(8,128)(2,1)S(1)}) custom-call(bf16[4,2,128,128]{3,2,1,0:T(8,128)(2,1)S(1)} %pad_maximum_fusion.1.kv_ref, bf16[512,128]{1,0:T(8,128)(2,1)S(1)} %maximum_bitcast_fusion.q_ref, s32[512,1]{1,0:T(8,128)S(1)} %copy.40.start_ref, bf16[64,1536]{1,0:T(8,128)(2,1)S(1)} %copy-done.6, ...), custom_call_target="tpu_custom_call" | custom-call | tf_op jit(solution)/shard_map/attention_layer/pallas_call | solution.py:350
  106.5 0.7 copy-done.7
  107.2 0.1 pad_maximum_fusion.2
  107.3 0.6 copy.44
  108.0 31.0 %spread.1 = bf16[32,64,1664]{2,1,0:T(8,128)(2,1)S(1)} custom-call(bf16[64,1664]{1,0:T(8,128)(2,1)S(1)} %get-tuple-element.11.rows_ref), custom_call_target="tpu_custom_call" | custom-call | tf_op jit(solution)/shard_map/spread/pallas_call | solution.py:483
  139.0 15.3 %run_expert.1 = bf16[2048,1536]{1,0:T(8,128)(2,1)S(1)} custom-call(bf16[2048,1664]{1,0:T(8,128)(2,1)S(1)} %bitcast.41, bf16[1536,768]{1,0:T(8,128)(2,1)S(1)} %bitcast.44, bf16[1536,768]{1,0:T(8,128)(2,1)S(1)} %bitcast.45, bf16[768,1536]{1,0:T(8,128)(2,1)S(1)} %bitcast.46), custom_call_target="tpu_custom_call" | custom-call | tf_op jit(solution)/shard_map/run_expert/pallas_call | solution.py:591
  154.3 34.4 %collect.1 = bf16[64,1536]{1,0:T(8,128)(2,1)S(1)} custom-call(bf16[32,64,1536]{2,1,0:T(8,128)(2,1)S(1)} %bitcast.42), custom_call_target="tpu_custom_call" | custom-call | tf_op jit(solution)/shard_map/collect/pallas_call | solution.py:711
  188.7 0.0 copy-done.8
  188.7 0.7 add_convert_fusion
  (29 shorter events, 0.2 us)
Async XLA Ops:
  0.6 56.4 %copy-start = (bf16[1536,256]{1,0:T(8,128)(2,1)S(1)}, bf16[1536,256]{1,0:T(8,128)(2,1)}, u32[]{:S(2)}) copy-start(bf16[1536,256]{1,0:T(8,128)(2,1)} %param.19) | copy-start | bytes 2359300
  0.6 5.9 %copy-start.6 = (bf16[64,1536]{1,0:T(8,128)(2,1)S(1)}, bf16[64,1536]{1,0:T(8,128)(2,1)}, u32[]{:S(2)}) copy-start(bf16[64,1536]{1,0:T(8,128)(2,1)} %tokens_ref.1) | copy-start | bytes 589828
  4.2 49.1 %copy-start.14 = (f32[1536]{0:T(1024)S(1)}, f32[1536]{0:T(1024)}, u32[]{:S(2)}) copy-start(f32[1536]{0:T(1024)} %param.16) | copy-start | bytes 18436
  6.5 1.0 copy-start.9
  49.9 1.7 copy-start.1
  53.7 1.6 copy-start.11
  55.3 1.7 copy-start.10
  57.1 1.0 copy-start.13
  58.1 2.0 %copy-start.12 = (bf16[512,128]{1,0:T(8,128)(2,1)S(1)}, bf16[512,128]{1,0:T(8,128)(2,1)}, u32[]{:S(2)}) copy-start(bf16[512,128]{1,0:T(8,128)(2,1)} %copy.47) | copy-start | bytes 393220
  58.1 2.0 %copy-start.2 = (bf16[8,16,8,1536]{3,2,1,0:T(8,128)(2,1)S(1)}, bf16[8,16,8,1536]{3,2,1,0:T(8,128)(2,1)}, u32[]{:S(2)}) copy-start(bf16[8,16,8,1536]{3,2,1,0:T(8,128)(2,1)} %copy-done.1) | copy-start | bytes 9437188
  106.5 0.7 copy-start.7
  107.2 31.8 %copy-start.5 = (bf16[1,768,1536]{2,1,0:T(8,128)(2,1)S(1)}, bf16[1,768,1536]{2,1,0:T(8,128)(2,1)}, u32[]{:S(2)}) copy-start(bf16[1,768,1536]{2,1,0:T(8,128)(2,1)} %param.25) | copy-start | bytes 7077892
  108.0 31.0 %copy-start.3 = (bf16[1,1536,768]{2,1,0:T(8,128)(2,1)S(1)}, bf16[1,1536,768]{2,1,0:T(8,128)(2,1)}, u32[]{:S(2)}) copy-start(bf16[1,1536,768]{2,1,0:T(8,128)(2,1)} %param.23) | copy-start | bytes 7077892
  108.0 31.0 %copy-start.4 = (bf16[1,1536,768]{2,1,0:T(8,128)(2,1)S(1)}, bf16[1,1536,768]{2,1,0:T(8,128)(2,1)}, u32[]{:S(2)}) copy-start(bf16[1,1536,768]{2,1,0:T(8,128)(2,1)} %param.24) | copy-start | bytes 7077892
  154.3 34.4 %copy-start.8 = (f32[64,1536]{1,0:T(8,128)S(1)}, f32[64,1536]{1,0:T(8,128)}, u32[]{:S(2)}) copy-start(f32[64,1536]{1,0:T(8,128)} %copy-done.7) | copy-start | bytes 1179652

commit v5 on v3

--- a/solution.py
+++ b/solution.py
@@ -77,7 +77,9 @@
 
 
 def tp_gather_kernel(
-    rows_ref, seg_ref, out, segs_ref,
+    rows_ref, seg_ref, gain_ref, w_query_ref, w_key_ref, w_value_ref,
+    query_ref, key_ref, value_ref, own_key_ref, own_value_ref, segs_ref,
+    out, w_query, w_key_value,
     send, recv, seg_send, seg_recv, far_send, far_recv, local,
 ):
     s, t, _, _, core, x, y = places()
@@ -106,12 +108,41 @@
     go(2, rows_ref, out.at[t], yp)
     rows_own = pltpu.make_async_copy(rows_ref, out.at[t], local.at[1])
     rows_own.start()
+    columns = w_key_ref.shape[1]
+    loads = [
+        pltpu.make_async_copy(w_query_ref, w_query, local.at[2]),
+        pltpu.make_async_copy(w_key_ref, w_key_value.at[:, pl.ds(0, columns)], local.at[3]),
+        pltpu.make_async_copy(w_value_ref, w_key_value.at[:, pl.ds(columns, columns)], local.at[4]),
+    ]
+    for load in loads:
+        load.start()
+
+    def normed(rank):
+        return rms_rows(out[rank], gain_ref[...]).astype(jnp.bfloat16)
+
+    def project(rank):
+        rows = normed(rank)
+        span = pl.ds(pl.multiple_of(rank * rows.shape[0], 64), rows.shape[0])
+        query_ref[span, :] = jnp.dot(rows, w_query[...], preferred_element_type=jnp.float32)
+        for offset, target in ((0, key_ref), (columns, value_ref)):
+            head = pl.ds(pl.multiple_of(offset + x * HD, HD), HD)
+            target[span, :] = jnp.dot(
+                rows, w_key_value[:, head], preferred_element_type=jnp.float32
+            ).astype(target.dtype)
+
     seg_own.wait()
     for k in range(7):
         moves.landed(segs_ref.at[0, t], seg_send.at[k], seg_recv.at[k])
     for k, peer in enumerate(ahead):
         moves.start(segs_ref.at[0], segs_ref.at[k + 1], far_send.at[k], far_recv.at[k], peer)
     low, high = pl.ds(0, 32), pl.ds(32, 32)
+    rows_own.wait()
+    for load in loads:
+        load.wait()
+    both = jnp.dot(normed(t), w_key_value[...], preferred_element_type=jnp.float32)
+    own_key_ref[...] = both[:, :columns]
+    own_value_ref[...] = both[:, columns:].astype(jnp.bfloat16)
+    project(t)
     landed(0, out.at[across + y])
     go(3, out.at[across + y], out.at[across + y], yn)
     go(4, out.at[across + y], out.at[across + y], yp)
@@ -119,38 +150,55 @@
     go(5, out.at[own + down, low], out.at[own + down, low], yn)
     landed(2, out.at[own + up])
     go(6, out.at[own + up, high], out.at[own + up, high], yp)
+    project(across + y)
     landed(3, out.at[across + down])
     go(7, out.at[across + down, low], out.at[across + down, low], yn)
     landed(4, out.at[across + up])
     go(8, out.at[across + up, high], out.at[across + up, high], yp)
+    project(own + down)
+    project(own + up)
+    project(across + down)
+    project(across + up)
     landed(5, out.at[own + two, low])
     landed(6, out.at[own + two, high])
+    project(own + two)
     landed(7, out.at[across + two, low])
     landed(8, out.at[across + two, high])
-    rows_own.wait()
+    project(across + two)
     for k in range(8):
         moves.landed(segs_ref.at[k + 1], far_send.at[k], far_recv.at[k])
     moves.drain()
 
 
-def tp_gather(rows, seg):
+def tp_gather(rows, seg, gain, w_query, w_key, w_value):
     count, width = rows.shape
     dma = pltpu.SemaphoreType.DMA
+    bf16, f32 = jnp.bfloat16, jnp.float32
+    shape = jax.ShapeDtypeStruct
     return pl.pallas_call(
         tp_gather_kernel,
         out_shape=(
-            jax.ShapeDtypeStruct((8, count, width), rows.dtype),
-            jax.ShapeDtypeStruct((9, 8, 1, 128), jnp.int32),
+            shape((8 * count, HD), f32),
+            shape((8 * count, HD), f32),
+            shape((8 * count, HD), bf16),
+            shape((count, KVH * HD), f32),
+            shape((count, KVH * HD), bf16),
+            shape((9, 8, 1, 128), jnp.int32),
         ),
-        in_specs=[IN_VMEM] * 2,
-        out_specs=(IN_VMEM,) * 2,
-        scratch_shapes=[dma((9,)), dma((9,)), dma((7,)), dma((7,)), dma((8,)), dma((8,)), dma((2,))],
-        compiler_params=params(1, vmem_limit_bytes=16 << 20),
+        in_specs=[IN_VMEM] * 3 + [ANY] * 3,
+        out_specs=(IN_VMEM,) * 6,
+        scratch_shapes=[
+            pltpu.VMEM((8, count, width), bf16),
+            pltpu.VMEM((width, HD), bf16),
+            pltpu.VMEM((width, 2 * KVH * HD), bf16),
+            dma((9,)), dma((9,)), dma((7,)), dma((7,)), dma((8,)), dma((8,)), dma((5,)),
+        ],
+        compiler_params=params(1, vmem_limit_bytes=20 << 20),
         name="tp_gather",
-    )(rows, seg)
-
-
-TILE = 128
+    )(rows, seg, gain, w_query, w_key, w_value)
+
+
+TILE = 256
 
 
 def attention_kernel(
@@ -204,8 +252,8 @@
     unit = math.log2(math.e) / math.sqrt(HD)
 
     def attend(j):
-        def tile(number, _):
-            rows = pl.ds(pl.multiple_of(number * TILE, TILE), TILE)
+        def tile(number):
+            rows = pl.ds(number * TILE, TILE)
             keys = slots[j, :, 0].reshape(count, HD)
             values = slots[j, :, 1].reshape(count, HD)
             scores = lax.dot_general(
@@ -226,9 +274,9 @@
                 weights.astype(jnp.bfloat16), values, preferred_element_type=jnp.float32
             )
             peak[rows, :] = newest
-            return 0
-
-        lax.fori_loop(0, count // TILE, tile, 0)
+
+        for number in range(count // TILE):
+            tile(number)
 
     def z_step(k, onward):
         piece = slots.at[2 * k, y]
@@ -505,83 +553,82 @@
     along_index = lax.broadcasted_iota(jnp.int32, (CHUNK, CHUNK), 1)
     zero_first = (((0,), (0,)), ((), ()))
 
-    def span(block):
-        return pl.ds(pl.multiple_of(block * CHUNK, CHUNK), CHUNK)
-
-    def number_rows(block, before):
-        routed = (rows_ref[span(block), width:].astype(f32) != 0.0).astype(f32)
+    tokens = rows_ref.shape[0]
+    lower, upper, same = [
+        test.astype(f32).astype(bf16)
+        for test in (along_index <= down_index, down_index <= along_index, down_index == along_index)
+    ]
+    before = jnp.zeros((1, 1), f32)
+    befores = []
+    for block in range(blocks):
+        routed = (rows_ref[pl.ds(block * CHUNK, CHUNK), width:].astype(f32) != 0.0).astype(f32)
         here = lax.broadcasted_iota(jnp.int32, routed.shape, 1) == expert
         routed = jnp.where(here, routed, 0.0)
         ones = routed.astype(bf16)
-        upto = jnp.dot((along_index <= down_index).astype(f32).astype(bf16), ones, preferred_element_type=f32)
         hit = jnp.sum(routed, axis=1, keepdims=True)
-        rank = jnp.sum(jnp.where(here, upto, 0.0), axis=1, keepdims=True)
-        column[span(block), :] = jnp.where(hit > 0.0, rank + (before - 1.0), -1.0)
-        upto = lax.dot_general(
-            ones, (down_index <= along_index).astype(f32).astype(bf16), zero_first, preferred_element_type=f32
-        )
-        same = lax.dot_general(
-            ones, (down_index == along_index).astype(f32).astype(bf16), zero_first, preferred_element_type=f32
-        )
-        hit = jnp.sum(same, axis=0, keepdims=True)
-        mine = lax.broadcasted_iota(jnp.int32, upto.shape, 0) == expert
-        rank = jnp.sum(jnp.where(mine, upto, 0.0), axis=0, keepdims=True)
-        lane[block] = jnp.where(hit > 0.0, rank + (before - 1.0), -1.0)
-        starts[block] = before.astype(jnp.int32)
-        return before + jnp.sum(routed)
-
-    routed = lax.fori_loop(0, blocks, number_rows, jnp.float32(0.0)).astype(jnp.int32)
-    starts[blocks] = routed
-
-    def one_chunk(number, _):
-        base = number * CHUNK
-        gathered[...] = jnp.zeros_like(gathered)
-
-        def touches(block):
-            first, end = starts[block], starts[block + 1]
-            return (first < base + CHUNK) & ((end > base) | (first >= base))
-
-        def gather(block, _):
-            @pl.when(touches(block))
-            def _():
-                slots = base + lax.broadcasted_iota(jnp.int32, (CHUNK, 1), 0)
-                picks = (lane[block] == slots.astype(f32)).astype(f32).astype(bf16)
-                gathered[...] += jnp.dot(picks, rows_ref[span(block), :], preferred_element_type=f32)
-
-            return 0
-
-        lax.fori_loop(0, blocks, gather, 0)
-        all_gates = gathered[:, width:]
+        rank = jnp.sum(jnp.dot(lower, ones, preferred_element_type=f32), axis=1, keepdims=True)
+        column[pl.ds(block * CHUNK, CHUNK), :] = jnp.where(hit > 0.0, rank + (before - 1.0), -1.0)
+        rank = jnp.sum(lax.dot_general(ones, upper, zero_first, preferred_element_type=f32), axis=0, keepdims=True)
+        hit = jnp.sum(lax.dot_general(ones, same, zero_first, preferred_element_type=f32), axis=0, keepdims=True)
+        lane[:, pl.ds(block * CHUNK, CHUNK)] = jnp.where(hit > 0.0, rank + (before - 1.0), -1.0)
+        befores.append(before)
+        before = before + jnp.sum(hit, axis=1, keepdims=True)
+    for block, count in enumerate(befores + [before]):
+        starts[block] = jnp.sum(count).astype(jnp.int32)
+    total = starts[blocks]
+
+    def picks_of(base, first, rows):
+        slots = base + lax.broadcasted_iota(jnp.int32, (CHUNK, 1), 0)
+        return (lane[:, pl.ds(first, rows)] == slots.astype(f32)).astype(f32).astype(bf16)
+
+    def backs_of(base, block):
+        slots = base + lax.broadcasted_iota(jnp.int32, (1, CHUNK), 1)
+        return (column[pl.ds(block * CHUNK, CHUNK), :] == slots.astype(f32)).astype(f32).astype(bf16)
+
+    def compute(rows, all_gates):
         here = lax.broadcasted_iota(jnp.int32, all_gates.shape, 1) == expert
         gates = jnp.sum(jnp.where(here, all_gates, 0.0), axis=1, keepdims=True)
-        rows = gathered[:, :width].astype(bf16)
+        rows = rows.astype(bf16)
         gate_out = jnp.dot(rows, gate_ref[...], preferred_element_type=f32)
         up_out = jnp.dot(rows, up_ref[...], preferred_element_type=f32)
         active = (jnp.maximum(gate_out, 0.0) * up_out).astype(bf16)
         down_out = jnp.dot(active, down_ref[...], preferred_element_type=f32) * gates
         contribution[...] = down_out.astype(bf16)
 
-        def place(block, _):
-            @pl.when(touches(block))
+    picks = picks_of(0, 0, tokens)
+    compute(
+        jnp.dot(picks, rows_ref[:, :width], preferred_element_type=f32),
+        jnp.dot(picks, rows_ref[:, width:], preferred_element_type=f32),
+    )
+    for block in range(blocks):
+        placed = jnp.dot(backs_of(0, block), contribution[...], preferred_element_type=f32)
+        out_ref[pl.ds(block * CHUNK, CHUNK), :] = placed.astype(bf16)
+
+    def more(number, _):
+        base = number * CHUNK
+        part = tokens // 4
+        gathered[...] = jnp.zeros_like(gathered)
+        for first in range(0, tokens, part):
+            low, high = starts[first // CHUNK], starts[(first + part) // CHUNK]
+
+            @pl.when((low < base + CHUNK) & (high > base))
             def _():
-                slots = base + lax.broadcasted_iota(jnp.int32, (1, CHUNK), 1)
-                back = (column[span(block), :] == slots.astype(f32)).astype(f32).astype(bf16)
-                placed = jnp.dot(back, contribution[...], preferred_element_type=f32)
-
-                @pl.when(starts[block] >= base)
-                def _():
-                    out_ref[span(block), :] = placed.astype(bf16)
-
-                @pl.when(starts[block] < base)
-                def _():
-                    out_ref[span(block), :] = (out_ref[span(block), :].astype(f32) + placed).astype(bf16)
-
-            return 0
-
-        lax.fori_loop(0, blocks, place, 0)
+                gathered[...] += jnp.dot(
+                    picks_of(base, first, part), rows_ref[pl.ds(first, part), :], preferred_element_type=f32
+                )
+
+        compute(gathered[:, :width], gathered[:, width:])
+        for block in range(blocks):
+
+            @pl.when((starts[block] < base + CHUNK) & (starts[block + 1] > base))
+            def _():
+                span = pl.ds(block * CHUNK, CHUNK)
+                placed = jnp.dot(backs_of(base, block), contribution[...], preferred_element_type=f32)
+                out_ref[span, :] = (out_ref[span, :].astype(f32) + placed).astype(bf16)
+
         return 0
 
-    lax.fori_loop(0, routed // CHUNK + 1, one_chunk, 0)
+    lax.fori_loop(1, (total + CHUNK - 1) // CHUNK, more, 0)
 
 
 def run_expert(rows, w_gate, w_up, w_down):
@@ -594,7 +641,7 @@
         out_specs=IN_VMEM,
         scratch_shapes=[
             pltpu.VMEM((tokens, 1), jnp.float32),
-            pltpu.VMEM((tokens // CHUNK, 1, CHUNK), jnp.float32),
+            pltpu.VMEM((1, tokens), jnp.float32),
             pltpu.VMEM((CHUNK, columns), jnp.float32),
             pltpu.VMEM((CHUNK, width), jnp.bfloat16),
             pltpu.SMEM((tokens // CHUNK + 1,), jnp.int32),
@@ -735,7 +782,9 @@
     block_first = seq_rank * tok_seq
 
     seg_row = jnp.pad(segment_ids, (0, HD - tok_dev), constant_values=-1).reshape(1, HD)
-    wide, segs = tp_gather(tokens, seg_row)
+    query, keys, values, own_keys, own_values, segs = tp_gather(
+        tokens, seg_row, attn_gain[None], w_query, w_key, w_value
+    )
 
     block_index = block_first + jnp.arange(tok_seq, dtype=jnp.int32)
     near = segs[:, :, 0, :tok_dev].reshape(9, tok_seq)
@@ -749,24 +798,14 @@
     angle = position[:, None] * inverse[None, :]
     cosine, sine = jnp.cos(angle), jnp.sin(angle)
 
-    normed = rms_rows(wide.reshape(tok_seq, width), attn_gain).astype(bf16)
-    query = rotate(jnp.dot(normed, w_query, preferred_element_type=f32), cosine, sine).astype(bf16)
-    keys = rotate(jnp.dot(normed, w_key, preferred_element_type=f32), cosine, sine).astype(bf16)
-    values = jnp.dot(normed, w_value, preferred_element_type=f32).astype(bf16)
-
-    def own_rows(matrix):
-        mine = lax.dynamic_slice_in_dim(matrix, tp_rank * tok_dev, tok_dev, 0)
-        return jnp.transpose(mine.reshape(tok_dev, KVH, HD), (1, 0, 2))
-
-    kv_cache = jnp.stack([own_rows(keys), own_rows(values)])
-    head = tp_rank // 4
-    kv_own = jnp.stack(
-        [
-            lax.dynamic_slice_in_dim(m, head * HD, HD, 1).reshape(4, tok_seq // 4, HD)
-            for m in (keys, values)
-        ],
-        axis=1,
+    query = rotate(query, cosine, sine).astype(bf16)
+    keys = rotate(keys, cosine, sine).astype(bf16)
+    own = lambda table: lax.dynamic_slice_in_dim(table, tp_rank * tok_dev, tok_dev, 0)
+    own_keys = rotate(own_keys, own(cosine), own(sine)).astype(bf16)
+    kv_cache = jnp.stack(
+        [jnp.transpose(m.reshape(tok_dev, KVH, HD), (1, 0, 2)) for m in (own_keys, own_values)]
     )
+    kv_own = jnp.stack([m.reshape(4, tok_seq // 4, HD) for m in (keys, values)], axis=1)
     resid, payload = attention_layer(
         kv_own, query, starts[:, None], tokens, w_out, moe_gain[None], w_router, routes
     )

time: 172 us -> 161 us (0.936); the launches traced: 172 us -> 158 us
  Pallas kernels: 154 us -> 145 us
  other arithmetic: 5.65 us -> 3.54 us
  matrix products: 1.74 us -> 0 us
    pallas_call x1, Pallas kernels: 12 us -> 6.54 us  [run_expert(): pl.pallas_call(expert_kernel, out_shape=jax.ShapeDtypeStruct((tokens, wid...]
    pallas_call x1, Pallas kernels: 45.3 us -> 40.6 us  [attention_layer(): pl.pallas_call(attention_kernel, out_shape=(jax.ShapeDtypeStruct((rows, w...]
    dot_general x1 -> x0, local copies, waits for them, and re-layouts: 2.32 us -> none  [on_device(): jnp.dot(normed, w_key, preferred_element_type=f32)]
    convert_element_type x3 -> x1, other arithmetic: 2.13 us -> 0.11 us  [on_device(): query = rotate(query, cosine, sine).astype(bf16)]
    dot_general x3 -> x0, matrix products: 1.74 us -> none  [the longest x1 0.6 us: on_device(): jnp.dot(normed, w_key, preferred_element_type=f32)]
    unnamed x30 -> x20, local copies, waits for them, and re-layouts: 4.47 us -> 6.1 us
where the time goes in v5:
time: 161 us; the launch traced here: 158 us
  Pallas kernels  145 us (90%)
  local copies, waits for them, and re-layouts  8.87 us (6%)
  other arithmetic  3.54 us (2%)
    pallas_call x1, Pallas kernels, attention_layer(): pl.pallas_call(attention_kernel, out_shape=(jax.ShapeDtypeStruct((rows, w...  40.6 us
    pallas_call x1, Pallas kernels, collect(): pl.pallas_call(collect_kernel, out_shape=jax.ShapeDtypeStruct((rows, widt...  37.4 us
    pallas_call x1, Pallas kernels, spread(): pl.pallas_call(spread_kernel, out_shape=jax.ShapeDtypeStruct((32,) + rows...  31.8 us
    pallas_call x1, Pallas kernels, tp_gather(): pl.pallas_call(tp_gather_kernel, out_shape=(shape((8 * count, HD), f32),...  28.4 us
    pallas_call x1, Pallas kernels, run_expert(): pl.pallas_call(expert_kernel, out_shape=jax.ShapeDtypeStruct((tokens, wid...  6.54 us
    unnamed x20, local copies, waits for them, and re-layouts  6.1 us

profile of v5, /device:TPU:8, one launch (start us, length us, event | category | flops | bytes accessed | tf_op | source)
XLA Modules:
  0.0 157.9 jit_solution(3160541813818808547)
XLA Ops:
  0.7 0.7 pad_bitcast_fusion.seg_ref
  1.3 0.7 broadcast_in_dim.28.gain_ref
  2.0 0.7 broadcast_in_dim.33.gain_ref
  2.7 0.1 broadcast_compare_fusion
  2.8 0.1 broadcast_subtract_fusion
  2.9 0.8 copy.39.routes_ref
  3.6 1.1 copy.38.router_ref
  4.8 0.0 copy-start.3
  4.8 1.1 copy-done.3
  5.9 0.0 copy-start.4
  5.9 1.1 copy-done.4
  7.0 0.0 copy-start.5
  7.0 0.9 copy-done.5
  8.0 0.0 copy-start.8
  8.0 1.0 copy-done.8
  9.0 28.4 %tp_gather.1 = (f32[512,128]{1,0:T(8,128)S(1)}, f32[512,128]{1,0:T(8,128)S(1)}, bf16[512,128]{1,0:T(8,128)(2,1)S(1)}, f32[64,256]{1,0:T(8,128)S(1)}, bf16[64,256...) custom-call(bf16[64,1536]{1,0:T(8,128)(2,1)S(1)} %copy-done.5, s32[1,128]{1,0:T(1,128)S(1)} %pad_bitcast_fusion.seg_ref, ...), custom_call_target="tpu_custom_call" | custom-call | tf_op jit(solution)/shard_map/tp_gather/pallas_call | solution.py:178
  37.4 0.0 copy-start.6
  37.4 0.0 copy-start.7
  37.4 0.1 eq.30
  37.5 0.1 slice_reduce_fusion
  37.6 0.1 eq.34
  37.6 0.2 select_reduce_fusion
  37.8 0.1 select_reduce_fusion.1
  37.9 1.3 fusion.13
  39.2 0.1 maximum_bitcast_fusion.q_ref
  39.4 0.1 fusion.17
  39.5 0.1 pad_maximum_fusion.1
  39.7 0.1 broadcast_multiply_fusion
  39.8 0.1 dynamic-slice_cosine_fusion
  40.0 0.1 maximum_bitcast_fusion.1
  40.1 0.6 pad_maximum_fusion.2
  40.7 0.1 copy.37.start_ref
  40.8 0.0 copy-done.6
  40.9 0.0 copy-done.7
  40.9 0.0 copy-start.2
  40.9 40.6 %attention_layer.1 = (f32[64,1536]{1,0:T(8,128)S(1)}, bf16[64,1664]{1,0:T(8,128)(2,1)S(1)}) custom-call(bf16[4,2,128,128]{3,2,1,0:T(8,128)(2,1)S(1)} %pad_maximum_fusion.kv_ref, bf16[512,128]{1,0:T(8,128)(2,1)S(1)} %maximum_bitcast_fusion.q_ref, s32[512,1]{1,0:T(8,128)S(1)} %copy.37.start_ref, bf16[64,1536]{1,0:T(8,128)(2,1)S(1)} %copy-done.6, ...), custom_call_target="tpu_custom_call" | custom-call | tf_op jit(solution)/shard_map/attention_layer/pallas_call | solution.py:396
  81.4 0.0 copy-start
  81.5 0.0 copy-start.1
  81.5 31.8 %spread.1 = bf16[32,64,1664]{2,1,0:T(8,128)(2,1)S(1)} custom-call(bf16[64,1664]{1,0:T(8,128)(2,1)S(1)} %get-tuple-element.15.rows_ref), custom_call_target="tpu_custom_call" | custom-call | tf_op jit(solution)/shard_map/spread/pallas_call | solution.py:530
  113.3 0.0 copy-done.2
  113.3 0.0 copy-done
  113.3 0.0 copy-done.1
  113.3 6.5 %run_expert.1 = bf16[2048,1536]{1,0:T(8,128)(2,1)S(1)} custom-call(bf16[2048,1664]{1,0:T(8,128)(2,1)S(1)} %bitcast.29, bf16[1536,768]{1,0:T(8,128)(2,1)S(1)} %bitcast.31, bf16[1536,768]{1,0:T(8,128)(2,1)S(1)} %bitcast.32, bf16[768,1536]{1,0:T(8,128)(2,1)S(1)} %bitcast.33), custom_call_target="tpu_custom_call" | custom-call | tf_op jit(solution)/shard_map/run_expert/pallas_call | solution.py:637
  119.8 37.4 %collect.1 = bf16[64,1536]{1,0:T(8,128)(2,1)S(1)} custom-call(bf16[32,64,1536]{2,1,0:T(8,128)(2,1)S(1)} %bitcast.30), custom_call_target="tpu_custom_call" | custom-call | tf_op jit(solution)/shard_map/collect/pallas_call | solution.py:757
  157.2 0.7 add_convert_fusion
  (9 shorter events, 0.1 us)
Async XLA Ops:
  4.8 1.1 copy-start.3
  5.9 1.1 copy-start.4
  7.0 0.9 copy-start.5
  8.0 1.0 copy-start.8
  37.4 3.5 %copy-start.6 = (bf16[64,1536]{1,0:T(8,128)(2,1)S(1)}, bf16[64,1536]{1,0:T(8,128)(2,1)}, u32[]{:S(2)}) copy-start(bf16[64,1536]{1,0:T(8,128)(2,1)} %tokens_ref.1) | copy-start | bytes 589828
  37.4 3.5 %copy-start.7 = (bf16[128,1536]{1,0:T(8,128)(2,1)S(1)}, bf16[128,1536]{1,0:T(8,128)(2,1)}, u32[]{:S(2)}) copy-start(bf16[128,1536]{1,0:T(8,128)(2,1)} %w_out_ref.1) | copy-start | bytes 1179652
  40.9 72.4 %copy-start.2 = (bf16[1,768,1536]{2,1,0:T(8,128)(2,1)S(1)}, bf16[1,768,1536]{2,1,0:T(8,128)(2,1)}, u32[]{:S(2)}) copy-start(bf16[1,768,1536]{2,1,0:T(8,128)(2,1)} %param.25) | copy-start | bytes 7077892
  81.4 31.8 %copy-start = (bf16[1,1536,768]{2,1,0:T(8,128)(2,1)S(1)}, bf16[1,1536,768]{2,1,0:T(8,128)(2,1)}, u32[]{:S(2)}) copy-start(bf16[1,1536,768]{2,1,0:T(8,128)(2,1)} %param.23) | copy-start | bytes 7077892
  81.5 31.8 %copy-start.1 = (bf16[1,1536,768]{2,1,0:T(8,128)(2,1)S(1)}, bf16[1,1536,768]{2,1,0:T(8,128)(2,1)}, u32[]{:S(2)}) copy-start(bf16[1,1536,768]{2,1,0:T(8,128)(2,1)} %param.24) | copy-start | bytes 7077892
